TPU v7x, 32 devices: a whole 2x2x4 slice. The times are simulated.
32 devices in a mesh: row: 8 (over y, x, core), col: 4 (over z).
Axes of the slice: x: 2, y: 2, z: 4, core: 2. Of those that a mesh axis runs over, the one named last changes fastest.
Arguments:
- amplitudes: bfloat16 [256, 4096], P('row', 'col'), may hold values from -6 to 6
- integrals: bfloat16 [4096, 4096], P('col', 'row'), may hold values from -0.25 to 0.25
- occupied_irreps: int32 [256], replicated, may hold values from 0 to 7, as said below
- contracted_irreps: int32 [4096], P('col'), may hold values from 0 to 7
- output_irreps: int32 [4096], P('row'), may hold values from 0 to 7, as said below
Outputs:
- ladder: float32 [256, 4096], P('col', 'row')
Inputs may be any that keep to these rules, and one draw needn't show every extreme that they name: `occupied_irreps`: in each aligned block of 64 occupied pairs, every irrep appears exactly 64 // 8 times. `output_irreps`: in each aligned block of 512 output pairs, every irrep appears exactly 512 // 8 times.
All inputs are finite; a program needn't handle non-finite values.
Results may differ from a plain program's by a relative error of at most 0.0003.
Values may be sent and summed in bfloat16 or wider, within the bound.
No kernel may reach another device: no remote copies, remote signals or barrier semaphores. Data moves between devices by JAX's collectives and lax.ppermute only.
A program may use at most 64 MiB of HBM per device.

v0:
```python
import jax
import jax.numpy as jnp
from jax import lax
from jax.sharding import PartitionSpec as P


def body(amplitudes, integrals, occupied_irreps, contracted_irreps, output_irreps):
    col_count = lax.axis_size("col")
    pairs = occupied_irreps.shape[0]
    pair_share = pairs // col_count
    own_irreps = lax.dynamic_slice_in_dim(
        occupied_irreps, lax.axis_index("col") * pair_share, pair_share, 0
    )
    allowed = contracted_irreps[:, None] == output_irreps[None, :]
    masked = jnp.where(allowed, integrals, jnp.zeros_like(integrals))
    partial_sums = jnp.dot(
        lax.all_gather(amplitudes, "row", axis=0, tiled=True),
        masked,
        preferred_element_type=jnp.float32,
    )
    summed = lax.psum_scatter(partial_sums, "col", scatter_dimension=0, tiled=True)
    matches = own_irreps[:, None] == output_irreps[None, :]
    return jnp.where(matches, summed, jnp.zeros_like(summed))


def solution(mesh):
    return jax.shard_map(
        body,
        mesh=mesh,
        in_specs=(P("row", "col"), P("col", "row"), P(), P("col"), P("row")),
        out_specs=P("col", "row"),
        check_vma=False,
    )
```

profile of v0, /device:TPU:0, one launch (start us, length us, event | category | flops | bytes accessed | tf_op | source)
XLA Modules:
  0.0 52.0 jit_solution(14986923095626221347)
XLA Ops:
  6.5 0.0 reduce-scatter.4.cloned.1.call-start
  6.5 11.6 %all_gather.3 = bf16[256,1024]{1,0:T(8,128)(2,1)S(1)} all-gather(bf16[32,1024]{1,0:T(8,128)(2,1)} %param.5), channel_id=1, replica_groups=mesh['row'=8,'col'=4] {'row'}, dimensions={0}, use_global_device_ids=true | all-gather | bytes 589824 | tf_op jit(solution)/shard_map/all_gather | solution.py:17
  18.1 1.9 %convolution_bitcast_fusion = f32[256,512]{0,1:T(8,128)S(1)} fusion(bf16[256,1024]{1,0:T(8,128)(2,1)S(1)} %all_gather.3, bf16[1024,512]{1,0:T(8,128)(2,1)} %param.6, s32[512]{0:T(512)} %param.9, s32[1024]{0:T(1024)} %param.8), kind=kOutput, calls=%fused_computation.1 | convolution fusion | flops 269484032 | bytes 2103296 | tf_op jit(solution)/shard_map/dot_general | solution.py:16
  20.1 0.0 copy-start.1
  20.1 0.0 copy-start
  20.1 1.0 %copy.8 = f32[256,512]{1,0:T(8,128)} copy(f32[256,512]{0,1:T(8,128)S(1)} %convolution_bitcast_fusion) | data formatting | bytes 1048576
  21.1 0.0 reduce-scatter.4.cloned.1.call-update
  21.1 0.0 copy-done.1
  21.1 0.1 dynamic_slice.3
  21.2 22.0 %reduce-scatter.4.cloned.1.call-done = f32[64,512]{1,0:T(8,128)} async-done(((f32[256,512]{1,0:T(8,128)}), f32[64,512]{1,0:T(8,128)}) %reduce-scatter.4.cloned.1.call-update) | async-done | bytes 131088
  43.2 1.0 %copy.9 = f32[64,512]{0,1:T(8,128)S(1)} copy(f32[64,512]{1,0:T(8,128)} %reduce-scatter.4.cloned.1.call-done) | data formatting | bytes 262144
  44.2 0.0 copy-done
  44.2 0.1 compare_select_fusion.2
  44.4 0.8 %copy.7 = f32[64,512]{1,0:T(8,128)} copy(f32[64,512]{0,1:T(8,128)S(1)} %compare_select_fusion.2) | data formatting | bytes 262144 | tf_op jit(solution)/shard_map/jit(_where)/select_n | solution.py:23
Async XLA Ops:
  6.5 36.7 %reduce-scatter.4.cloned.1.call-start = ((), (), s32[]{:S(2)}) async-start(), calls=%async_computation.1 | async-start | bytes 655360
  20.1 1.1 %copy-start.1 = (s32[256]{0:T(256)S(1)}, s32[256]{0:T(256)}, u32[]{:S(2)}) copy-start(s32[256]{0:T(256)} %param.7) | copy-start | bytes 3076
  20.1 24.2 %copy-start = (s32[512]{0:T(512)S(1)}, s32[512]{0:T(512)}, u32[]{:S(2)}) copy-start(s32[512]{0:T(512)} %param.9) | copy-start | bytes 6148
Sparse Core Ops, SparseCore 0:
  21.2 21.9 reduce-scatter.3
where the time goes:
time: 52.2 us; the launch traced here: 52 us
  waiting for transfers between devices  22 us (42%)
  between operations  13.4 us (26%)
  blocking collectives  11.6 us (22%)
  local copies, waits for them, and re-layouts  2.88 us (6%)
  matrix products  1.93 us (4%)
    unnamed x2, waiting for transfers between devices  22 us
    all_gather x1, blocking collectives, body(): lax.all_gather(amplitudes, 'row', axis=0, tiled=True)  11.6 us
    unnamed x6, local copies, waits for them, and re-layouts  2.03 us
    dot_general x1, matrix products, body(): jnp.dot(lax.all_gather(amplitudes, 'row', axis=0, tiled=True), masked, pr...  1.93 us
  transfers between devices with their start and end apart: 1, of which 1 were waited for; matrix products, arithmetic and copies ran while one was open for 0% of the time, Pallas kernels for 0%

commit v1 on v0

v1 whole, which is shorter than its diff:
```python
import jax
import jax.numpy as jnp
from jax import lax
from jax.sharding import PartitionSpec as P

IRREPS = 8


def swap(x, axis, mask):
    count = lax.axis_size(axis)
    return lax.ppermute(x, axis, [(i, i ^ mask) for i in range(count)])


def ranks(labels, order):
    same = labels[:, None] == labels[None, :]
    before = order[None, :] < order[:, None]
    return jnp.sum((same & before).astype(jnp.int32), axis=1)


def body(amplitudes, integrals, occupied_irreps, contracted_irreps, output_irreps):
    rows, cols = lax.axis_size("row"), lax.axis_size("col")
    pairs = occupied_irreps.shape[0]
    own = amplitudes.shape[0]
    block = pairs // cols
    slots = block // IRREPS
    share = block // own
    row, col = lax.axis_index("row"), lax.axis_index("col")
    place, member = row // share, row % share

    raw, labels, order = [amplitudes], [], []
    step = 1
    while step < share:
        both = jnp.concatenate(raw, 0)
        raw.append(swap(both, "row", step))
        step *= 2
    raw = jnp.concatenate(raw, 0)
    for j in range(share):
        first = (member ^ j) * own
        labels.append(lax.dynamic_slice_in_dim(occupied_irreps, place * block + first, own, 0))
        order.append(first + jnp.arange(own, dtype=jnp.int32))
    labels, order = jnp.concatenate(labels), jnp.concatenate(order)
    rank = ranks(labels, order)
    pick = (rank[None, :] == jnp.arange(slots, dtype=jnp.int32)[:, None]).astype(jnp.bfloat16)
    kept = jnp.where(labels[:, None] == contracted_irreps[None, :], raw, jnp.zeros_like(raw))
    packed = jnp.dot(pick, kept, preferred_element_type=jnp.float32).astype(jnp.bfloat16)

    step = share
    while step < rows:
        packed = jnp.concatenate([packed, swap(packed, "row", step)], 0)
        step *= 2

    masked = jnp.where(contracted_irreps[:, None] == output_irreps[None, :], integrals, jnp.zeros_like(integrals))
    sums = jnp.dot(packed, masked, preferred_element_type=jnp.float32)
    turn = col ^ place
    parts = [lax.dynamic_slice_in_dim(sums, (turn ^ t) * slots, slots, 0) for t in range(cols)]
    step = cols // 2
    while step >= 1:
        got = swap(jnp.concatenate(parts[step:], 0), "col", step)
        parts = [parts[t] + got[t * slots : (t + 1) * slots] for t in range(step)]
        step //= 2
    total = parts[0]

    mine = lax.dynamic_slice_in_dim(occupied_irreps, col * block, block, 0)
    slot = ranks(mine, jnp.arange(block, dtype=jnp.int32))
    out = jnp.zeros((block, total.shape[1]), jnp.float32)
    match = mine[:, None] == output_irreps[None, :]
    for s in range(slots):
        out = jnp.where(match & (slot[:, None] == s), total[s][None, :], out)
    return out


def solution(mesh):
    return jax.shard_map(
        body,
        mesh=mesh,
        in_specs=(P("row", "col"), P("col", "row"), P(), P("col"), P("row")),
        out_specs=P("col", "row"),
        check_vma=False,
    )
```

time: 52.2 us -> 22.9 us (0.44)
  waiting for transfers between devices: 22 us -> 6.61 us
  between operations: 13.4 us -> 0.06 us
  blocking collectives: 11.6 us -> 0 us
  starting transfers between devices: 0.01 us -> 10.3 us
  local copies, waits for them, and re-layouts: 2.88 us -> 1.6 us
  other arithmetic: 0.13 us -> 1.38 us
  matrix products: 1.93 us -> 2.75 us
    unnamed x2 -> x0, waiting for transfers between devices: 22 us -> none
    all_gather x1 -> x0, blocking collectives: 11.6 us -> none  [body(): lax.all_gather(amplitudes, 'row', axis=0, tiled=True)]
    ppermute x0 -> x5, starting transfers between devices: none -> 10.3 us  [swap(): return lax.ppermute(x, axis, [(i, i ^ mask) for i in range(count)])]
    ppermute x0 -> x5, waiting for transfers between devices: none -> 6.61 us  [swap(): return lax.ppermute(x, axis, [(i, i ^ mask) for i in range(count)])]
    unnamed x6 -> x2, local copies, waits for them, and re-layouts: 2.03 us -> 0.01 us
    dynamic_slice x1 -> x3, local copies, waits for them, and re-layouts: 0.08 us -> 1.58 us  [the longest x1 0.83 us: body(): lax.dynamic_slice_in_dim(occupied_irreps, place * block + first, own, 0)]
    dot_general x1 -> x2, matrix products: 1.93 us -> 2.75 us  [the longest x1 1.71 us: body(): sums = jnp.dot(packed, masked, preferred_element_type=jnp.float32)]
    select_n x1, other arithmetic: 0.13 us -> 0.91 us  [body(): out = jnp.where(match & (slot[:, None] == s), total[s][None, :], out)]
  transfers between devices with their start and end apart: 1 -> 5, of which waited for: 1 -> 4; matrix products, arithmetic and copies ran while one was open for 0% -> 9% of each run, Pallas kernels for 0% -> 0%
where the time goes in v1:
time: 22.9 us; the launch traced here: 22.7 us
  starting transfers between devices  10.3 us (45%)
  waiting for transfers between devices  6.61 us (29%)
  matrix products  2.75 us (12%)
  local copies, waits for them, and re-layouts  1.6 us (7%)
  other arithmetic  1.38 us (6%)
    ppermute x5, starting transfers between devices, swap(): return lax.ppermute(x, axis, [(i, i ^ mask) for i in range(count)])  10.3 us
    ppermute x5, waiting for transfers between devices, swap(): return lax.ppermute(x, axis, [(i, i ^ mask) for i in range(count)])  6.61 us
    dot_general x1, matrix products, body(): sums = jnp.dot(packed, masked, preferred_element_type=jnp.float32)  1.71 us
    dot_general x1, matrix products, body(): jnp.dot(pick, kept, preferred_element_type=jnp.float32).astype(jnp.bfloat16)  1.04 us
    select_n x1, other arithmetic, body(): out = jnp.where(match & (slot[:, None] == s), total[s][None, :], out)  0.91 us
    dynamic_slice x1, local copies, waits for them, and re-layouts, body(): lax.dynamic_slice_in_dim(occupied_irreps, place * block + first, own, 0)  0.83 us
    dynamic_slice x1, local copies, waits for them, and re-layouts, body(): mine = lax.dynamic_slice_in_dim(occupied_irreps, col * block, block, 0)  0.75 us
  transfers between devices with their start and end apart: 5, of which 4 were waited for; matrix products, arithmetic and copies ran while one was open for 9% of the time, Pallas kernels for 0%

profile of v1, /device:TPU:0, one launch (start us, length us, event | category | flops | bytes accessed | tf_op | source)
XLA Modules:
  0.0 22.7 jit_solution(14906007011595228335)
XLA Ops:
  0.0 0.5 %collective-permute-start = (bf16[32,1024]{1,0:T(8,128)(2,1)}, bf16[32,1024]{1,0:T(8,128)(2,1)S(1)}, u32[]{:S(2)}, u32[]{:S(2)}) collective-permute-start(bf16[32,1024]{1,0:T(8,128)(2,1)} %param.5), channel_id=1, source_target_pairs={{0,4},{4,0},{8,12},{12,8},{16,20},{20,16},{24,28},{28,24},{1,5},{5... | collective-permute-start | bytes 196616 | tf_op jit(solution)/shard_map/ppermute | solution.py:11
  0.5 0.8 %fusion.23 = (s32[32]{0:T(128)S(1)}, s32[32]{0:T(128)S(1)}) fusion(s32[256]{0:T(256)} %param.7, s32[]{:T(128)S(6)} %select_n.68, s32[]{:T(128)S(6)} %select_n.69), kind=kLoop, calls=%fused_computation.57 | loop fusion | bytes 520 | tf_op jit(solution)/shard_map/dynamic_slice | solution.py:39
  1.3 0.1 pad_add_fusion
  1.4 0.2 convert_reduce_fusion
  1.6 0.0 collective-permute-done
  1.6 1.0 %convolution_convert_fusion = bf16[8,1024]{1,0:T(8,128)(2,1)S(1)} fusion(bf16[32,1024]{1,0:T(8,128)(2,1)S(1)} %collective-permute-done, bf16[32,1024]{1,0:T(8,128)(2,1)} %param.5, s32[1024]{0:T(1024)} %param.8, s32[64]{0:T(128)S(1)} %get-tuple-element.25, s32[64]{0:T(128)S(1)} %convert_reduce_fusion), kind=kOutput, calls=%fused_computation.1 | convolution fusion | flops 1450496 | bytes 152064 | tf_op jit(solution)/shard_map/dot_general | solution.py:45
  2.6 2.8 %collective-permute-start.1 = (bf16[8,1024]{1,0:T(8,128)(2,1)S(1)}, bf16[8,1024]{1,0:T(8,128)(2,1)S(1)}, u32[]{:S(2)}, u32[]{:S(2)}) collective-permute-start(bf16[8,1024]{1,0:T(8,128)(2,1)S(1)} %convolution_convert_fusion), channel_id=1, source_target_pairs={{0,8},{4,12},{8,0},{12,4},{16,24},{20,28},{24,16},{28,20},{1,9},{5... | collective-permute-start | bytes 49160 | tf_op jit(solution)/shard_map/ppermute | solution.py:11
  5.5 1.7 %collective-permute-done.1 = bf16[8,1024]{1,0:T(8,128)(2,1)S(1)} collective-permute-done((bf16[8,1024]{1,0:T(8,128)(2,1)S(1)}, bf16[8,1024]{1,0:T(8,128)(2,1)S(1)}, u32[]{:S(2)}, u32[]{:S(2)}) %collective-permute-start.1) | collective-permute-done | bytes 16416 | tf_op jit(solution)/shard_map/ppermute | solution.py:11
  7.2 2.1 %collective-permute-start.2 = (bf16[16,1024]{1,0:T(8,128)(2,1)S(1)}, bf16[16,1024]{1,0:T(8,128)(2,1)S(1)}, u32[]{:S(2)}, u32[]{:S(2)}) collective-permute-start(bf16[16,1024]{1,0:T(8,128)(2,1)S(1)} %pad_maximum_fusion), channel_id=1, source_target_pairs={{0,16},{4,20},{8,24},{12,28},{16,0},{20,4},{24,8},{28,12},{1,17},{... | collective-permute-start | bytes 98312 | tf_op jit(solution)/shard_map/ppermute | solution.py:11
  9.2 0.8 %dynamic_slice.21 = s32[64]{0:T(128)S(1)} dynamic-slice(s32[256]{0:T(256)} %param.7, s32[]{:T(128)S(6)} %select_n.65), dynamic_slice_sizes={64} | dynamic-slice | bytes 516 | tf_op jit(solution)/shard_map/dynamic_slice | solution.py:63
  10.0 0.0 copy-start
  10.0 1.1 %collective-permute-done.2 = bf16[16,1024]{1,0:T(8,128)(2,1)S(1)} collective-permute-done((bf16[16,1024]{1,0:T(8,128)(2,1)S(1)}, bf16[16,1024]{1,0:T(8,128)(2,1)S(1)}, u32[]{:S(2)}, u32[]{:S(2)}) %collective-permute-start.2) | collective-permute-done | bytes 32800 | tf_op jit(solution)/shard_map/ppermute | solution.py:11
  11.1 1.7 %fusion = f32[32,512]{1,0:T(8,128)S(1)} fusion(bf16[1024,512]{1,0:T(8,128)(2,1)} %param.6, s32[512]{0:T(512)} %param.9, s32[1024]{0:T(1024)} %param.8, bf16[16,1024]{1,0:T(8,128)(2,1)S(1)} %collective-permute-done.2, bf16[8,1024]{1,0:T(8,128)(2,1)S(1)} %collective-permute-done.1, bf16[8,1024]{1,0:T(8,128)(2,1)S(1)} %convolution_convert_fusion), kind=kOutput, calls=%fused_computation.2 | convolution fusion | flops 34799616 | bytes 1185792 | tf_op jit(solution)/shard_map/dot_general | solution.py:53
  12.9 3.2 %collective-permute-start.3 = (f32[16,512]{1,0:T(8,128)S(1)}, f32[16,512]{1,0:T(8,128)S(1)}, u32[]{:S(2)}, u32[]{:S(2)}) collective-permute-start(f32[16,512]{1,0:T(8,128)S(1)} %pad_maximum_fusion.1), channel_id=1, source_target_pairs={{0,2},{1,3},{2,0},{3,1},{4,6},{5,7},{6,4},{7,5},{8,10},{9,11},{10,... | collective-permute-start | bytes 98312 | tf_op jit(solution)/shard_map/ppermute | solution.py:11
  16.0 0.2 convert_reduce_fusion.1
  16.2 1.8 %collective-permute-done.3 = f32[16,512]{1,0:T(8,128)S(1)} collective-permute-done((f32[16,512]{1,0:T(8,128)S(1)}, f32[16,512]{1,0:T(8,128)S(1)}, u32[]{:S(2)}, u32[]{:S(2)}) %collective-permute-start.3) | collective-permute-done | bytes 32800 | tf_op jit(solution)/shard_map/ppermute | solution.py:11
  18.0 1.8 %collective-permute-start.4 = (f32[8,512]{1,0:T(8,128)S(1)}, f32[8,512]{1,0:T(8,128)S(1)}, u32[]{:S(2)}, u32[]{:S(2)}) collective-permute-start(f32[8,512]{1,0:T(8,128)S(1)} %slice_add_fusion), channel_id=1, source_target_pairs={{0,1},{1,0},{2,3},{3,2},{4,5},{5,4},{6,7},{7,6},{8,9},{9,8},{10,11... | collective-permute-start | bytes 49160 | tf_op jit(solution)/shard_map/ppermute | solution.py:11
  19.8 1.9 %collective-permute-done.4 = f32[8,512]{1,0:T(8,128)S(1)} collective-permute-done((f32[8,512]{1,0:T(8,128)S(1)}, f32[8,512]{1,0:T(8,128)S(1)}, u32[]{:S(2)}, u32[]{:S(2)}) %collective-permute-start.4) | collective-permute-done | bytes 16416 | tf_op jit(solution)/shard_map/ppermute | solution.py:11
  21.8 0.0 copy-done
  21.8 0.9 %select_select_fusion = f32[64,512]{1,0:T(8,128)} fusion(f32[512]{0:T(512)S(1)} %bitcast.9, f32[512]{0:T(512)S(1)} %bitcast.10, f32[512]{0:T(512)S(1)} %bitcast.11, f32[512]{0:T(512)S(1)} %bitcast.12, f32[512]{0:T(512)S(1)} %bitcast.13, f32[512]{0:T(512)S(1)} %bitcast.14, f32[512]{0:T(512)S(1)} %bitcast.15, f32[512]{0:T(512)S(1)} %bitcast.8, ...), kind=kLoop, calls=%fused_computation.18 | loop fusion | flops 557056 | bytes 150272 | tf_op jit(solution)/shard_map/jit(_where)/select_n | solution.py:68
  (9 shorter events, 0.1 us)
Async XLA Ops:
  0.0 1.6 %collective-permute-start = (bf16[32,1024]{1,0:T(8,128)(2,1)}, bf16[32,1024]{1,0:T(8,128)(2,1)S(1)}, u32[]{:S(2)}, u32[]{:S(2)}) collective-permute-start(bf16[32,1024]{1,0:T(8,128)(2,1)} %param.5), channel_id=1, source_target_pairs={{0,4},{4,0},{8,12},{12,8},{16,20},{20,16},{24,28},{28,24},{1,5},{5... | collective-permute-start | bytes 196616 | tf_op jit(solution)/shard_map/ppermute | solution.py:11
  2.6 4.6 %collective-permute-start.1 = (bf16[8,1024]{1,0:T(8,128)(2,1)S(1)}, bf16[8,1024]{1,0:T(8,128)(2,1)S(1)}, u32[]{:S(2)}, u32[]{:S(2)}) collective-permute-start(bf16[8,1024]{1,0:T(8,128)(2,1)S(1)} %convolution_convert_fusion), channel_id=1, source_target_pairs={{0,8},{4,12},{8,0},{12,4},{16,24},{20,28},{24,16},{28,20},{1,9},{5... | collective-permute-start | bytes 49160 | tf_op jit(solution)/shard_map/ppermute | solution.py:11
  7.2 3.9 %collective-permute-start.2 = (bf16[16,1024]{1,0:T(8,128)(2,1)S(1)}, bf16[16,1024]{1,0:T(8,128)(2,1)S(1)}, u32[]{:S(2)}, u32[]{:S(2)}) collective-permute-start(bf16[16,1024]{1,0:T(8,128)(2,1)S(1)} %pad_maximum_fusion), channel_id=1, source_target_pairs={{0,16},{4,20},{8,24},{12,28},{16,0},{20,4},{24,8},{28,12},{1,17},{... | collective-permute-start | bytes 98312 | tf_op jit(solution)/shard_map/ppermute | solution.py:11
  10.0 11.8 %copy-start = (s32[512]{0:T(512)S(1)}, s32[512]{0:T(512)}, u32[]{:S(2)}) copy-start(s32[512]{0:T(512)} %param.9) | copy-start | bytes 6148
  12.9 5.2 %collective-permute-start.3 = (f32[16,512]{1,0:T(8,128)S(1)}, f32[16,512]{1,0:T(8,128)S(1)}, u32[]{:S(2)}, u32[]{:S(2)}) collective-permute-start(f32[16,512]{1,0:T(8,128)S(1)} %pad_maximum_fusion.1), channel_id=1, source_target_pairs={{0,2},{1,3},{2,0},{3,1},{4,6},{5,7},{6,4},{7,5},{8,10},{9,11},{10,... | collective-permute-start | bytes 98312 | tf_op jit(solution)/shard_map/ppermute | solution.py:11
  18.0 3.7 %collective-permute-start.4 = (f32[8,512]{1,0:T(8,128)S(1)}, f32[8,512]{1,0:T(8,128)S(1)}, u32[]{:S(2)}, u32[]{:S(2)}) collective-permute-start(f32[8,512]{1,0:T(8,128)S(1)} %slice_add_fusion), channel_id=1, source_target_pairs={{0,1},{1,0},{2,3},{3,2},{4,5},{5,4},{6,7},{7,6},{8,9},{9,8},{10,11... | collective-permute-start | bytes 49160 | tf_op jit(solution)/shard_map/ppermute | solution.py:11

commit v2 on v1

--- a/solution.py
+++ b/solution.py
@@ -9,6 +9,12 @@
 def swap(x, axis, mask):
     count = lax.axis_size(axis)
     return lax.ppermute(x, axis, [(i, i ^ mask) for i in range(count)])
+
+
+def swap_both(x, flip, mask):
+    rows, cols = lax.axis_size("row"), lax.axis_size("col")
+    pairs = [(r * cols + c, (r ^ flip) * cols + (c ^ mask)) for r in range(rows) for c in range(cols)]
+    return lax.ppermute(x, ("row", "col"), pairs)
 
 
 def ranks(labels, order):
@@ -26,6 +32,8 @@
     share = block // own
     row, col = lax.axis_index("row"), lax.axis_index("col")
     place, member = row // share, row % share
+
+    flip = 1 if share == 2 else 0
 
     raw, labels, order = [amplitudes], [], []
     step = 1
@@ -46,19 +54,29 @@
 
     step = share
     while step < rows:
-        packed = jnp.concatenate([packed, swap(packed, "row", step)], 0)
+        packed = jnp.concatenate([packed, swap(packed, "row", step + flip)], 0)
         step *= 2
 
     masked = jnp.where(contracted_irreps[:, None] == output_irreps[None, :], integrals, jnp.zeros_like(integrals))
-    sums = jnp.dot(packed, masked, preferred_element_type=jnp.float32)
+    masked = lax.optimization_barrier(masked)
     turn = col ^ place
-    parts = [lax.dynamic_slice_in_dim(sums, (turn ^ t) * slots, slots, 0) for t in range(cols)]
-    step = cols // 2
-    while step >= 1:
-        got = swap(jnp.concatenate(parts[step:], 0), "col", step)
-        parts = [parts[t] + got[t * slots : (t + 1) * slots] for t in range(step)]
-        step //= 2
-    total = parts[0]
+    parts = []
+    if flip:
+        other = swap(masked, "row", 1)
+    blocks = [lax.dynamic_slice_in_dim(packed, (turn ^ t) * slots, slots, 0) for t in range(cols)]
+    odd = [bin(t).count("1") % 2 * flip for t in range(cols)]
+    sums = [None] * cols
+    for side in range(1 + flip):
+        ours = [t for t in range(cols) if odd[t] == side]
+        some = jnp.dot(jnp.concatenate([blocks[t] for t in ours], 0), other if side else masked, preferred_element_type=jnp.float32)
+        for n, t in enumerate(ours):
+            sums[t] = some[n * slots : (n + 1) * slots]
+    step = 1
+    while step < cols:
+        got = swap_both(jnp.concatenate(sums[1::2], 0), flip, step)
+        sums = [part + got[t * slots : (t + 1) * slots] for t, part in enumerate(sums[::2])]
+        step *= 2
+    total = sums[0]
 
     mine = lax.dynamic_slice_in_dim(occupied_irreps, col * block, block, 0)
     slot = ranks(mine, jnp.arange(block, dtype=jnp.int32))

time: 22.9 us -> 19.6 us (0.86)
  matrix products: 2.75 us -> 0.7 us
  other arithmetic: 1.38 us -> 2.93 us
  local copies, waits for them, and re-layouts: 1.6 us -> 0.2 us
  waiting for transfers between devices: 6.61 us -> 5.83 us
  starting transfers between devices: 10.3 us -> 9.7 us
    ppermute x5 -> x4, starting transfers between devices: 10.3 us -> 4.99 us  [swap(): return lax.ppermute(x, axis, [(i, i ^ mask) for i in range(count)])]
    ppermute x0 -> x2, starting transfers between devices: none -> 4.71 us  [swap_both(): return lax.ppermute(x, ('row', 'col'), pairs)]
    ppermute x5 -> x4, waiting for transfers between devices: 6.61 us -> 2.97 us  [swap(): return lax.ppermute(x, axis, [(i, i ^ mask) for i in range(count)])]
    ppermute x0 -> x2, waiting for transfers between devices: none -> 2.86 us  [swap_both(): return lax.ppermute(x, ('row', 'col'), pairs)]
    select_n x0 -> x1, other arithmetic: none -> 1.54 us  [body(): jnp.where(contracted_irreps[:, None] == output_irreps[None, :], integrals...]
    dot_general x1 -> x2, matrix products: 1.71 us -> 0.49 us  [body(): jnp.dot(jnp.concatenate([blocks[t] for t in ours], 0), other if side else...]
    dot_general x1, matrix products: 1.04 us -> 0.2 us  [body(): jnp.dot(pick, kept, preferred_element_type=jnp.float32).astype(jnp.bfloat16)]
    dynamic_slice x1, local copies, waits for them, and re-layouts: 0.83 us -> 0.08 us  [body(): lax.dynamic_slice_in_dim(occupied_irreps, place * block + first, own, 0)]
  transfers between devices with their start and end apart: 5 -> 6, of which waited for: 4 -> 4; matrix products, arithmetic and copies ran while one was open for 9% -> 13% of each run, Pallas kernels for 0% -> 0%
where the time goes in v2:
time: 19.6 us; the launch traced here: 19.5 us
  starting transfers between devices  9.7 us (49%)
  waiting for transfers between devices  5.83 us (30%)
  other arithmetic  2.93 us (15%)
  matrix products  0.7 us (4%)
  local copies, waits for them, and re-layouts  0.2 us (1%)
    ppermute x4, starting transfers between devices, swap(): return lax.ppermute(x, axis, [(i, i ^ mask) for i in range(count)])  4.99 us
    ppermute x2, starting transfers between devices, swap_both(): return lax.ppermute(x, ('row', 'col'), pairs)  4.71 us
    ppermute x4, waiting for transfers between devices, swap(): return lax.ppermute(x, axis, [(i, i ^ mask) for i in range(count)])  2.97 us
    ppermute x2, waiting for transfers between devices, swap_both(): return lax.ppermute(x, ('row', 'col'), pairs)  2.86 us
    select_n x1, other arithmetic, body(): jnp.where(contracted_irreps[:, None] == output_irreps[None, :], integrals...  1.54 us
    select_n x1, other arithmetic, body(): out = jnp.where(match & (slot[:, None] == s), total[s][None, :], out)  0.91 us
    dot_general x2, matrix products, body(): jnp.dot(jnp.concatenate([blocks[t] for t in ours], 0), other if side else...  0.49 us
  transfers between devices with their start and end apart: 6, of which 4 were waited for; matrix products, arithmetic and copies ran while one was open for 13% of the time, Pallas kernels for 0%

profile of v2, /device:TPU:0, one launch (start us, length us, event | category | flops | bytes accessed | tf_op | source)
XLA Modules:
  0.0 19.5 jit_solution(654768775625245418)
XLA Ops:
  0.0 0.0 copy-start.3
  0.0 0.0 copy-start.1
  0.0 0.0 copy-start.2
  0.0 0.5 %collective-permute-start = (bf16[32,1024]{1,0:T(8,128)(2,1)}, bf16[32,1024]{1,0:T(8,128)(2,1)S(1)}, u32[]{:S(2)}, u32[]{:S(2)}) collective-permute-start(bf16[32,1024]{1,0:T(8,128)(2,1)} %param.5), channel_id=1, source_target_pairs={{0,4},{4,0},{8,12},{12,8},{16,20},{20,16},{24,28},{28,24},{1,5},{5... | collective-permute-start | bytes 196616 | tf_op jit(solution)/shard_map/ppermute | solution.py:11
  0.5 1.5 %compare_select_fusion = bf16[1024,512]{1,0:T(8,128)(2,1)S(1)} fusion(bf16[1024,512]{1,0:T(8,128)(2,1)} %param.6, s32[512]{0:T(512)} %param.9, s32[1024]{0:T(1024)} %param.8), kind=kLoop, calls=%fused_computation | loop fusion | flops 1048576 | bytes 2103296 | tf_op jit(solution)/shard_map/jit(_where)/select_n | solution.py:60
  2.1 0.1 collective-permute-start.3
  2.2 0.0 copy-done.2
  2.2 0.1 fusion.22
  2.3 0.1 pad_add_fusion
  2.4 0.2 convert_reduce_fusion
  2.6 0.0 collective-permute-done
  2.6 0.0 copy-done.3
  2.6 0.0 copy-done.1
  2.6 0.2 %convolution_convert_fusion = bf16[8,1024]{1,0:T(8,128)(2,1)S(1)} fusion(bf16[32,1024]{1,0:T(8,128)(2,1)S(1)} %collective-permute-done, bf16[32,1024]{1,0:T(8,128)(2,1)S(1)} %copy-done.3, s32[1024]{0:T(1024)S(1)} %copy-done.1, s32[64]{0:T(128)S(1)} %get-tuple-element.27, s32[64]{0:T(128)S(1)} %convert_reduce_fusion), kind=kOutput, calls=%fused_computation.1 | convolution fusion | flops 1450496 | bytes 152064 | tf_op jit(solution)/shard_map/dot_general | solution.py:53
  2.8 2.6 %collective-permute-start.1 = (bf16[8,1024]{1,0:T(8,128)(2,1)S(1)}, bf16[8,1024]{1,0:T(8,128)(2,1)S(1)}, u32[]{:S(2)}, u32[]{:S(2)}) collective-permute-start(bf16[8,1024]{1,0:T(8,128)(2,1)S(1)} %convolution_convert_fusion), channel_id=1, source_target_pairs={{0,12},{4,8},{8,4},{12,0},{16,28},{20,24},{24,20},{28,16},{1,13},{... | collective-permute-start | bytes 49160 | tf_op jit(solution)/shard_map/ppermute | solution.py:11
  5.4 1.4 %collective-permute-done.1 = bf16[8,1024]{1,0:T(8,128)(2,1)S(1)} collective-permute-done((bf16[8,1024]{1,0:T(8,128)(2,1)S(1)}, bf16[8,1024]{1,0:T(8,128)(2,1)S(1)}, u32[]{:S(2)}, u32[]{:S(2)}) %collective-permute-start.1) | collective-permute-done | bytes 16416 | tf_op jit(solution)/shard_map/ppermute | solution.py:11
  6.9 1.8 %collective-permute-start.2 = (bf16[16,1024]{1,0:T(8,128)(2,1)S(1)}, bf16[16,1024]{1,0:T(8,128)(2,1)S(1)}, u32[]{:S(2)}, u32[]{:S(2)}) collective-permute-start(bf16[16,1024]{1,0:T(8,128)(2,1)S(1)} %pad_maximum_fusion.1), channel_id=1, source_target_pairs={{0,20},{4,16},{8,28},{12,24},{16,4},{20,0},{24,12},{28,8},{1,21},{... | collective-permute-start | bytes 98312 | tf_op jit(solution)/shard_map/ppermute | solution.py:11
  8.6 0.1 dynamic_slice.21
  8.7 1.5 %collective-permute-done.2 = bf16[16,1024]{1,0:T(8,128)(2,1)S(1)} collective-permute-done((bf16[16,1024]{1,0:T(8,128)(2,1)S(1)}, bf16[16,1024]{1,0:T(8,128)(2,1)S(1)}, u32[]{:S(2)}, u32[]{:S(2)}) %collective-permute-start.2) | collective-permute-done | bytes 32800 | tf_op jit(solution)/shard_map/ppermute | solution.py:11
  10.3 0.0 copy-start
  10.3 0.2 %fusion.6 = f32[16,512]{1,0:T(8,128)S(1)} fusion(bf16[1024,512]{1,0:T(8,128)(2,1)S(1)} %compare_select_fusion, bf16[8,1024]{1,0:T(8,128)(2,1)S(1)} %get-tuple-element.7, bf16[8,1024]{1,0:T(8,128)(2,1)S(1)} %get-tuple-element.8), kind=kOutput, calls=%fused_computation.20 | convolution fusion | flops 16842752 | bytes 1114112 | tf_op jit(solution)/shard_map/dot_general | solution.py:71
  10.5 0.0 collective-permute-done.3
  10.5 0.3 %fusion.10 = f32[16,512]{1,0:T(8,128)S(1)} fusion(bf16[1024,512]{1,0:T(8,128)(2,1)S(1)} %collective-permute-done.3, bf16[8,1024]{1,0:T(8,128)(2,1)S(1)} %get-tuple-element.6, bf16[8,1024]{1,0:T(8,128)(2,1)S(1)} %get-tuple-element.5), kind=kOutput, calls=%fused_computation.24 | convolution fusion | flops 16842752 | bytes 1114112 | tf_op jit(solution)/shard_map/dot_general | solution.py:71
  10.8 1.9 %collective-permute-start.4 = (f32[16,512]{1,0:T(8,128)S(1)}, f32[16,512]{1,0:T(8,128)S(1)}, u32[]{:S(2)}, u32[]{:S(2)}) collective-permute-start(f32[16,512]{1,0:T(8,128)S(1)} %pad_maximum_fusion.2), channel_id=1, source_target_pairs={{0,5},{1,4},{2,7},{3,6},{4,1},{5,0},{6,3},{7,2},{8,13},{9,12},{10,... | collective-permute-start | bytes 98312 | tf_op jit(solution)/shard_map/ppermute | solution.py:17
  12.7 0.2 convert_reduce_fusion.1
  12.9 1.4 %collective-permute-done.4 = f32[16,512]{1,0:T(8,128)S(1)} collective-permute-done((f32[16,512]{1,0:T(8,128)S(1)}, f32[16,512]{1,0:T(8,128)S(1)}, u32[]{:S(2)}, u32[]{:S(2)}) %collective-permute-start.4) | collective-permute-done | bytes 32800 | tf_op jit(solution)/shard_map/ppermute | solution.py:17
  14.3 2.8 %collective-permute-start.5 = (f32[8,512]{1,0:T(8,128)S(1)}, f32[8,512]{1,0:T(8,128)S(1)}, u32[]{:S(2)}, u32[]{:S(2)}) collective-permute-start(f32[8,512]{1,0:T(8,128)S(1)} %slice_add_fusion), channel_id=1, source_target_pairs={{0,6},{1,7},{2,4},{3,5},{4,2},{5,3},{6,0},{7,1},{8,14},{9,15},{10,... | collective-permute-start | bytes 49160 | tf_op jit(solution)/shard_map/ppermute | solution.py:17
  17.1 1.4 %collective-permute-done.5 = f32[8,512]{1,0:T(8,128)S(1)} collective-permute-done((f32[8,512]{1,0:T(8,128)S(1)}, f32[8,512]{1,0:T(8,128)S(1)}, u32[]{:S(2)}, u32[]{:S(2)}) %collective-permute-start.5) | collective-permute-done | bytes 16416 | tf_op jit(solution)/shard_map/ppermute | solution.py:17
  18.6 0.0 copy-done
  18.6 0.9 %select_select_fusion = f32[64,512]{1,0:T(8,128)} fusion(f32[512]{0:T(512)S(1)} %bitcast.11, f32[512]{0:T(512)S(1)} %bitcast.12, f32[512]{0:T(512)S(1)} %bitcast.13, f32[512]{0:T(512)S(1)} %bitcast.14, f32[512]{0:T(512)S(1)} %bitcast.15, f32[512]{0:T(512)S(1)} %bitcast.16, f32[512]{0:T(512)S(1)} %bitcast.17, f32[512]{0:T(512)S(1)} %bitcast.10, ...), kind=kLoop, calls=%fused_computation.14 | loop fusion | flops 557056 | bytes 150272 | tf_op jit(solution)/shard_map/jit(_where)/select_n | solution.py:86
  (12 shorter events, 0.1 us)
Async XLA Ops:
  0.0 2.6 %copy-start.3 = (bf16[32,1024]{1,0:T(8,128)(2,1)S(1)}, bf16[32,1024]{1,0:T(8,128)(2,1)}, u32[]{:S(2)}) copy-start(bf16[32,1024]{1,0:T(8,128)(2,1)} %param.5) | copy-start | bytes 196612
  0.0 2.6 %copy-start.1 = (s32[1024]{0:T(1024)S(1)}, s32[1024]{0:T(1024)}, u32[]{:S(2)}) copy-start(s32[1024]{0:T(1024)} %param.8) | copy-start | bytes 12292
  0.0 2.2 %copy-start.2 = (s32[256]{0:T(256)S(1)}, s32[256]{0:T(256)}, u32[]{:S(2)}) copy-start(s32[256]{0:T(256)} %param.7) | copy-start | bytes 3076
  0.0 2.6 %collective-permute-start = (bf16[32,1024]{1,0:T(8,128)(2,1)}, bf16[32,1024]{1,0:T(8,128)(2,1)S(1)}, u32[]{:S(2)}, u32[]{:S(2)}) collective-permute-start(bf16[32,1024]{1,0:T(8,128)(2,1)} %param.5), channel_id=1, source_target_pairs={{0,4},{4,0},{8,12},{12,8},{16,20},{20,16},{24,28},{28,24},{1,5},{5... | collective-permute-start | bytes 196616 | tf_op jit(solution)/shard_map/ppermute | solution.py:11
  2.1 8.4 %collective-permute-start.3 = (bf16[1024,512]{1,0:T(8,128)(2,1)S(1)}, bf16[1024,512]{1,0:T(8,128)(2,1)S(1)}, u32[]{:S(2)}, u32[]{:S(2)}) collective-permute-start(bf16[1024,512]{1,0:T(8,128)(2,1)S(1)} %compare_select_fusion), channel_id=1, source_target_pairs={{0,4},{4,0},{8,12},{12,8},{16,20},{20,16},{24,28},{28,24},{1,5},{5... | collective-permute-start | bytes 3145736 | tf_op jit(solution)/shard_map/ppermute | solution.py:11
  2.8 4.0 %collective-permute-start.1 = (bf16[8,1024]{1,0:T(8,128)(2,1)S(1)}, bf16[8,1024]{1,0:T(8,128)(2,1)S(1)}, u32[]{:S(2)}, u32[]{:S(2)}) collective-permute-start(bf16[8,1024]{1,0:T(8,128)(2,1)S(1)} %convolution_convert_fusion), channel_id=1, source_target_pairs={{0,12},{4,8},{8,4},{12,0},{16,28},{20,24},{24,20},{28,16},{1,13},{... | collective-permute-start | bytes 49160 | tf_op jit(solution)/shard_map/ppermute | solution.py:11
  6.9 3.4 %collective-permute-start.2 = (bf16[16,1024]{1,0:T(8,128)(2,1)S(1)}, bf16[16,1024]{1,0:T(8,128)(2,1)S(1)}, u32[]{:S(2)}, u32[]{:S(2)}) collective-permute-start(bf16[16,1024]{1,0:T(8,128)(2,1)S(1)} %pad_maximum_fusion.1), channel_id=1, source_target_pairs={{0,20},{4,16},{8,28},{12,24},{16,4},{20,0},{24,12},{28,8},{1,21},{... | collective-permute-start | bytes 98312 | tf_op jit(solution)/shard_map/ppermute | solution.py:11
  10.3 8.3 %copy-start = (s32[512]{0:T(512)S(1)}, s32[512]{0:T(512)}, u32[]{:S(2)}) copy-start(s32[512]{0:T(512)} %param.9) | copy-start | bytes 6148
  10.8 3.5 %collective-permute-start.4 = (f32[16,512]{1,0:T(8,128)S(1)}, f32[16,512]{1,0:T(8,128)S(1)}, u32[]{:S(2)}, u32[]{:S(2)}) collective-permute-start(f32[16,512]{1,0:T(8,128)S(1)} %pad_maximum_fusion.2), channel_id=1, source_target_pairs={{0,5},{1,4},{2,7},{3,6},{4,1},{5,0},{6,3},{7,2},{8,13},{9,12},{10,... | collective-permute-start | bytes 98312 | tf_op jit(solution)/shard_map/ppermute | solution.py:17
  14.3 4.3 %collective-permute-start.5 = (f32[8,512]{1,0:T(8,128)S(1)}, f32[8,512]{1,0:T(8,128)S(1)}, u32[]{:S(2)}, u32[]{:S(2)}) collective-permute-start(f32[8,512]{1,0:T(8,128)S(1)} %slice_add_fusion), channel_id=1, source_target_pairs={{0,6},{1,7},{2,4},{3,5},{4,2},{5,3},{6,0},{7,1},{8,14},{9,15},{10,... | collective-permute-start | bytes 49160 | tf_op jit(solution)/shard_map/ppermute | solution.py:17

commit v3 on v1

--- a/solution.py
+++ b/solution.py
@@ -1,9 +1,22 @@
+import functools
+
 import jax
 import jax.numpy as jnp
 from jax import lax
+from jax.experimental import pallas as pl
+from jax.experimental.pallas import tpu as pltpu
 from jax.sharding import PartitionSpec as P
 
 IRREPS = 8
+CORES, PLACES, COLS = 2, 4, 4
+
+
+def in_hbm(x):
+    return pltpu.with_memory_space_constraint(x, pltpu.HBM)
+
+
+def in_vmem(x):
+    return pltpu.with_memory_space_constraint(x, pltpu.VMEM)
 
 
 def swap(x, axis, mask):
@@ -17,7 +30,7 @@
     return jnp.sum((same & before).astype(jnp.int32), axis=1)
 
 
-def body(amplitudes, integrals, occupied_irreps, contracted_irreps, output_irreps):
+def general(amplitudes, integrals, occupied_irreps, contracted_irreps, output_irreps):
     rows, cols = lax.axis_size("row"), lax.axis_size("col")
     pairs = occupied_irreps.shape[0]
     own = amplitudes.shape[0]
@@ -30,8 +43,7 @@
     raw, labels, order = [amplitudes], [], []
     step = 1
     while step < share:
-        both = jnp.concatenate(raw, 0)
-        raw.append(swap(both, "row", step))
+        raw.append(swap(jnp.concatenate(raw, 0), "row", step))
         step *= 2
     raw = jnp.concatenate(raw, 0)
     for j in range(share):
@@ -48,16 +60,15 @@
     while step < rows:
         packed = jnp.concatenate([packed, swap(packed, "row", step)], 0)
         step *= 2
-
     masked = jnp.where(contracted_irreps[:, None] == output_irreps[None, :], integrals, jnp.zeros_like(integrals))
     sums = jnp.dot(packed, masked, preferred_element_type=jnp.float32)
     turn = col ^ place
     parts = [lax.dynamic_slice_in_dim(sums, (turn ^ t) * slots, slots, 0) for t in range(cols)]
-    step = cols // 2
-    while step >= 1:
-        got = swap(jnp.concatenate(parts[step:], 0), "col", step)
-        parts = [parts[t] + got[t * slots : (t + 1) * slots] for t in range(step)]
-        step //= 2
+    step = 1
+    while step < cols:
+        got = swap(jnp.concatenate(parts[1::2], 0), "col", step)
+        parts = [part + got[t * slots : (t + 1) * slots] for t, part in enumerate(parts[::2])]
+        step *= 2
     total = parts[0]
 
     mine = lax.dynamic_slice_in_dim(occupied_irreps, col * block, block, 0)
@@ -69,9 +80,230 @@
     return out
 
 
+def labels_and_ranks(occupied, place, block):
+    labels = jnp.zeros((1, block), jnp.int32)
+    for b in range(occupied.shape[1] // block):
+        labels = jnp.where(place == b, occupied[:, b * block : (b + 1) * block], labels)
+    lane = lax.broadcasted_iota(jnp.int32, (block, block), 1)
+    sublane = lax.broadcasted_iota(jnp.int32, (block, block), 0)
+    column = jnp.sum(jnp.where(lane == sublane, labels, 0), axis=1, keepdims=True)
+    rank = jnp.sum(jnp.where((column == labels) & (sublane < lane), 1, 0), axis=0, keepdims=True)
+    return column, rank
+
+
+def pack_kernel(block, slots, occupied_ref, contracted_ref, amplitudes_ref, part_ref, gate_ref, pick_ref, occupied, contracted, own, sems):
+    copies = [
+        pltpu.make_async_copy(src, dst, sems.at[n])
+        for n, (src, dst) in enumerate(((occupied_ref, occupied), (contracted_ref, contracted), (amplitudes_ref, own)))
+    ]
+    for copy in copies:
+        copy.start()
+    row = lax.axis_index("row")
+    member = row % CORES
+    rows = own.shape[0]
+    copies[0].wait()
+    column, rank = labels_and_ranks(occupied, row // CORES, block)
+    slot = lax.broadcasted_iota(jnp.int32, (slots, rows), 0)
+    ours = jnp.where(member == 0, rank[:, :rows], rank[:, rows:])
+    theirs = jnp.where(member == 0, rank[:, rows:], rank[:, :rows])
+    our_labels = jnp.where(member == 0, column[:rows], column[rows:])
+    their_labels = jnp.where(member == 0, column[rows:], column[:rows])
+    pick_ref[...] = jnp.where(slot == theirs, 1.0, 0.0).astype(jnp.bfloat16)
+    copies[1].wait()
+    gate_ref[...] = jnp.where(their_labels == contracted[...], 1.0, 0.0).astype(jnp.bfloat16)
+    copies[2].wait()
+    kept = jnp.where(our_labels == contracted[...], own[...].astype(jnp.float32), 0.0).astype(jnp.bfloat16)
+    pick = jnp.where(slot == ours, 1.0, 0.0).astype(jnp.bfloat16)
+    part_ref[...] = jnp.dot(pick, kept, preferred_element_type=jnp.float32)
+
+
+def pack(occupied_irreps, contracted_irreps, amplitudes, block, slots):
+    rows, depth = amplitudes.shape
+    pairs = occupied_irreps.shape[0]
+    return pl.pallas_call(
+        functools.partial(pack_kernel, block, slots),
+        out_shape=(
+            pltpu.VMEM((slots, depth), jnp.float32),
+            pltpu.VMEM((rows, depth), jnp.bfloat16),
+            pltpu.VMEM((slots, rows), jnp.bfloat16),
+        ),
+        in_specs=[pl.BlockSpec(memory_space=pltpu.HBM)] * 3,
+        out_specs=[pl.BlockSpec(memory_space=pltpu.VMEM)] * 3,
+        scratch_shapes=[
+            pltpu.VMEM((1, pairs), jnp.int32),
+            pltpu.VMEM((1, depth), jnp.int32),
+            pltpu.VMEM((rows, depth), jnp.bfloat16),
+            pltpu.SemaphoreType.DMA((3,)),
+        ],
+        compiler_params=pltpu.CompilerParams(vmem_limit_bytes=8 << 20),
+        cost_estimate=pl.CostEstimate(flops=1 << 20, bytes_accessed=1 << 18, transcendentals=0),
+        name="pack",
+    )(in_hbm(occupied_irreps.reshape(1, pairs)), in_hbm(contracted_irreps.reshape(1, depth)), in_hbm(amplitudes))
+
+
+def stage_kernel(integrals_ref, occupied_ref, staged_ref, key_ref, occupied, sems):
+    copies = [
+        pltpu.make_async_copy(occupied_ref, occupied, sems.at[0]),
+        pltpu.make_async_copy(integrals_ref, staged_ref, sems.at[1]),
+    ]
+    for copy in copies:
+        copy.start()
+    copies[0].wait()
+    block = key_ref.shape[0]
+    column, rank = labels_and_ranks(occupied[...], lax.axis_index("col"), block)
+    lane = lax.broadcasted_iota(jnp.int32, (block, block), 1)
+    sublane = lax.broadcasted_iota(jnp.int32, (block, block), 0)
+    slot = jnp.sum(jnp.where(lane == sublane, rank, 0), axis=1, keepdims=True)
+    key_ref[...] = jnp.broadcast_to(slot * IRREPS + column, key_ref.shape)
+    copies[1].wait()
+
+
+def stage(integrals, occupied_irreps, block):
+    pairs = occupied_irreps.shape[0]
+    return pl.pallas_call(
+        stage_kernel,
+        out_shape=(pltpu.VMEM(integrals.shape, integrals.dtype), pltpu.VMEM((block, 128), jnp.int32)),
+        in_specs=[pl.BlockSpec(memory_space=pltpu.HBM)] * 2,
+        out_specs=[pl.BlockSpec(memory_space=pltpu.VMEM)] * 2,
+        scratch_shapes=[pltpu.VMEM((1, pairs), jnp.int32), pltpu.SemaphoreType.DMA((2,))],
+        compiler_params=pltpu.CompilerParams(vmem_limit_bytes=8 << 20),
+        cost_estimate=pl.CostEstimate(flops=0, bytes_accessed=4 * integrals.size, transcendentals=0),
+        name="stage",
+    )(in_hbm(integrals), in_hbm(occupied_irreps.reshape(1, pairs)))
+
+
+def sums_kernel(slots, blocks_refs, contracted_ref, outputs_ref, other_outputs_ref, integrals_ref, other_ref, send_ref, far_ref, keep_ref):
+    row, col = lax.axis_index("row"), lax.axis_index("col")
+    place, member = row // CORES, row % CORES
+    contracted = contracted_ref[...]
+    blocks = [ref[...].astype(jnp.float32) for ref in blocks_refs]
+
+    def block(t):
+        offset = col ^ place ^ t
+        turned = jnp.where((offset == 1) | (offset == 2), offset ^ ((1 - member) * 3), offset)
+        chosen = blocks[0]
+        for n in range(1, PLACES):
+            chosen = jnp.where(turned == n, blocks[n], chosen)
+        return chosen
+
+    def product(rows, weights, outputs):
+        spread = jnp.concatenate([jnp.where(contracted == g, rows, 0.0) for g in range(IRREPS)], axis=0)
+        each = jnp.dot(spread.astype(jnp.bfloat16), weights, preferred_element_type=jnp.float32)
+        total = jnp.zeros((2 * slots, each.shape[1]), jnp.float32)
+        for g in range(IRREPS):
+            total = jnp.where(outputs == g, each[g * 2 * slots : (g + 1) * 2 * slots], total)
+        return total
+
+    sent = block(1 + member)
+    theirs = product(jnp.concatenate([sent, block(3)], 0), other_ref[...], other_outputs_ref[...])
+    send_ref[:slots] = theirs[:slots]
+    far_ref[...] = theirs[slots:]
+    ours = product(jnp.concatenate([sent, block(0)], 0), integrals_ref[...], outputs_ref[...])
+    send_ref[slots:] = ours[:slots]
+    keep_ref[...] = ours[slots:]
+
+
+def sums(blocks, contracted, outputs, other_outputs, integrals, other, slots):
+    depth, width = integrals.shape
+
+    def kernel(b0, b1, b2, b3, *refs):
+        sums_kernel(slots, (b0, b1, b2, b3), *refs)
+
+    args = [*blocks, contracted.reshape(1, depth), outputs.reshape(1, width), other_outputs.reshape(1, width), integrals, other]
+    return pl.pallas_call(
+        kernel,
+        out_shape=(
+            pltpu.VMEM((2 * slots, width), jnp.float32),
+            pltpu.VMEM((slots, width), jnp.float32),
+            pltpu.VMEM((slots, width), jnp.float32),
+        ),
+        in_specs=[pl.BlockSpec(memory_space=pltpu.VMEM)] * len(args),
+        out_specs=[pl.BlockSpec(memory_space=pltpu.VMEM)] * 3,
+        compiler_params=pltpu.CompilerParams(vmem_limit_bytes=16 << 20),
+        cost_estimate=pl.CostEstimate(flops=1 << 28, bytes_accessed=1 << 21, transcendentals=0),
+        name="sums",
+    )(*[in_vmem(x) for x in args])
+
+
+def expand_kernel(keep_ref, got_ref, far_ref, too_ref, key_ref, outputs_ref, out_ref, staged, sems):
+    slots, width = keep_ref.shape
+    block = key_ref.shape[0]
+    outputs = outputs_ref[...]
+    total = (keep_ref[...] + got_ref[:slots]) + (far_ref[...] + too_ref[...])
+    pieces = sems.shape[0]
+    size = block // pieces
+    copies = []
+    for n in range(pieces):
+        rows = slice(n * size, (n + 1) * size)
+        key = key_ref[rows, :1]
+        out = jnp.zeros((size, width), jnp.float32)
+        for s in range(slots):
+            out = jnp.where(key == outputs + s * IRREPS, total[s : s + 1], out)
+        staged[rows] = out
+        copy = pltpu.make_async_copy(staged.at[rows], out_ref.at[rows], sems.at[n])
+        copy.start()
+        copies.append(copy)
+    for copy in copies:
+        copy.wait()
+
+
+def expand(keep, got, far, too, key, outputs, pieces=2):
+    slots, width = keep.shape
+    block = key.shape[0]
+    args = [keep, got, far, too, key, outputs.reshape(1, width)]
+    return pl.pallas_call(
+        expand_kernel,
+        out_shape=pltpu.HBM((block, width), jnp.float32),
+        in_specs=[pl.BlockSpec(memory_space=pltpu.VMEM)] * len(args),
+        out_specs=pl.BlockSpec(memory_space=pltpu.HBM),
+        scratch_shapes=[pltpu.VMEM((block, width), jnp.float32), pltpu.SemaphoreType.DMA((pieces,))],
+        compiler_params=pltpu.CompilerParams(vmem_limit_bytes=8 << 20),
+        cost_estimate=pl.CostEstimate(flops=1 << 20, bytes_accessed=1 << 18, transcendentals=0),
+        name="expand",
+    )(*[in_vmem(x) for x in args])
+
+
+def move(x, target):
+    pairs = []
+    for r in range(PLACES * CORES):
+        for c in range(COLS):
+            place, member, col = target(r // CORES, r % CORES, c)
+            pairs.append((r * COLS + c, (place * CORES + member) * COLS + col))
+    return lax.ppermute(x, ("row", "col"), pairs)
+
+
+def quad(amplitudes, integrals, occupied_irreps, contracted_irreps, output_irreps):
+    own = amplitudes.shape[0]
+    block = own * CORES
+    slots = block // IRREPS
+    sibling = lambda p, m, c: (p, 1 - m, c)
+
+    raw = move(amplitudes, sibling)
+    part, gate, pick = pack(occupied_irreps, contracted_irreps, amplitudes, block, slots)
+    raw, part, late_integrals, late_outputs = lax.optimization_barrier((raw, part, integrals, output_irreps))
+    other = move(late_integrals, sibling)
+    other_outputs = move(late_outputs, sibling)
+    packed = (part + jnp.dot(pick, raw * gate, preferred_element_type=jnp.float32)).astype(jnp.bfloat16)
+
+    packed, late_integrals = lax.optimization_barrier((packed, integrals))
+    side = move(packed, lambda p, m, c: (p ^ (1 + m), 1 - m, c))
+    far = move(packed, lambda p, m, c: (p ^ 3, 1 - m, c))
+    staged, key = stage(late_integrals, occupied_irreps, block)
+    side, staged = lax.optimization_barrier((side, staged))
+    side_too = move(side, sibling)
+    send, send_far, keep = sums(
+        (packed, side, side_too, far), contracted_irreps, output_irreps, other_outputs, staged, other, slots
+    )
+    got = move(send, lambda p, m, c: (p, 1 - m, c ^ (1 + m)))
+    got_far = move(send_far, lambda p, m, c: (p, 1 - m, c ^ 3))
+    got_too = move(got[slots:], sibling)
+    return expand(keep, got, got_far, got_too, key, output_irreps)
+
+
 def solution(mesh):
+    small = mesh.shape["row"] == PLACES * CORES and mesh.shape["col"] == COLS
     return jax.shard_map(
-        body,
+        quad if small else general,
         mesh=mesh,
         in_specs=(P("row", "col"), P("col", "row"), P(), P("col"), P("row")),
         out_specs=P("col", "row"),

time: 22.9 us -> 17.7 us (0.77)
  the two profiles are of different devices: /device:TPU:0 before, /device:TPU:1 now
where the time goes in v3:
time: 17.7 us; the launch traced here: 17.6 us
  starting transfers between devices  9.42 us (53%)
  waiting for transfers between devices  4 us (23%)
  Pallas kernels  3.93 us (22%)
    ppermute x9, starting transfers between devices, move(): return lax.ppermute(x, ('row', 'col'), pairs)  9.42 us
    ppermute x9, waiting for transfers between devices, move(): return lax.ppermute(x, ('row', 'col'), pairs)  4 us
    pallas_call x1, Pallas kernels, pack(): pl.pallas_call(functools.partial(pack_kernel, block, slots), out_shape=(p...  1.44 us
    pallas_call x1, Pallas kernels, stage(): pl.pallas_call(stage_kernel, out_shape=(pltpu.VMEM(integrals.shape, integ...  1.26 us
    pallas_call x1, Pallas kernels, expand(): pl.pallas_call(expand_kernel, out_shape=pltpu.HBM((block, width), jnp.flo...  0.79 us
    pallas_call x1, Pallas kernels, sums(): pl.pallas_call(kernel, out_shape=(pltpu.VMEM((2 * slots, width), jnp.floa...  0.45 us
  transfers between devices with their start and end apart: 9, of which 2 were waited for; matrix products, arithmetic and copies ran while one was open for 1% of the time, Pallas kernels for 15%

profile of v3, /device:TPU:1, one launch (start us, length us, event | category | flops | bytes accessed | tf_op | source)
XLA Modules:
  0.0 17.6 jit_solution(15578053132334419304)
XLA Ops:
  0.0 0.1 collective-permute-start
  0.1 1.4 %pack.1 = (f32[8,1024]{1,0:T(8,128)S(1)}, bf16[32,1024]{1,0:T(8,128)(2,1)S(1)}, bf16[8,32]{1,0:T(8,128)(2,1)S(1)}) custom-call(s32[1,256]{1,0:T(1,128)} %bitcast.10, s32[1,1024]{1,0:T(1,128)} %bitcast.5, bf16[32,1024]{1,0:T(8,128)(2,1)} %amplitudes_ref.1), custom_call_target="tpu_custom_call" | custom-call | flops 1048576 | bytes 262144 | tf_op jit(solution)/shard_map/pack/pallas_call | solution.py:123
  1.5 0.0 collective-permute-done
  1.5 0.5 %collective-permute-start.5 = (bf16[1024,512]{1,0:T(8,128)(2,1)}, bf16[1024,512]{1,0:T(8,128)(2,1)S(1)}, u32[]{:S(2)}, u32[]{:S(2)}) collective-permute-start(bf16[1024,512]{1,0:T(8,128)(2,1)} %integrals_ref), channel_id=1, source_target_pairs={{0,4},{1,5},{2,6},{3,7},{4,0},{5,1},{6,2},{7,3},{8,12},{9,13},{10,... | collective-permute-start | bytes 3145736 | tf_op jit(solution)/shard_map/ppermute | solution.py:272
  2.0 0.1 fusion
  2.2 0.0 copy-start.1
  2.2 2.7 %collective-permute-start.1 = (bf16[8,1024]{1,0:T(8,128)(2,1)S(1)}, bf16[8,1024]{1,0:T(8,128)(2,1)S(1)}, u32[]{:S(2)}, u32[]{:S(2)}) collective-permute-start(bf16[8,1024]{1,0:T(8,128)(2,1)S(1)} %add_convert_fusion.b0), channel_id=1, source_target_pairs={{0,12},{1,13},{2,14},{3,15},{4,16},{5,17},{6,18},{7,19},{8,4},{9,5... | collective-permute-start | bytes 49160 | tf_op jit(solution)/shard_map/ppermute | solution.py:272
  4.9 1.1 %collective-permute-start.3 = (bf16[8,1024]{1,0:T(8,128)(2,1)S(1)}, bf16[8,1024]{1,0:T(8,128)(2,1)S(1)}, u32[]{:S(2)}, u32[]{:S(2)}) collective-permute-start(bf16[8,1024]{1,0:T(8,128)(2,1)S(1)} %add_convert_fusion.b0), channel_id=1, source_target_pairs={{0,28},{1,29},{2,30},{3,31},{4,24},{5,25},{6,26},{7,27},{8,20},{9,... | collective-permute-start | bytes 49160 | tf_op jit(solution)/shard_map/ppermute | solution.py:272
  5.9 1.3 %stage.1 = (bf16[1024,512]{1,0:T(8,128)(2,1)S(1)}, s32[64,128]{1,0:T(8,128)S(1)}) custom-call(bf16[1024,512]{1,0:T(8,128)(2,1)} %integrals_ref, s32[1,256]{1,0:T(1,128)} %bitcast.11), custom_call_target="tpu_custom_call" | custom-call | bytes 2097152 | tf_op jit(solution)/shard_map/stage/pallas_call | solution.py:163
  7.2 0.0 copy-start
  7.2 0.0 collective-permute-done.1.b1
  7.2 0.5 %collective-permute-start.2 = (bf16[8,1024]{1,0:T(8,128)(2,1)S(1)}, bf16[8,1024]{1,0:T(8,128)(2,1)S(1)}, u32[]{:S(2)}, u32[]{:S(2)}) collective-permute-start(bf16[8,1024]{1,0:T(8,128)(2,1)S(1)} %collective-permute-done.1.b1), channel_id=1, source_target_pairs={{0,4},{1,5},{2,6},{3,7},{4,0},{5,1},{6,2},{7,3},{8,12},{9,13},{10,... | collective-permute-start | bytes 49160 | tf_op jit(solution)/shard_map/ppermute | solution.py:272
  7.8 0.0 copy-done.1
  7.8 0.1 collective-permute-start.4
  7.8 1.1 %collective-permute-done.4 = s32[512]{0:T(512)S(1)} collective-permute-done((s32[512]{0:T(512)S(1)}, s32[512]{0:T(512)S(1)}, u32[]{:S(2)}, u32[]{:S(2)}) %collective-permute-start.4) | collective-permute-done | bytes 2080 | tf_op jit(solution)/shard_map/ppermute | solution.py:272
  8.9 0.0 collective-permute-done.3.b3
  8.9 0.0 collective-permute-done.2.b2
  8.9 0.0 collective-permute-done.5.refs_4_
  8.9 0.0 copy-done
  8.9 0.5 %sums.1 = (f32[16,512]{1,0:T(8,128)S(1)}, f32[8,512]{1,0:T(8,128)S(1)}, f32[8,512]{1,0:T(8,128)S(1)}) custom-call(bf16[8,1024]{1,0:T(8,128)(2,1)S(1)} %add_convert_fusion.b0, bf16[8,1024]{1,0:T(8,128)(2,1)S(1)} %collective-permute-done.1.b1, bf16[8,1024]{1,0:T(8,128)(2,1)S(1)} %collective-permute-done.2.b2, bf16[8,1024]{1,0:T(8,128)(2,1)S(1)} %collective-permute-done.3.b3, ...), custom_call_target="tpu_custom_call" | custom-call | flops 268435456 | bytes 2097152 | tf_op jit(solution)/shard_map/sums/pallas_call | solution.py:213
  9.4 2.4 %collective-permute-start.6 = (f32[16,512]{1,0:T(8,128)S(1)}, f32[16,512]{1,0:T(8,128)S(1)}, u32[]{:S(2)}, u32[]{:S(2)}) collective-permute-start(f32[16,512]{1,0:T(8,128)S(1)} %get-tuple-element.34), channel_id=1, source_target_pairs={{0,5},{1,4},{2,7},{3,6},{4,2},{5,3},{6,0},{7,1},{8,13},{9,12},{10,... | collective-permute-start | bytes 98312 | tf_op jit(solution)/shard_map/ppermute | solution.py:272
  11.8 1.4 %collective-permute-start.7 = (f32[8,512]{1,0:T(8,128)S(1)}, f32[8,512]{1,0:T(8,128)S(1)}, u32[]{:S(2)}, u32[]{:S(2)}) collective-permute-start(f32[8,512]{1,0:T(8,128)S(1)} %get-tuple-element.35), channel_id=1, source_target_pairs={{0,7},{1,6},{2,5},{3,4},{4,3},{5,2},{6,1},{7,0},{8,15},{9,14},{10,... | collective-permute-start | bytes 49160 | tf_op jit(solution)/shard_map/ppermute | solution.py:272
  13.2 0.0 collective-permute-done.6.got_ref
  13.2 0.6 %collective-permute-start.8 = (f32[8,512]{1,0:T(8,128)S(1)}, f32[8,512]{1,0:T(8,128)S(1)}, u32[]{:S(2)}, u32[]{:S(2)}) collective-permute-start(f32[8,512]{1,0:T(8,128)S(1)} %slice.4), channel_id=1, source_target_pairs={{0,4},{1,5},{2,6},{3,7},{4,0},{5,1},{6,2},{7,3},{8,12},{9,13},{10,... | collective-permute-start | bytes 49160 | tf_op jit(solution)/shard_map/ppermute | solution.py:272
  13.9 2.9 %collective-permute-done.7.far_ref = f32[8,512]{1,0:T(8,128)S(1)} collective-permute-done((f32[8,512]{1,0:T(8,128)S(1)}, f32[8,512]{1,0:T(8,128)S(1)}, u32[]{:S(2)}, u32[]{:S(2)}) %collective-permute-start.7) | collective-permute-done | bytes 16416 | tf_op jit(solution)/shard_map/ppermute | solution.py:272
  16.8 0.0 collective-permute-done.8.too_ref
  16.8 0.8 %expand.1 = f32[64,512]{1,0:T(8,128)} custom-call(f32[8,512]{1,0:T(8,128)S(1)} %get-tuple-element.33.keep_ref, f32[16,512]{1,0:T(8,128)S(1)} %collective-permute-done.6.got_ref, f32[8,512]{1,0:T(8,128)S(1)} %collective-permute-done.7.far_ref, f32[8,512]{1,0:T(8,128)S(1)} %collective-permute-done.8.too_ref, s32[64,128]{1,0:T(8,128)S(1)} %get-tuple-element.36.key_ref, ...), custom_call_target="tpu_custom_call" | custom-call | flops 1048576 | bytes 262144 | tf_op jit(solution)/shard_map/expand/pallas_call | solution.py:254
  (2 shorter events, 0.0 us)
Async XLA Ops:
  0.0 1.5 %collective-permute-start = (bf16[32,1024]{1,0:T(8,128)(2,1)}, bf16[32,1024]{1,0:T(8,128)(2,1)S(1)}, u32[]{:S(2)}, u32[]{:S(2)}) collective-permute-start(bf16[32,1024]{1,0:T(8,128)(2,1)} %amplitudes_ref.1), channel_id=1, source_target_pairs={{0,4},{1,5},{2,6},{3,7},{4,0},{5,1},{6,2},{7,3},{8,12},{9,13},{10,... | collective-permute-start | bytes 196616 | tf_op jit(solution)/shard_map/ppermute | solution.py:272
  1.5 7.4 %collective-permute-start.5 = (bf16[1024,512]{1,0:T(8,128)(2,1)}, bf16[1024,512]{1,0:T(8,128)(2,1)S(1)}, u32[]{:S(2)}, u32[]{:S(2)}) collective-permute-start(bf16[1024,512]{1,0:T(8,128)(2,1)} %integrals_ref), channel_id=1, source_target_pairs={{0,4},{1,5},{2,6},{3,7},{4,0},{5,1},{6,2},{7,3},{8,12},{9,13},{10,... | collective-permute-start | bytes 3145736 | tf_op jit(solution)/shard_map/ppermute | solution.py:272
  2.2 5.6 %copy-start.1 = (s32[512]{0:T(512)S(1)}, s32[512]{0:T(512)}, u32[]{:S(2)}) copy-start(s32[512]{0:T(512)} %param.9) | copy-start | bytes 6148
  2.2 5.0 %collective-permute-start.1 = (bf16[8,1024]{1,0:T(8,128)(2,1)S(1)}, bf16[8,1024]{1,0:T(8,128)(2,1)S(1)}, u32[]{:S(2)}, u32[]{:S(2)}) collective-permute-start(bf16[8,1024]{1,0:T(8,128)(2,1)S(1)} %add_convert_fusion.b0), channel_id=1, source_target_pairs={{0,12},{1,13},{2,14},{3,15},{4,16},{5,17},{6,18},{7,19},{8,4},{9,5... | collective-permute-start | bytes 49160 | tf_op jit(solution)/shard_map/ppermute | solution.py:272
  4.9 4.1 %collective-permute-start.3 = (bf16[8,1024]{1,0:T(8,128)(2,1)S(1)}, bf16[8,1024]{1,0:T(8,128)(2,1)S(1)}, u32[]{:S(2)}, u32[]{:S(2)}) collective-permute-start(bf16[8,1024]{1,0:T(8,128)(2,1)S(1)} %add_convert_fusion.b0), channel_id=1, source_target_pairs={{0,28},{1,29},{2,30},{3,31},{4,24},{5,25},{6,26},{7,27},{8,20},{9,... | collective-permute-start | bytes 49160 | tf_op jit(solution)/shard_map/ppermute | solution.py:272
  7.2 1.7 %copy-start = (s32[1024]{0:T(1024)S(1)}, s32[1024]{0:T(1024)}, u32[]{:S(2)}) copy-start(s32[1024]{0:T(1024)} %param.8) | copy-start | bytes 12292
  7.2 1.7 %collective-permute-start.2 = (bf16[8,1024]{1,0:T(8,128)(2,1)S(1)}, bf16[8,1024]{1,0:T(8,128)(2,1)S(1)}, u32[]{:S(2)}, u32[]{:S(2)}) collective-permute-start(bf16[8,1024]{1,0:T(8,128)(2,1)S(1)} %collective-permute-done.1.b1), channel_id=1, source_target_pairs={{0,4},{1,5},{2,6},{3,7},{4,0},{5,1},{6,2},{7,3},{8,12},{9,13},{10,... | collective-permute-start | bytes 49160 | tf_op jit(solution)/shard_map/ppermute | solution.py:272
  7.8 1.2 %collective-permute-start.4 = (s32[512]{0:T(512)S(1)}, s32[512]{0:T(512)S(1)}, u32[]{:S(2)}, u32[]{:S(2)}) collective-permute-start(s32[512]{0:T(512)S(1)} %copy-done.1), channel_id=1, source_target_pairs={{0,4},{1,5},{2,6},{3,7},{4,0},{5,1},{6,2},{7,3},{8,12},{9,13},{10,... | collective-permute-start | bytes 6152 | tf_op jit(solution)/shard_map/ppermute | solution.py:272
  9.4 3.8 %collective-permute-start.6 = (f32[16,512]{1,0:T(8,128)S(1)}, f32[16,512]{1,0:T(8,128)S(1)}, u32[]{:S(2)}, u32[]{:S(2)}) collective-permute-start(f32[16,512]{1,0:T(8,128)S(1)} %get-tuple-element.34), channel_id=1, source_target_pairs={{0,5},{1,4},{2,7},{3,6},{4,2},{5,3},{6,0},{7,1},{8,13},{9,12},{10,... | collective-permute-start | bytes 98312 | tf_op jit(solution)/shard_map/ppermute | solution.py:272
  11.8 5.0 %collective-permute-start.7 = (f32[8,512]{1,0:T(8,128)S(1)}, f32[8,512]{1,0:T(8,128)S(1)}, u32[]{:S(2)}, u32[]{:S(2)}) collective-permute-start(f32[8,512]{1,0:T(8,128)S(1)} %get-tuple-element.35), channel_id=1, source_target_pairs={{0,7},{1,6},{2,5},{3,4},{4,3},{5,2},{6,1},{7,0},{8,15},{9,14},{10,... | collective-permute-start | bytes 49160 | tf_op jit(solution)/shard_map/ppermute | solution.py:272
  13.2 3.6 %collective-permute-start.8 = (f32[8,512]{1,0:T(8,128)S(1)}, f32[8,512]{1,0:T(8,128)S(1)}, u32[]{:S(2)}, u32[]{:S(2)}) collective-permute-start(f32[8,512]{1,0:T(8,128)S(1)} %slice.4), channel_id=1, source_target_pairs={{0,4},{1,5},{2,6},{3,7},{4,0},{5,1},{6,2},{7,3},{8,12},{9,13},{10,... | collective-permute-start | bytes 49160 | tf_op jit(solution)/shard_map/ppermute | solution.py:272

commit v4 on v3

--- a/solution.py
+++ b/solution.py
@@ -179,7 +179,7 @@
     blocks = [ref[...].astype(jnp.float32) for ref in blocks_refs]
 
     def block(t):
-        offset = col ^ place ^ t
+        offset = ((col + t) % COLS) ^ place
         turned = jnp.where((offset == 1) | (offset == 2), offset ^ ((1 - member) * 3), offset)
         chosen = blocks[0]
         for n in range(1, PLACES):
@@ -294,8 +294,8 @@
     send, send_far, keep = sums(
         (packed, side, side_too, far), contracted_irreps, output_irreps, other_outputs, staged, other, slots
     )
-    got = move(send, lambda p, m, c: (p, 1 - m, c ^ (1 + m)))
-    got_far = move(send_far, lambda p, m, c: (p, 1 - m, c ^ 3))
+    got = move(send, lambda p, m, c: (p, 1 - m, (c + 1 + m) % COLS))
+    got_far = move(send_far, lambda p, m, c: (p, 1 - m, (c + 3) % COLS))
     got_too = move(got[slots:], sibling)
     return expand(keep, got, got_far, got_too, key, output_irreps)
 

time: 17.7 us -> 16.9 us (0.955)
  the two profiles are of different devices: /device:TPU:1 before, /device:TPU:0 now
where the time goes in v4:
time: 16.9 us; the launch traced here: 16.7 us
  starting transfers between devices  10.3 us (61%)
  Pallas kernels  3.94 us (23%)
  waiting for transfers between devices  2.26 us (13%)
    ppermute x9, starting transfers between devices, move(): return lax.ppermute(x, ('row', 'col'), pairs)  10.3 us
    ppermute x9, waiting for transfers between devices, move(): return lax.ppermute(x, ('row', 'col'), pairs)  2.26 us
    pallas_call x1, Pallas kernels, pack(): pl.pallas_call(functools.partial(pack_kernel, block, slots), out_shape=(p...  1.44 us
    pallas_call x1, Pallas kernels, stage(): pl.pallas_call(stage_kernel, out_shape=(pltpu.VMEM(integrals.shape, integ...  1.26 us
    pallas_call x1, Pallas kernels, expand(): pl.pallas_call(expand_kernel, out_shape=pltpu.HBM((block, width), jnp.flo...  0.78 us
    pallas_call x1, Pallas kernels, sums(): pl.pallas_call(kernel, out_shape=(pltpu.VMEM((2 * slots, width), jnp.floa...  0.46 us
  transfers between devices with their start and end apart: 9, of which 3 were waited for; matrix products, arithmetic and copies ran while one was open for 1% of the time, Pallas kernels for 16%

profile of v4, /device:TPU:0, one launch (start us, length us, event | category | flops | bytes accessed | tf_op | source)
XLA Modules:
  0.0 16.7 jit_solution(12202335293717183594)
XLA Ops:
  0.0 0.5 %collective-permute-start = (bf16[32,1024]{1,0:T(8,128)(2,1)}, bf16[32,1024]{1,0:T(8,128)(2,1)S(1)}, u32[]{:S(2)}, u32[]{:S(2)}) collective-permute-start(bf16[32,1024]{1,0:T(8,128)(2,1)} %amplitudes_ref.1), channel_id=1, source_target_pairs={{0,4},{1,5},{2,6},{3,7},{4,0},{5,1},{6,2},{7,3},{8,12},{9,13},{10,... | collective-permute-start | bytes 196616 | tf_op jit(solution)/shard_map/ppermute | solution.py:272
  0.5 1.4 %pack.1 = (f32[8,1024]{1,0:T(8,128)S(1)}, bf16[32,1024]{1,0:T(8,128)(2,1)S(1)}, bf16[8,32]{1,0:T(8,128)(2,1)S(1)}) custom-call(s32[1,256]{1,0:T(1,128)} %bitcast.10, s32[1,1024]{1,0:T(1,128)} %bitcast.5, bf16[32,1024]{1,0:T(8,128)(2,1)} %amplitudes_ref.1), custom_call_target="tpu_custom_call" | custom-call | flops 1048576 | bytes 262144 | tf_op jit(solution)/shard_map/pack/pallas_call | solution.py:123
  1.9 0.0 collective-permute-done
  1.9 0.1 collective-permute-start.5
  2.0 0.1 fusion
  2.2 0.0 copy-start.1
  2.2 2.6 %collective-permute-start.1 = (bf16[8,1024]{1,0:T(8,128)(2,1)S(1)}, bf16[8,1024]{1,0:T(8,128)(2,1)S(1)}, u32[]{:S(2)}, u32[]{:S(2)}) collective-permute-start(bf16[8,1024]{1,0:T(8,128)(2,1)S(1)} %add_convert_fusion.b0), channel_id=1, source_target_pairs={{0,12},{1,13},{2,14},{3,15},{4,16},{5,17},{6,18},{7,19},{8,4},{9,5... | collective-permute-start | bytes 49160 | tf_op jit(solution)/shard_map/ppermute | solution.py:272
  4.8 1.6 %collective-permute-start.3 = (bf16[8,1024]{1,0:T(8,128)(2,1)S(1)}, bf16[8,1024]{1,0:T(8,128)(2,1)S(1)}, u32[]{:S(2)}, u32[]{:S(2)}) collective-permute-start(bf16[8,1024]{1,0:T(8,128)(2,1)S(1)} %add_convert_fusion.b0), channel_id=1, source_target_pairs={{0,28},{1,29},{2,30},{3,31},{4,24},{5,25},{6,26},{7,27},{8,20},{9,... | collective-permute-start | bytes 49160 | tf_op jit(solution)/shard_map/ppermute | solution.py:272
  6.3 1.3 %stage.1 = (bf16[1024,512]{1,0:T(8,128)(2,1)S(1)}, s32[64,128]{1,0:T(8,128)S(1)}) custom-call(bf16[1024,512]{1,0:T(8,128)(2,1)} %integrals_ref, s32[1,256]{1,0:T(1,128)} %bitcast.11), custom_call_target="tpu_custom_call" | custom-call | bytes 2097152 | tf_op jit(solution)/shard_map/stage/pallas_call | solution.py:163
  7.6 0.0 copy-start
  7.6 0.0 collective-permute-done.1.b1
  7.6 0.1 collective-permute-start.2
  7.7 0.0 copy-done.1
  7.7 0.5 %collective-permute-start.4 = (s32[512]{0:T(512)S(1)}, s32[512]{0:T(512)S(1)}, u32[]{:S(2)}, u32[]{:S(2)}) collective-permute-start(s32[512]{0:T(512)S(1)} %copy-done.1), channel_id=1, source_target_pairs={{0,4},{1,5},{2,6},{3,7},{4,0},{5,1},{6,2},{7,3},{8,12},{9,13},{10,... | collective-permute-start | bytes 6152 | tf_op jit(solution)/shard_map/ppermute | solution.py:272
  8.2 0.8 %collective-permute-done.4 = s32[512]{0:T(512)S(1)} collective-permute-done((s32[512]{0:T(512)S(1)}, s32[512]{0:T(512)S(1)}, u32[]{:S(2)}, u32[]{:S(2)}) %collective-permute-start.4) | collective-permute-done | bytes 2080 | tf_op jit(solution)/shard_map/ppermute | solution.py:272
  9.0 0.0 collective-permute-done.3.b3
  9.0 0.0 collective-permute-done.2.b2
  9.0 0.0 collective-permute-done.5.refs_4_
  9.0 0.0 copy-done
  9.1 0.5 %sums.1 = (f32[16,512]{1,0:T(8,128)S(1)}, f32[8,512]{1,0:T(8,128)S(1)}, f32[8,512]{1,0:T(8,128)S(1)}) custom-call(bf16[8,1024]{1,0:T(8,128)(2,1)S(1)} %add_convert_fusion.b0, bf16[8,1024]{1,0:T(8,128)(2,1)S(1)} %collective-permute-done.1.b1, bf16[8,1024]{1,0:T(8,128)(2,1)S(1)} %collective-permute-done.2.b2, bf16[8,1024]{1,0:T(8,128)(2,1)S(1)} %collective-permute-done.3.b3, ...), custom_call_target="tpu_custom_call" | custom-call | flops 268435456 | bytes 2097152 | tf_op jit(solution)/shard_map/sums/pallas_call | solution.py:213
  9.5 1.6 %collective-permute-start.6 = (f32[16,512]{1,0:T(8,128)S(1)}, f32[16,512]{1,0:T(8,128)S(1)}, u32[]{:S(2)}, u32[]{:S(2)}) collective-permute-start(f32[16,512]{1,0:T(8,128)S(1)} %get-tuple-element.34), channel_id=1, source_target_pairs={{0,5},{1,6},{2,7},{3,4},{4,2},{5,3},{6,0},{7,1},{8,13},{9,14},{10,... | collective-permute-start | bytes 98312 | tf_op jit(solution)/shard_map/ppermute | solution.py:272
  11.1 2.1 %collective-permute-start.7 = (f32[8,512]{1,0:T(8,128)S(1)}, f32[8,512]{1,0:T(8,128)S(1)}, u32[]{:S(2)}, u32[]{:S(2)}) collective-permute-start(f32[8,512]{1,0:T(8,128)S(1)} %get-tuple-element.35), channel_id=1, source_target_pairs={{0,7},{1,4},{2,5},{3,6},{4,3},{5,0},{6,1},{7,2},{8,15},{9,12},{10,... | collective-permute-start | bytes 49160 | tf_op jit(solution)/shard_map/ppermute | solution.py:272
  13.2 0.6 %collective-permute-done.6.got_ref = f32[16,512]{1,0:T(8,128)S(1)} collective-permute-done((f32[16,512]{1,0:T(8,128)S(1)}, f32[16,512]{1,0:T(8,128)S(1)}, u32[]{:S(2)}, u32[]{:S(2)}) %collective-permute-start.6) | collective-permute-done | bytes 32800 | tf_op jit(solution)/shard_map/ppermute | solution.py:272
  13.8 1.2 %collective-permute-start.8 = (f32[8,512]{1,0:T(8,128)S(1)}, f32[8,512]{1,0:T(8,128)S(1)}, u32[]{:S(2)}, u32[]{:S(2)}) collective-permute-start(f32[8,512]{1,0:T(8,128)S(1)} %slice.4), channel_id=1, source_target_pairs={{0,4},{1,5},{2,6},{3,7},{4,0},{5,1},{6,2},{7,3},{8,12},{9,13},{10,... | collective-permute-start | bytes 49160 | tf_op jit(solution)/shard_map/ppermute | solution.py:272
  15.1 0.0 collective-permute-done.7.far_ref
  15.1 0.8 %collective-permute-done.8.too_ref = f32[8,512]{1,0:T(8,128)S(1)} collective-permute-done((f32[8,512]{1,0:T(8,128)S(1)}, f32[8,512]{1,0:T(8,128)S(1)}, u32[]{:S(2)}, u32[]{:S(2)}) %collective-permute-start.8) | collective-permute-done | bytes 16416 | tf_op jit(solution)/shard_map/ppermute | solution.py:272
  15.9 0.8 %expand.1 = f32[64,512]{1,0:T(8,128)} custom-call(f32[8,512]{1,0:T(8,128)S(1)} %get-tuple-element.33.keep_ref, f32[16,512]{1,0:T(8,128)S(1)} %collective-permute-done.6.got_ref, f32[8,512]{1,0:T(8,128)S(1)} %collective-permute-done.7.far_ref, f32[8,512]{1,0:T(8,128)S(1)} %collective-permute-done.8.too_ref, s32[64,128]{1,0:T(8,128)S(1)} %get-tuple-element.36.key_ref, ...), custom_call_target="tpu_custom_call" | custom-call | flops 1048576 | bytes 262144 | tf_op jit(solution)/shard_map/expand/pallas_call | solution.py:254
  (2 shorter events, 0.0 us)
Async XLA Ops:
  0.0 1.9 %collective-permute-start = (bf16[32,1024]{1,0:T(8,128)(2,1)}, bf16[32,1024]{1,0:T(8,128)(2,1)S(1)}, u32[]{:S(2)}, u32[]{:S(2)}) collective-permute-start(bf16[32,1024]{1,0:T(8,128)(2,1)} %amplitudes_ref.1), channel_id=1, source_target_pairs={{0,4},{1,5},{2,6},{3,7},{4,0},{5,1},{6,2},{7,3},{8,12},{9,13},{10,... | collective-permute-start | bytes 196616 | tf_op jit(solution)/shard_map/ppermute | solution.py:272
  1.9 7.1 %collective-permute-start.5 = (bf16[1024,512]{1,0:T(8,128)(2,1)}, bf16[1024,512]{1,0:T(8,128)(2,1)S(1)}, u32[]{:S(2)}, u32[]{:S(2)}) collective-permute-start(bf16[1024,512]{1,0:T(8,128)(2,1)} %integrals_ref), channel_id=1, source_target_pairs={{0,4},{1,5},{2,6},{3,7},{4,0},{5,1},{6,2},{7,3},{8,12},{9,13},{10,... | collective-permute-start | bytes 3145736 | tf_op jit(solution)/shard_map/ppermute | solution.py:272
  2.2 5.6 %copy-start.1 = (s32[512]{0:T(512)S(1)}, s32[512]{0:T(512)}, u32[]{:S(2)}) copy-start(s32[512]{0:T(512)} %param.9) | copy-start | bytes 6148
  2.2 5.5 %collective-permute-start.1 = (bf16[8,1024]{1,0:T(8,128)(2,1)S(1)}, bf16[8,1024]{1,0:T(8,128)(2,1)S(1)}, u32[]{:S(2)}, u32[]{:S(2)}) collective-permute-start(bf16[8,1024]{1,0:T(8,128)(2,1)S(1)} %add_convert_fusion.b0), channel_id=1, source_target_pairs={{0,12},{1,13},{2,14},{3,15},{4,16},{5,17},{6,18},{7,19},{8,4},{9,5... | collective-permute-start | bytes 49160 | tf_op jit(solution)/shard_map/ppermute | solution.py:272
  4.8 4.3 %collective-permute-start.3 = (bf16[8,1024]{1,0:T(8,128)(2,1)S(1)}, bf16[8,1024]{1,0:T(8,128)(2,1)S(1)}, u32[]{:S(2)}, u32[]{:S(2)}) collective-permute-start(bf16[8,1024]{1,0:T(8,128)(2,1)S(1)} %add_convert_fusion.b0), channel_id=1, source_target_pairs={{0,28},{1,29},{2,30},{3,31},{4,24},{5,25},{6,26},{7,27},{8,20},{9,... | collective-permute-start | bytes 49160 | tf_op jit(solution)/shard_map/ppermute | solution.py:272
  7.6 1.4 %copy-start = (s32[1024]{0:T(1024)S(1)}, s32[1024]{0:T(1024)}, u32[]{:S(2)}) copy-start(s32[1024]{0:T(1024)} %param.8) | copy-start | bytes 12292
  7.6 1.4 %collective-permute-start.2 = (bf16[8,1024]{1,0:T(8,128)(2,1)S(1)}, bf16[8,1024]{1,0:T(8,128)(2,1)S(1)}, u32[]{:S(2)}, u32[]{:S(2)}) collective-permute-start(bf16[8,1024]{1,0:T(8,128)(2,1)S(1)} %collective-permute-done.1.b1), channel_id=1, source_target_pairs={{0,4},{1,5},{2,6},{3,7},{4,0},{5,1},{6,2},{7,3},{8,12},{9,13},{10,... | collective-permute-start | bytes 49160 | tf_op jit(solution)/shard_map/ppermute | solution.py:272
  7.7 1.3 %collective-permute-start.4 = (s32[512]{0:T(512)S(1)}, s32[512]{0:T(512)S(1)}, u32[]{:S(2)}, u32[]{:S(2)}) collective-permute-start(s32[512]{0:T(512)S(1)} %copy-done.1), channel_id=1, source_target_pairs={{0,4},{1,5},{2,6},{3,7},{4,0},{5,1},{6,2},{7,3},{8,12},{9,13},{10,... | collective-permute-start | bytes 6152 | tf_op jit(solution)/shard_map/ppermute | solution.py:272
  9.5 4.3 %collective-permute-start.6 = (f32[16,512]{1,0:T(8,128)S(1)}, f32[16,512]{1,0:T(8,128)S(1)}, u32[]{:S(2)}, u32[]{:S(2)}) collective-permute-start(f32[16,512]{1,0:T(8,128)S(1)} %get-tuple-element.34), channel_id=1, source_target_pairs={{0,5},{1,6},{2,7},{3,4},{4,2},{5,3},{6,0},{7,1},{8,13},{9,14},{10,... | collective-permute-start | bytes 98312 | tf_op jit(solution)/shard_map/ppermute | solution.py:272
  11.1 4.0 %collective-permute-start.7 = (f32[8,512]{1,0:T(8,128)S(1)}, f32[8,512]{1,0:T(8,128)S(1)}, u32[]{:S(2)}, u32[]{:S(2)}) collective-permute-start(f32[8,512]{1,0:T(8,128)S(1)} %get-tuple-element.35), channel_id=1, source_target_pairs={{0,7},{1,4},{2,5},{3,6},{4,3},{5,0},{6,1},{7,2},{8,15},{9,12},{10,... | collective-permute-start | bytes 49160 | tf_op jit(solution)/shard_map/ppermute | solution.py:272
  13.8 2.1 %collective-permute-start.8 = (f32[8,512]{1,0:T(8,128)S(1)}, f32[8,512]{1,0:T(8,128)S(1)}, u32[]{:S(2)}, u32[]{:S(2)}) collective-permute-start(f32[8,512]{1,0:T(8,128)S(1)} %slice.4), channel_id=1, source_target_pairs={{0,4},{1,5},{2,6},{3,7},{4,0},{5,1},{6,2},{7,3},{8,12},{9,13},{10,... | collective-permute-start | bytes 49160 | tf_op jit(solution)/shard_map/ppermute | solution.py:272

commit v5 on v4

--- a/solution.py
+++ b/solution.py
@@ -80,96 +80,124 @@
     return out
 
 
-def labels_and_ranks(occupied, place, block):
+def keys(occupied, place, block):
+    slots = block // IRREPS
     labels = jnp.zeros((1, block), jnp.int32)
     for b in range(occupied.shape[1] // block):
         labels = jnp.where(place == b, occupied[:, b * block : (b + 1) * block], labels)
+    irrep = lax.broadcasted_iota(jnp.int32, (IRREPS, block), 0)
+    same = jnp.where(labels == irrep, 1.0, 0.0)
     lane = lax.broadcasted_iota(jnp.int32, (block, block), 1)
     sublane = lax.broadcasted_iota(jnp.int32, (block, block), 0)
-    column = jnp.sum(jnp.where(lane == sublane, labels, 0), axis=1, keepdims=True)
-    rank = jnp.sum(jnp.where((column == labels) & (sublane < lane), 1, 0), axis=0, keepdims=True)
-    return column, rank
-
-
-def pack_kernel(block, slots, occupied_ref, contracted_ref, amplitudes_ref, part_ref, gate_ref, pick_ref, occupied, contracted, own, sems):
+    before = jnp.where(sublane < lane, 1.0, 0.0).astype(jnp.bfloat16)
+    counts = jnp.dot(same.astype(jnp.bfloat16), before, preferred_element_type=jnp.float32)
+    rank = jnp.sum(same * counts, axis=0, keepdims=True)
+    return labels * slots + rank.astype(jnp.int32)
+
+
+def pack_kernel(block, occupied_ref, contracted_ref, amplitudes_ref, order_ref, contracted_out, own_out, occupied, sems):
     copies = [
         pltpu.make_async_copy(src, dst, sems.at[n])
-        for n, (src, dst) in enumerate(((occupied_ref, occupied), (contracted_ref, contracted), (amplitudes_ref, own)))
+        for n, (src, dst) in enumerate(
+            ((occupied_ref, occupied), (contracted_ref, contracted_out), (amplitudes_ref, own_out))
+        )
     ]
     for copy in copies:
         copy.start()
-    row = lax.axis_index("row")
-    member = row % CORES
-    rows = own.shape[0]
     copies[0].wait()
-    column, rank = labels_and_ranks(occupied, row // CORES, block)
-    slot = lax.broadcasted_iota(jnp.int32, (slots, rows), 0)
-    ours = jnp.where(member == 0, rank[:, :rows], rank[:, rows:])
-    theirs = jnp.where(member == 0, rank[:, rows:], rank[:, :rows])
-    our_labels = jnp.where(member == 0, column[:rows], column[rows:])
-    their_labels = jnp.where(member == 0, column[rows:], column[:rows])
-    pick_ref[...] = jnp.where(slot == theirs, 1.0, 0.0).astype(jnp.bfloat16)
-    copies[1].wait()
-    gate_ref[...] = jnp.where(their_labels == contracted[...], 1.0, 0.0).astype(jnp.bfloat16)
-    copies[2].wait()
-    kept = jnp.where(our_labels == contracted[...], own[...].astype(jnp.float32), 0.0).astype(jnp.bfloat16)
-    pick = jnp.where(slot == ours, 1.0, 0.0).astype(jnp.bfloat16)
-    part_ref[...] = jnp.dot(pick, kept, preferred_element_type=jnp.float32)
-
-
-def pack(occupied_irreps, contracted_irreps, amplitudes, block, slots):
+    key = keys(occupied[...], lax.axis_index("row") // CORES, block)
+    sublane = lax.broadcasted_iota(jnp.int32, (block, block), 0)
+    order_ref[...] = jnp.where(key == sublane, 1.0, 0.0).astype(jnp.bfloat16)
+    for copy in copies[1:]:
+        copy.wait()
+
+
+def pack(occupied_irreps, contracted_irreps, amplitudes, block):
     rows, depth = amplitudes.shape
     pairs = occupied_irreps.shape[0]
     return pl.pallas_call(
-        functools.partial(pack_kernel, block, slots),
+        functools.partial(pack_kernel, block),
         out_shape=(
-            pltpu.VMEM((slots, depth), jnp.float32),
+            pltpu.VMEM((block, block), jnp.bfloat16),
+            pltpu.VMEM((1, depth), jnp.int32),
             pltpu.VMEM((rows, depth), jnp.bfloat16),
-            pltpu.VMEM((slots, rows), jnp.bfloat16),
         ),
         in_specs=[pl.BlockSpec(memory_space=pltpu.HBM)] * 3,
         out_specs=[pl.BlockSpec(memory_space=pltpu.VMEM)] * 3,
-        scratch_shapes=[
-            pltpu.VMEM((1, pairs), jnp.int32),
-            pltpu.VMEM((1, depth), jnp.int32),
-            pltpu.VMEM((rows, depth), jnp.bfloat16),
-            pltpu.SemaphoreType.DMA((3,)),
-        ],
+        scratch_shapes=[pltpu.VMEM((1, pairs), jnp.int32), pltpu.SemaphoreType.DMA((3,))],
         compiler_params=pltpu.CompilerParams(vmem_limit_bytes=8 << 20),
         cost_estimate=pl.CostEstimate(flops=1 << 20, bytes_accessed=1 << 18, transcendentals=0),
         name="pack",
     )(in_hbm(occupied_irreps.reshape(1, pairs)), in_hbm(contracted_irreps.reshape(1, depth)), in_hbm(amplitudes))
 
 
-def stage_kernel(integrals_ref, occupied_ref, staged_ref, key_ref, occupied, sems):
+def fold_kernel(slots, order_ref, contracted_ref, own_ref, raw_ref, packed_ref):
+    first = lax.axis_index("row") % CORES == 0
+    own, raw = own_ref[...], raw_ref[...]
+    rows = jnp.concatenate([jnp.where(first, own, raw), jnp.where(first, raw, own)], axis=0)
+    ordered = jnp.dot(order_ref[...], rows, preferred_element_type=jnp.float32)
+    contracted = contracted_ref[...]
+    packed = jnp.zeros((slots, contracted.shape[1]), jnp.float32)
+    for g in range(IRREPS):
+        packed = jnp.where(contracted == g, ordered[g * slots : (g + 1) * slots], packed)
+    packed_ref[...] = packed.astype(jnp.bfloat16)
+
+
+def fold(order, contracted, own, raw, slots):
+    args = [order, contracted, own, raw]
+    return pl.pallas_call(
+        functools.partial(fold_kernel, slots),
+        out_shape=pltpu.VMEM((slots, own.shape[1]), jnp.bfloat16),
+        in_specs=[pl.BlockSpec(memory_space=pltpu.VMEM)] * len(args),
+        out_specs=pl.BlockSpec(memory_space=pltpu.VMEM),
+        compiler_params=pltpu.CompilerParams(vmem_limit_bytes=8 << 20),
+        cost_estimate=pl.CostEstimate(flops=1 << 23, bytes_accessed=1 << 17, transcendentals=0),
+        name="fold",
+    )(*[in_vmem(x) for x in args])
+
+
+def stage_kernel(integrals_ref, occupied_ref, outputs_ref, staged_ref, key_ref, outputs_out, occupied, sems):
+    pieces = sems.shape[0] - 2
+    size = integrals_ref.shape[0] // pieces
     copies = [
-        pltpu.make_async_copy(occupied_ref, occupied, sems.at[0]),
-        pltpu.make_async_copy(integrals_ref, staged_ref, sems.at[1]),
+        pltpu.make_async_copy(src, dst, sems.at[n])
+        for n, (src, dst) in enumerate(
+            ((occupied_ref, occupied), (outputs_ref, outputs_out))
+        )
     ]
+    for n in range(pieces):
+        rows = pl.ds(n * size, size)
+        copies.append(pltpu.make_async_copy(integrals_ref.at[rows], staged_ref.at[rows], sems.at[2 + n]))
     for copy in copies:
         copy.start()
     copies[0].wait()
     block = key_ref.shape[0]
-    column, rank = labels_and_ranks(occupied[...], lax.axis_index("col"), block)
+    key = keys(occupied[...], lax.axis_index("col"), block)
     lane = lax.broadcasted_iota(jnp.int32, (block, block), 1)
     sublane = lax.broadcasted_iota(jnp.int32, (block, block), 0)
-    slot = jnp.sum(jnp.where(lane == sublane, rank, 0), axis=1, keepdims=True)
-    key_ref[...] = jnp.broadcast_to(slot * IRREPS + column, key_ref.shape)
-    copies[1].wait()
-
-
-def stage(integrals, occupied_irreps, block):
+    column = jnp.sum(jnp.where(lane == sublane, key, 0), axis=1, keepdims=True)
+    key_ref[...] = jnp.broadcast_to(column, key_ref.shape)
+    for copy in copies[1:]:
+        copy.wait()
+
+
+def stage(integrals, occupied_irreps, outputs, block, pieces=4):
+    depth, width = integrals.shape
     pairs = occupied_irreps.shape[0]
     return pl.pallas_call(
         stage_kernel,
-        out_shape=(pltpu.VMEM(integrals.shape, integrals.dtype), pltpu.VMEM((block, 128), jnp.int32)),
-        in_specs=[pl.BlockSpec(memory_space=pltpu.HBM)] * 2,
-        out_specs=[pl.BlockSpec(memory_space=pltpu.VMEM)] * 2,
-        scratch_shapes=[pltpu.VMEM((1, pairs), jnp.int32), pltpu.SemaphoreType.DMA((2,))],
+        out_shape=(
+            pltpu.VMEM(integrals.shape, integrals.dtype),
+            pltpu.VMEM((block, 128), jnp.int32),
+            pltpu.VMEM((1, width), jnp.int32),
+        ),
+        in_specs=[pl.BlockSpec(memory_space=pltpu.HBM)] * 3,
+        out_specs=[pl.BlockSpec(memory_space=pltpu.VMEM)] * 3,
+        scratch_shapes=[pltpu.VMEM((1, pairs), jnp.int32), pltpu.SemaphoreType.DMA((2 + pieces,))],
         compiler_params=pltpu.CompilerParams(vmem_limit_bytes=8 << 20),
         cost_estimate=pl.CostEstimate(flops=0, bytes_accessed=4 * integrals.size, transcendentals=0),
         name="stage",
-    )(in_hbm(integrals), in_hbm(occupied_irreps.reshape(1, pairs)))
+    )(*[in_hbm(x) for x in (integrals, occupied_irreps.reshape(1, pairs), outputs.reshape(1, width))])
 
 
 def sums_kernel(slots, blocks_refs, contracted_ref, outputs_ref, other_outputs_ref, integrals_ref, other_ref, send_ref, far_ref, keep_ref):
@@ -238,7 +266,7 @@
         key = key_ref[rows, :1]
         out = jnp.zeros((size, width), jnp.float32)
         for s in range(slots):
-            out = jnp.where(key == outputs + s * IRREPS, total[s : s + 1], out)
+            out = jnp.where(key == outputs * slots + s, total[s : s + 1], out)
         staged[rows] = out
         copy = pltpu.make_async_copy(staged.at[rows], out_ref.at[rows], sems.at[n])
         copy.start()
@@ -279,25 +307,24 @@
     sibling = lambda p, m, c: (p, 1 - m, c)
 
     raw = move(amplitudes, sibling)
-    part, gate, pick = pack(occupied_irreps, contracted_irreps, amplitudes, block, slots)
-    raw, part, late_integrals, late_outputs = lax.optimization_barrier((raw, part, integrals, output_irreps))
+    order, contracted, ours = pack(occupied_irreps, contracted_irreps, amplitudes, block)
+    raw, order, late_integrals, late_outputs = lax.optimization_barrier((raw, order, integrals, output_irreps))
     other = move(late_integrals, sibling)
     other_outputs = move(late_outputs, sibling)
-    packed = (part + jnp.dot(pick, raw * gate, preferred_element_type=jnp.float32)).astype(jnp.bfloat16)
+    packed = fold(order, contracted, ours, raw, slots)
 
     packed, late_integrals = lax.optimization_barrier((packed, integrals))
     side = move(packed, lambda p, m, c: (p ^ (1 + m), 1 - m, c))
     far = move(packed, lambda p, m, c: (p ^ 3, 1 - m, c))
-    staged, key = stage(late_integrals, occupied_irreps, block)
-    side, staged = lax.optimization_barrier((side, staged))
+    staged, key, outputs = stage(late_integrals, occupied_irreps, output_irreps, block)
     side_too = move(side, sibling)
     send, send_far, keep = sums(
-        (packed, side, side_too, far), contracted_irreps, output_irreps, other_outputs, staged, other, slots
+        (packed, side, side_too, far), contracted, outputs, other_outputs, staged, other, slots
     )
     got = move(send, lambda p, m, c: (p, 1 - m, (c + 1 + m) % COLS))
     got_far = move(send_far, lambda p, m, c: (p, 1 - m, (c + 3) % COLS))
     got_too = move(got[slots:], sibling)
-    return expand(keep, got, got_far, got_too, key, output_irreps)
+    return expand(keep, got, got_far, got_too, key, outputs)
 
 
 def solution(mesh):

time: 16.9 us -> 16.6 us (0.982)
  waiting for transfers between devices: 2.26 us -> 2.59 us
  Pallas kernels: 3.94 us -> 3.69 us
  starting transfers between devices: 10.3 us -> 10.1 us
    ppermute x9, waiting for transfers between devices: 2.26 us -> 2.59 us  [move(): return lax.ppermute(x, ('row', 'col'), pairs)]
    pallas_call x1 -> x2, Pallas kernels: 1.44 us -> 1.16 us  [the longest x1 0.99 us: pack(): pl.pallas_call(functools.partial(pack_kernel, block), out_shape=(pltpu.VM...]
  transfers between devices with their start and end apart: 9 -> 9, of which waited for: 3 -> 5; matrix products, arithmetic and copies ran while one was open for 1% -> 0% of each run, Pallas kernels for 16% -> 15%
where the time goes in v5:
time: 16.6 us; the launch traced here: 16.5 us
  starting transfers between devices  10.1 us (61%)
  Pallas kernels  3.69 us (22%)
  waiting for transfers between devices  2.59 us (16%)
    ppermute x9, starting transfers between devices, move(): return lax.ppermute(x, ('row', 'col'), pairs)  10.1 us
    ppermute x9, waiting for transfers between devices, move(): return lax.ppermute(x, ('row', 'col'), pairs)  2.59 us
    pallas_call x1, Pallas kernels, stage(): pl.pallas_call(stage_kernel, out_shape=(pltpu.VMEM(integrals.shape, integ...  1.27 us
    pallas_call x1, Pallas kernels, pack(): pl.pallas_call(functools.partial(pack_kernel, block), out_shape=(pltpu.VM...  0.99 us
    pallas_call x1, Pallas kernels, expand(): pl.pallas_call(expand_kernel, out_shape=pltpu.HBM((block, width), jnp.flo...  0.78 us
    pallas_call x1, Pallas kernels, sums(): pl.pallas_call(kernel, out_shape=(pltpu.VMEM((2 * slots, width), jnp.floa...  0.47 us
  transfers between devices with their start and end apart: 9, of which 5 were waited for; matrix products, arithmetic and copies ran while one was open for 0% of the time, Pallas kernels for 15%

profile of v5, /device:TPU:0, one launch (start us, length us, event | category | flops | bytes accessed | tf_op | source)
XLA Modules:
  0.0 16.5 jit_solution(8344941713716071925)
XLA Ops:
  0.0 0.5 %collective-permute-start = (bf16[32,1024]{1,0:T(8,128)(2,1)}, bf16[32,1024]{1,0:T(8,128)(2,1)S(1)}, u32[]{:S(2)}, u32[]{:S(2)}) collective-permute-start(bf16[32,1024]{1,0:T(8,128)(2,1)} %amplitudes_ref.1), channel_id=1, source_target_pairs={{0,4},{1,5},{2,6},{3,7},{4,0},{5,1},{6,2},{7,3},{8,12},{9,13},{10,... | collective-permute-start | bytes 196616 | tf_op jit(solution)/shard_map/ppermute | solution.py:300
  0.5 1.0 %pack.1 = (bf16[64,64]{1,0:T(8,128)(2,1)S(1)}, s32[1,1024]{1,0:T(1,128)S(1)}, bf16[32,1024]{1,0:T(8,128)(2,1)S(1)}) custom-call(s32[1,256]{1,0:T(1,128)} %bitcast.5, s32[1,1024]{1,0:T(1,128)} %bitcast.7, bf16[32,1024]{1,0:T(8,128)(2,1)} %amplitudes_ref.1), custom_call_target="tpu_custom_call" | custom-call | flops 1048576 | bytes 262144 | tf_op jit(solution)/shard_map/pack/pallas_call | solution.py:118
  1.5 0.1 collective-permute-done.raw_ref
  1.6 0.4 %collective-permute-start.5 = (bf16[1024,512]{1,0:T(8,128)(2,1)}, bf16[1024,512]{1,0:T(8,128)(2,1)S(1)}, u32[]{:S(2)}, u32[]{:S(2)}) collective-permute-start(bf16[1024,512]{1,0:T(8,128)(2,1)} %integrals_ref), channel_id=1, source_target_pairs={{0,4},{1,5},{2,6},{3,7},{4,0},{5,1},{6,2},{7,3},{8,12},{9,13},{10,... | collective-permute-start | bytes 3145736 | tf_op jit(solution)/shard_map/ppermute | solution.py:300
  1.9 0.0 copy-start
  1.9 0.2 %fold.1.b0 = bf16[8,1024]{1,0:T(8,128)(2,1)S(1)} custom-call(bf16[64,64]{1,0:T(8,128)(2,1)S(1)} %get-tuple-element.21.order_ref, s32[1,1024]{1,0:T(1,128)S(1)} %get-tuple-element.22.contracted_ref.refs_0_, bf16[32,1024]{1,0:T(8,128)(2,1)S(1)} %get-tuple-element.23.own_ref, bf16[32,1024]{1,0:T(8,128)(2,1)S(1)} %collective-permute-done.raw_ref), custom_call_target="tpu_custom_call" | custom-call | flops 8388608 | bytes 131072 | tf_op jit(solution)/shard_map/fold/pallas_call | solution.py:148
  2.1 2.7 %collective-permute-start.1 = (bf16[8,1024]{1,0:T(8,128)(2,1)S(1)}, bf16[8,1024]{1,0:T(8,128)(2,1)S(1)}, u32[]{:S(2)}, u32[]{:S(2)}) collective-permute-start(bf16[8,1024]{1,0:T(8,128)(2,1)S(1)} %fold.1.b0), channel_id=1, source_target_pairs={{0,12},{1,13},{2,14},{3,15},{4,16},{5,17},{6,18},{7,19},{8,4},{9,5... | collective-permute-start | bytes 49160 | tf_op jit(solution)/shard_map/ppermute | solution.py:300
  4.8 1.2 %collective-permute-start.3 = (bf16[8,1024]{1,0:T(8,128)(2,1)S(1)}, bf16[8,1024]{1,0:T(8,128)(2,1)S(1)}, u32[]{:S(2)}, u32[]{:S(2)}) collective-permute-start(bf16[8,1024]{1,0:T(8,128)(2,1)S(1)} %fold.1.b0), channel_id=1, source_target_pairs={{0,28},{1,29},{2,30},{3,31},{4,24},{5,25},{6,26},{7,27},{8,20},{9,... | collective-permute-start | bytes 49160 | tf_op jit(solution)/shard_map/ppermute | solution.py:300
  6.0 0.2 %collective-permute-done.1.b1 = bf16[8,1024]{1,0:T(8,128)(2,1)S(1)} collective-permute-done((bf16[8,1024]{1,0:T(8,128)(2,1)S(1)}, bf16[8,1024]{1,0:T(8,128)(2,1)S(1)}, u32[]{:S(2)}, u32[]{:S(2)}) %collective-permute-start.1) | collective-permute-done | bytes 16416 | tf_op jit(solution)/shard_map/ppermute | solution.py:300
  6.2 0.2 collective-permute-start.2
  6.4 0.0 copy-done
  6.4 0.4 %collective-permute-start.4 = (s32[512]{0:T(512)S(1)}, s32[512]{0:T(512)S(1)}, u32[]{:S(2)}, u32[]{:S(2)}) collective-permute-start(s32[512]{0:T(512)S(1)} %copy-done), channel_id=1, source_target_pairs={{0,4},{1,5},{2,6},{3,7},{4,0},{5,1},{6,2},{7,3},{8,12},{9,13},{10,... | collective-permute-start | bytes 6152 | tf_op jit(solution)/shard_map/ppermute | solution.py:300
  6.7 1.3 %stage.1 = (bf16[1024,512]{1,0:T(8,128)(2,1)S(1)}, s32[64,128]{1,0:T(8,128)S(1)}, s32[1,512]{1,0:T(1,128)S(1)}) custom-call(bf16[1024,512]{1,0:T(8,128)(2,1)} %integrals_ref, s32[1,256]{1,0:T(1,128)} %bitcast.6, s32[1,512]{1,0:T(1,128)} %bitcast.8), custom_call_target="tpu_custom_call" | custom-call | bytes 2097152 | tf_op jit(solution)/shard_map/stage/pallas_call | solution.py:187
  8.0 0.0 collective-permute-done.4
  8.0 0.8 %collective-permute-done.3.b3 = bf16[8,1024]{1,0:T(8,128)(2,1)S(1)} collective-permute-done((bf16[8,1024]{1,0:T(8,128)(2,1)S(1)}, bf16[8,1024]{1,0:T(8,128)(2,1)S(1)}, u32[]{:S(2)}, u32[]{:S(2)}) %collective-permute-start.3) | collective-permute-done | bytes 16416 | tf_op jit(solution)/shard_map/ppermute | solution.py:300
  8.8 0.0 collective-permute-done.2.b2
  8.8 0.0 collective-permute-done.5.refs_4_
  8.8 0.5 %sums.1 = (f32[16,512]{1,0:T(8,128)S(1)}, f32[8,512]{1,0:T(8,128)S(1)}, f32[8,512]{1,0:T(8,128)S(1)}) custom-call(bf16[8,1024]{1,0:T(8,128)(2,1)S(1)} %fold.1.b0, bf16[8,1024]{1,0:T(8,128)(2,1)S(1)} %collective-permute-done.1.b1, bf16[8,1024]{1,0:T(8,128)(2,1)S(1)} %collective-permute-done.2.b2, bf16[8,1024]{1,0:T(8,128)(2,1)S(1)} %collective-permute-done.3.b3, ...), custom_call_target="tpu_custom_call" | custom-call | flops 268435456 | bytes 2097152 | tf_op jit(solution)/shard_map/sums/pallas_call | solution.py:241
  9.3 1.4 %collective-permute-start.6 = (f32[16,512]{1,0:T(8,128)S(1)}, f32[16,512]{1,0:T(8,128)S(1)}, u32[]{:S(2)}, u32[]{:S(2)}) collective-permute-start(f32[16,512]{1,0:T(8,128)S(1)} %get-tuple-element.32), channel_id=1, source_target_pairs={{0,5},{1,6},{2,7},{3,4},{4,2},{5,3},{6,0},{7,1},{8,13},{9,14},{10,... | collective-permute-start | bytes 98312 | tf_op jit(solution)/shard_map/ppermute | solution.py:300
  10.7 2.3 %collective-permute-start.7 = (f32[8,512]{1,0:T(8,128)S(1)}, f32[8,512]{1,0:T(8,128)S(1)}, u32[]{:S(2)}, u32[]{:S(2)}) collective-permute-start(f32[8,512]{1,0:T(8,128)S(1)} %get-tuple-element.33), channel_id=1, source_target_pairs={{0,7},{1,4},{2,5},{3,6},{4,3},{5,0},{6,1},{7,2},{8,15},{9,12},{10,... | collective-permute-start | bytes 49160 | tf_op jit(solution)/shard_map/ppermute | solution.py:300
  13.0 0.6 %collective-permute-done.6.got_ref = f32[16,512]{1,0:T(8,128)S(1)} collective-permute-done((f32[16,512]{1,0:T(8,128)S(1)}, f32[16,512]{1,0:T(8,128)S(1)}, u32[]{:S(2)}, u32[]{:S(2)}) %collective-permute-start.6) | collective-permute-done | bytes 32800 | tf_op jit(solution)/shard_map/ppermute | solution.py:300
  13.6 1.2 %collective-permute-start.8 = (f32[8,512]{1,0:T(8,128)S(1)}, f32[8,512]{1,0:T(8,128)S(1)}, u32[]{:S(2)}, u32[]{:S(2)}) collective-permute-start(f32[8,512]{1,0:T(8,128)S(1)} %slice.4), channel_id=1, source_target_pairs={{0,4},{1,5},{2,6},{3,7},{4,0},{5,1},{6,2},{7,3},{8,12},{9,13},{10,... | collective-permute-start | bytes 49160 | tf_op jit(solution)/shard_map/ppermute | solution.py:300
  14.8 0.0 collective-permute-done.7.far_ref
  14.8 0.8 %collective-permute-done.8.too_ref = f32[8,512]{1,0:T(8,128)S(1)} collective-permute-done((f32[8,512]{1,0:T(8,128)S(1)}, f32[8,512]{1,0:T(8,128)S(1)}, u32[]{:S(2)}, u32[]{:S(2)}) %collective-permute-start.8) | collective-permute-done | bytes 16416 | tf_op jit(solution)/shard_map/ppermute | solution.py:300
  15.7 0.8 %expand.1 = f32[64,512]{1,0:T(8,128)} custom-call(f32[8,512]{1,0:T(8,128)S(1)} %get-tuple-element.31.keep_ref, f32[16,512]{1,0:T(8,128)S(1)} %collective-permute-done.6.got_ref, f32[8,512]{1,0:T(8,128)S(1)} %collective-permute-done.7.far_ref, f32[8,512]{1,0:T(8,128)S(1)} %collective-permute-done.8.too_ref, s32[64,128]{1,0:T(8,128)S(1)} %get-tuple-element.34.key_ref, ...), custom_call_target="tpu_custom_call" | custom-call | flops 1048576 | bytes 262144 | tf_op jit(solution)/shard_map/expand/pallas_call | solution.py:282
  (1 shorter events, 0.0 us)
Async XLA Ops:
  0.0 1.6 %collective-permute-start = (bf16[32,1024]{1,0:T(8,128)(2,1)}, bf16[32,1024]{1,0:T(8,128)(2,1)S(1)}, u32[]{:S(2)}, u32[]{:S(2)}) collective-permute-start(bf16[32,1024]{1,0:T(8,128)(2,1)} %amplitudes_ref.1), channel_id=1, source_target_pairs={{0,4},{1,5},{2,6},{3,7},{4,0},{5,1},{6,2},{7,3},{8,12},{9,13},{10,... | collective-permute-start | bytes 196616 | tf_op jit(solution)/shard_map/ppermute | solution.py:300
  1.6 7.3 %collective-permute-start.5 = (bf16[1024,512]{1,0:T(8,128)(2,1)}, bf16[1024,512]{1,0:T(8,128)(2,1)S(1)}, u32[]{:S(2)}, u32[]{:S(2)}) collective-permute-start(bf16[1024,512]{1,0:T(8,128)(2,1)} %integrals_ref), channel_id=1, source_target_pairs={{0,4},{1,5},{2,6},{3,7},{4,0},{5,1},{6,2},{7,3},{8,12},{9,13},{10,... | collective-permute-start | bytes 3145736 | tf_op jit(solution)/shard_map/ppermute | solution.py:300
  1.9 4.4 %copy-start = (s32[512]{0:T(512)S(1)}, s32[512]{0:T(512)}, u32[]{:S(2)}) copy-start(s32[512]{0:T(512)} %param.9) | copy-start | bytes 6148
  2.1 4.1 %collective-permute-start.1 = (bf16[8,1024]{1,0:T(8,128)(2,1)S(1)}, bf16[8,1024]{1,0:T(8,128)(2,1)S(1)}, u32[]{:S(2)}, u32[]{:S(2)}) collective-permute-start(bf16[8,1024]{1,0:T(8,128)(2,1)S(1)} %fold.1.b0), channel_id=1, source_target_pairs={{0,12},{1,13},{2,14},{3,15},{4,16},{5,17},{6,18},{7,19},{8,4},{9,5... | collective-permute-start | bytes 49160 | tf_op jit(solution)/shard_map/ppermute | solution.py:300
  4.8 4.1 %collective-permute-start.3 = (bf16[8,1024]{1,0:T(8,128)(2,1)S(1)}, bf16[8,1024]{1,0:T(8,128)(2,1)S(1)}, u32[]{:S(2)}, u32[]{:S(2)}) collective-permute-start(bf16[8,1024]{1,0:T(8,128)(2,1)S(1)} %fold.1.b0), channel_id=1, source_target_pairs={{0,28},{1,29},{2,30},{3,31},{4,24},{5,25},{6,26},{7,27},{8,20},{9,... | collective-permute-start | bytes 49160 | tf_op jit(solution)/shard_map/ppermute | solution.py:300
  6.2 2.6 %collective-permute-start.2 = (bf16[8,1024]{1,0:T(8,128)(2,1)S(1)}, bf16[8,1024]{1,0:T(8,128)(2,1)S(1)}, u32[]{:S(2)}, u32[]{:S(2)}) collective-permute-start(bf16[8,1024]{1,0:T(8,128)(2,1)S(1)} %collective-permute-done.1.b1), channel_id=1, source_target_pairs={{0,4},{1,5},{2,6},{3,7},{4,0},{5,1},{6,2},{7,3},{8,12},{9,13},{10,... | collective-permute-start | bytes 49160 | tf_op jit(solution)/shard_map/ppermute | solution.py:300
  6.4 1.6 %collective-permute-start.4 = (s32[512]{0:T(512)S(1)}, s32[512]{0:T(512)S(1)}, u32[]{:S(2)}, u32[]{:S(2)}) collective-permute-start(s32[512]{0:T(512)S(1)} %copy-done), channel_id=1, source_target_pairs={{0,4},{1,5},{2,6},{3,7},{4,0},{5,1},{6,2},{7,3},{8,12},{9,13},{10,... | collective-permute-start | bytes 6152 | tf_op jit(solution)/shard_map/ppermute | solution.py:300
  9.3 4.3 %collective-permute-start.6 = (f32[16,512]{1,0:T(8,128)S(1)}, f32[16,512]{1,0:T(8,128)S(1)}, u32[]{:S(2)}, u32[]{:S(2)}) collective-permute-start(f32[16,512]{1,0:T(8,128)S(1)} %get-tuple-element.32), channel_id=1, source_target_pairs={{0,5},{1,6},{2,7},{3,4},{4,2},{5,3},{6,0},{7,1},{8,13},{9,14},{10,... | collective-permute-start | bytes 98312 | tf_op jit(solution)/shard_map/ppermute | solution.py:300
  10.7 4.1 %collective-permute-start.7 = (f32[8,512]{1,0:T(8,128)S(1)}, f32[8,512]{1,0:T(8,128)S(1)}, u32[]{:S(2)}, u32[]{:S(2)}) collective-permute-start(f32[8,512]{1,0:T(8,128)S(1)} %get-tuple-element.33), channel_id=1, source_target_pairs={{0,7},{1,4},{2,5},{3,6},{4,3},{5,0},{6,1},{7,2},{8,15},{9,12},{10,... | collective-permute-start | bytes 49160 | tf_op jit(solution)/shard_map/ppermute | solution.py:300
  13.6 2.1 %collective-permute-start.8 = (f32[8,512]{1,0:T(8,128)S(1)}, f32[8,512]{1,0:T(8,128)S(1)}, u32[]{:S(2)}, u32[]{:S(2)}) collective-permute-start(f32[8,512]{1,0:T(8,128)S(1)} %slice.4), channel_id=1, source_target_pairs={{0,4},{1,5},{2,6},{3,7},{4,0},{5,1},{6,2},{7,3},{8,12},{9,13},{10,... | collective-permute-start | bytes 49160 | tf_op jit(solution)/shard_map/ppermute | solution.py:300

commit v6 on v5

--- a/solution.py
+++ b/solution.py
@@ -9,6 +9,7 @@
 
 IRREPS = 8
 CORES, PLACES, COLS = 2, 4, 4
+LABEL_ROWS = 16
 
 
 def in_hbm(x):
@@ -95,11 +96,17 @@
     return labels * slots + rank.astype(jnp.int32)
 
 
-def pack_kernel(block, occupied_ref, contracted_ref, amplitudes_ref, order_ref, contracted_out, own_out, occupied, sems):
+def pack_kernel(block, occupied_ref, contracted_ref, outputs_ref, amplitudes_ref, integrals_ref, order_ref, key_ref, contracted_out, outputs_out, own_out, staged_ref, occupied, sems):
     copies = [
         pltpu.make_async_copy(src, dst, sems.at[n])
         for n, (src, dst) in enumerate(
-            ((occupied_ref, occupied), (contracted_ref, contracted_out), (amplitudes_ref, own_out))
+            (
+                (occupied_ref, occupied),
+                (contracted_ref, contracted_out),
+                (outputs_ref, outputs_out),
+                (amplitudes_ref, own_out),
+                (integrals_ref, staged_ref.at[pl.ds(0, integrals_ref.shape[0])]),
+            )
         )
     ]
     for copy in copies:
@@ -108,27 +115,45 @@
     key = keys(occupied[...], lax.axis_index("row") // CORES, block)
     sublane = lax.broadcasted_iota(jnp.int32, (block, block), 0)
     order_ref[...] = jnp.where(key == sublane, 1.0, 0.0).astype(jnp.bfloat16)
-    for copy in copies[1:]:
+    key = keys(occupied[...], lax.axis_index("col"), block)
+    lane = lax.broadcasted_iota(jnp.int32, (block, block), 1)
+    column = jnp.sum(jnp.where(lane == sublane, key, 0), axis=1, keepdims=True)
+    key_ref[...] = jnp.broadcast_to(column, key_ref.shape)
+    copies[2].wait()
+    labels = outputs_out[...].astype(jnp.float32).astype(jnp.bfloat16)
+    staged_ref[integrals_ref.shape[0] :] = jnp.broadcast_to(labels, (LABEL_ROWS, labels.shape[1]))
+    for copy in (copies[1], *copies[3:]):
         copy.wait()
 
 
-def pack(occupied_irreps, contracted_irreps, amplitudes, block):
+def pack(occupied_irreps, contracted_irreps, output_irreps, amplitudes, integrals, block):
     rows, depth = amplitudes.shape
+    width = output_irreps.shape[0]
     pairs = occupied_irreps.shape[0]
+    args = (
+        occupied_irreps.reshape(1, pairs),
+        contracted_irreps.reshape(1, depth),
+        output_irreps.reshape(1, width),
+        amplitudes,
+        integrals,
+    )
     return pl.pallas_call(
         functools.partial(pack_kernel, block),
         out_shape=(
             pltpu.VMEM((block, block), jnp.bfloat16),
+            pltpu.VMEM((block, 128), jnp.int32),
             pltpu.VMEM((1, depth), jnp.int32),
+            pltpu.VMEM((1, width), jnp.int32),
             pltpu.VMEM((rows, depth), jnp.bfloat16),
+            pltpu.VMEM((depth + LABEL_ROWS, width), jnp.bfloat16),
         ),
-        in_specs=[pl.BlockSpec(memory_space=pltpu.HBM)] * 3,
-        out_specs=[pl.BlockSpec(memory_space=pltpu.VMEM)] * 3,
-        scratch_shapes=[pltpu.VMEM((1, pairs), jnp.int32), pltpu.SemaphoreType.DMA((3,))],
+        in_specs=[pl.BlockSpec(memory_space=pltpu.HBM)] * len(args),
+        out_specs=[pl.BlockSpec(memory_space=pltpu.VMEM)] * 6,
+        scratch_shapes=[pltpu.VMEM((1, pairs), jnp.int32), pltpu.SemaphoreType.DMA((len(args),))],
         compiler_params=pltpu.CompilerParams(vmem_limit_bytes=8 << 20),
         cost_estimate=pl.CostEstimate(flops=1 << 20, bytes_accessed=1 << 18, transcendentals=0),
         name="pack",
-    )(in_hbm(occupied_irreps.reshape(1, pairs)), in_hbm(contracted_irreps.reshape(1, depth)), in_hbm(amplitudes))
+    )(*[in_hbm(x) for x in args])
 
 
 def fold_kernel(slots, order_ref, contracted_ref, own_ref, raw_ref, packed_ref):
@@ -156,88 +181,47 @@
     )(*[in_vmem(x) for x in args])
 
 
-def stage_kernel(integrals_ref, occupied_ref, outputs_ref, staged_ref, key_ref, outputs_out, occupied, sems):
-    pieces = sems.shape[0] - 2
-    size = integrals_ref.shape[0] // pieces
-    copies = [
-        pltpu.make_async_copy(src, dst, sems.at[n])
-        for n, (src, dst) in enumerate(
-            ((occupied_ref, occupied), (outputs_ref, outputs_out))
-        )
-    ]
-    for n in range(pieces):
-        rows = pl.ds(n * size, size)
-        copies.append(pltpu.make_async_copy(integrals_ref.at[rows], staged_ref.at[rows], sems.at[2 + n]))
-    for copy in copies:
-        copy.start()
-    copies[0].wait()
-    block = key_ref.shape[0]
-    key = keys(occupied[...], lax.axis_index("col"), block)
-    lane = lax.broadcasted_iota(jnp.int32, (block, block), 1)
-    sublane = lax.broadcasted_iota(jnp.int32, (block, block), 0)
-    column = jnp.sum(jnp.where(lane == sublane, key, 0), axis=1, keepdims=True)
-    key_ref[...] = jnp.broadcast_to(column, key_ref.shape)
-    for copy in copies[1:]:
-        copy.wait()
-
-
-def stage(integrals, occupied_irreps, outputs, block, pieces=4):
-    depth, width = integrals.shape
-    pairs = occupied_irreps.shape[0]
-    return pl.pallas_call(
-        stage_kernel,
-        out_shape=(
-            pltpu.VMEM(integrals.shape, integrals.dtype),
-            pltpu.VMEM((block, 128), jnp.int32),
-            pltpu.VMEM((1, width), jnp.int32),
-        ),
-        in_specs=[pl.BlockSpec(memory_space=pltpu.HBM)] * 3,
-        out_specs=[pl.BlockSpec(memory_space=pltpu.VMEM)] * 3,
-        scratch_shapes=[pltpu.VMEM((1, pairs), jnp.int32), pltpu.SemaphoreType.DMA((2 + pieces,))],
-        compiler_params=pltpu.CompilerParams(vmem_limit_bytes=8 << 20),
-        cost_estimate=pl.CostEstimate(flops=0, bytes_accessed=4 * integrals.size, transcendentals=0),
-        name="stage",
-    )(*[in_hbm(x) for x in (integrals, occupied_irreps.reshape(1, pairs), outputs.reshape(1, width))])
-
-
-def sums_kernel(slots, blocks_refs, contracted_ref, outputs_ref, other_outputs_ref, integrals_ref, other_ref, send_ref, far_ref, keep_ref):
+def sums_kernel(slots, blocks_refs, contracted_ref, staged_ref, other_ref, send_ref, far_ref, keep_ref):
     row, col = lax.axis_index("row"), lax.axis_index("col")
     place, member = row // CORES, row % CORES
     contracted = contracted_ref[...]
     blocks = [ref[...].astype(jnp.float32) for ref in blocks_refs]
 
     def block(t):
-        offset = ((col + t) % COLS) ^ place
-        turned = jnp.where((offset == 1) | (offset == 2), offset ^ ((1 - member) * 3), offset)
+        back = (place - col - t) % PLACES
+        turned = jnp.where((back == 1) | (back == 2), 1 + (back + member) % 2, back)
         chosen = blocks[0]
         for n in range(1, PLACES):
             chosen = jnp.where(turned == n, blocks[n], chosen)
         return chosen
 
-    def product(rows, weights, outputs):
+    depth = contracted.shape[1]
+
+    def product(rows, ref):
+        outputs = ref[depth : depth + 1].astype(jnp.float32)
         spread = jnp.concatenate([jnp.where(contracted == g, rows, 0.0) for g in range(IRREPS)], axis=0)
-        each = jnp.dot(spread.astype(jnp.bfloat16), weights, preferred_element_type=jnp.float32)
+        each = jnp.dot(spread.astype(jnp.bfloat16), ref[:depth], preferred_element_type=jnp.float32)
         total = jnp.zeros((2 * slots, each.shape[1]), jnp.float32)
         for g in range(IRREPS):
             total = jnp.where(outputs == g, each[g * 2 * slots : (g + 1) * 2 * slots], total)
         return total
 
     sent = block(1 + member)
-    theirs = product(jnp.concatenate([sent, block(3)], 0), other_ref[...], other_outputs_ref[...])
+    theirs = product(jnp.concatenate([sent, block(3)], 0), other_ref)
     send_ref[:slots] = theirs[:slots]
     far_ref[...] = theirs[slots:]
-    ours = product(jnp.concatenate([sent, block(0)], 0), integrals_ref[...], outputs_ref[...])
+    ours = product(jnp.concatenate([sent, block(0)], 0), staged_ref)
     send_ref[slots:] = ours[:slots]
     keep_ref[...] = ours[slots:]
 
 
-def sums(blocks, contracted, outputs, other_outputs, integrals, other, slots):
-    depth, width = integrals.shape
+def sums(blocks, contracted, staged, other, slots):
+    width = staged.shape[1]
 
     def kernel(b0, b1, b2, b3, *refs):
         sums_kernel(slots, (b0, b1, b2, b3), *refs)
 
-    args = [*blocks, contracted.reshape(1, depth), outputs.reshape(1, width), other_outputs.reshape(1, width), integrals, other]
+    args = [*blocks, contracted, staged, other]
     return pl.pallas_call(
         kernel,
         out_shape=(
@@ -307,19 +291,18 @@
     sibling = lambda p, m, c: (p, 1 - m, c)
 
     raw = move(amplitudes, sibling)
-    order, contracted, ours = pack(occupied_irreps, contracted_irreps, amplitudes, block)
-    raw, order, late_integrals, late_outputs = lax.optimization_barrier((raw, order, integrals, output_irreps))
-    other = move(late_integrals, sibling)
-    other_outputs = move(late_outputs, sibling)
+    order, key, contracted, outputs, ours, staged = pack(
+        occupied_irreps, contracted_irreps, output_irreps, amplitudes, integrals, block
+    )
+    raw, order, staged = lax.optimization_barrier((raw, order, staged))
+    other = move(staged, sibling)
     packed = fold(order, contracted, ours, raw, slots)
 
-    packed, late_integrals = lax.optimization_barrier((packed, integrals))
-    side = move(packed, lambda p, m, c: (p ^ (1 + m), 1 - m, c))
-    far = move(packed, lambda p, m, c: (p ^ 3, 1 - m, c))
-    staged, key, outputs = stage(late_integrals, occupied_irreps, output_irreps, block)
+    side = move(packed, lambda p, m, c: ((p + 1 + m) % PLACES, 1 - m, c))
+    far = move(packed, lambda p, m, c: ((p + 3) % PLACES, 1 - m, c))
     side_too = move(side, sibling)
     send, send_far, keep = sums(
-        (packed, side, side_too, far), contracted, outputs, other_outputs, staged, other, slots
+        (packed, side, side_too, far), contracted, staged, other, slots
     )
     got = move(send, lambda p, m, c: (p, 1 - m, (c + 1 + m) % COLS))
     got_far = move(send_far, lambda p, m, c: (p, 1 - m, (c + 3) % COLS))

time: 16.6 us -> 16.3 us (0.982)
  starting transfers between devices: 10.1 us -> 11.2 us
  Pallas kernels: 3.69 us -> 2.77 us
  waiting for transfers between devices: 2.59 us -> 2.17 us
    pallas_call x1 -> x0, Pallas kernels: 1.27 us -> none  [stage(): pl.pallas_call(stage_kernel, out_shape=(pltpu.VMEM(integrals.shape, integ...]
    ppermute x9 -> x8, starting transfers between devices: 10.1 us -> 11.2 us  [move(): return lax.ppermute(x, ('row', 'col'), pairs)]
    ppermute x9 -> x8, waiting for transfers between devices: 2.59 us -> 2.17 us  [move(): return lax.ppermute(x, ('row', 'col'), pairs)]
    pallas_call x1, Pallas kernels: 0.99 us -> 1.35 us  [pack(): pl.pallas_call(functools.partial(pack_kernel, block), out_shape=(pltpu.VM...]
  transfers between devices with their start and end apart: 9 -> 8, of which waited for: 5 -> 4; matrix products, arithmetic and copies ran while one was open for 0% -> 0% of each run, Pallas kernels for 15% -> 9%
where the time goes in v6:
time: 16.3 us; the launch traced here: 16.2 us
  starting transfers between devices  11.2 us (69%)
  Pallas kernels  2.77 us (17%)
  waiting for transfers between devices  2.17 us (13%)
    ppermute x8, starting transfers between devices, move(): return lax.ppermute(x, ('row', 'col'), pairs)  11.2 us
    ppermute x8, waiting for transfers between devices, move(): return lax.ppermute(x, ('row', 'col'), pairs)  2.17 us
    pallas_call x1, Pallas kernels, pack(): pl.pallas_call(functools.partial(pack_kernel, block), out_shape=(pltpu.VM...  1.35 us
    pallas_call x1, Pallas kernels, expand(): pl.pallas_call(expand_kernel, out_shape=pltpu.HBM((block, width), jnp.flo...  0.78 us
    pallas_call x1, Pallas kernels, sums(): pl.pallas_call(kernel, out_shape=(pltpu.VMEM((2 * slots, width), jnp.floa...  0.46 us
  transfers between devices with their start and end apart: 8, of which 4 were waited for; matrix products, arithmetic and copies ran while one was open for 0% of the time, Pallas kernels for 9%

profile of v6, /device:TPU:0, one launch (start us, length us, event | category | flops | bytes accessed | tf_op | source)
XLA Modules:
  0.0 16.2 jit_solution(4851796788530089222)
XLA Ops:
  0.0 0.5 %collective-permute-start = (bf16[32,1024]{1,0:T(8,128)(2,1)}, bf16[32,1024]{1,0:T(8,128)(2,1)S(1)}, u32[]{:S(2)}, u32[]{:S(2)}) collective-permute-start(bf16[32,1024]{1,0:T(8,128)(2,1)} %amplitudes_ref.1), channel_id=1, source_target_pairs={{0,4},{1,5},{2,6},{3,7},{4,0},{5,1},{6,2},{7,3},{8,12},{9,13},{10,... | collective-permute-start | bytes 196616 | tf_op jit(solution)/shard_map/ppermute | solution.py:284
  0.5 1.4 %pack.1 = (bf16[64,64]{1,0:T(8,128)(2,1)S(1)}, s32[64,128]{1,0:T(8,128)S(1)}, s32[1,1024]{1,0:T(1,128)S(1)}, s32[1,512]{1,0:T(1,128)S(1)}, bf16[32,1024]{1,0:T(8,128)(2,1)S(1)}, /*index=5*/bf16[1040,512]{1,0:T(8,128)(2,1)S(1)}) custom-call(s32[1,256]{1,0:T(1,128)} %bitcast.5, s32[1,1024]{1,0:T(1,128)} %bitcast.3, s32[1,512]{1,0:T(1,128)} %bitcast.4, ...), custom_call_target="tpu_custom_call" | custom-call | flops 1048576 | bytes 262144 | tf_op jit(solution)/shard_map/pack/pallas_call | solution.py:140
  1.8 0.0 collective-permute-done.raw_ref
  1.8 0.1 collective-permute-start.4
  1.9 0.2 %fold.1.b0 = bf16[8,1024]{1,0:T(8,128)(2,1)S(1)} custom-call(bf16[64,64]{1,0:T(8,128)(2,1)S(1)} %get-tuple-element.19.order_ref, s32[1,1024]{1,0:T(1,128)S(1)} %get-tuple-element.20.contracted_ref.refs_0_, bf16[32,1024]{1,0:T(8,128)(2,1)S(1)} %get-tuple-element.21.own_ref, bf16[32,1024]{1,0:T(8,128)(2,1)S(1)} %collective-permute-done.raw_ref), custom_call_target="tpu_custom_call" | custom-call | flops 8388608 | bytes 131072 | tf_op jit(solution)/shard_map/fold/pallas_call | solution.py:173
  2.1 2.6 %collective-permute-start.1 = (bf16[8,1024]{1,0:T(8,128)(2,1)S(1)}, bf16[8,1024]{1,0:T(8,128)(2,1)S(1)}, u32[]{:S(2)}, u32[]{:S(2)}) collective-permute-start(bf16[8,1024]{1,0:T(8,128)(2,1)S(1)} %fold.1.b0), channel_id=1, source_target_pairs={{0,12},{1,13},{2,14},{3,15},{4,16},{5,17},{6,18},{7,19},{8,20},{9,... | collective-permute-start | bytes 49160 | tf_op jit(solution)/shard_map/ppermute | solution.py:284
  4.7 1.6 %collective-permute-start.3 = (bf16[8,1024]{1,0:T(8,128)(2,1)S(1)}, bf16[8,1024]{1,0:T(8,128)(2,1)S(1)}, u32[]{:S(2)}, u32[]{:S(2)}) collective-permute-start(bf16[8,1024]{1,0:T(8,128)(2,1)S(1)} %fold.1.b0), channel_id=1, source_target_pairs={{0,28},{1,29},{2,30},{3,31},{4,24},{5,25},{6,26},{7,27},{8,4},{9,5... | collective-permute-start | bytes 49160 | tf_op jit(solution)/shard_map/ppermute | solution.py:284
  6.3 0.0 collective-permute-done.1.b1
  6.3 1.3 %collective-permute-start.2 = (bf16[8,1024]{1,0:T(8,128)(2,1)S(1)}, bf16[8,1024]{1,0:T(8,128)(2,1)S(1)}, u32[]{:S(2)}, u32[]{:S(2)}) collective-permute-start(bf16[8,1024]{1,0:T(8,128)(2,1)S(1)} %collective-permute-done.1.b1), channel_id=1, source_target_pairs={{0,4},{1,5},{2,6},{3,7},{4,0},{5,1},{6,2},{7,3},{8,12},{9,13},{10,... | collective-permute-start | bytes 49160 | tf_op jit(solution)/shard_map/ppermute | solution.py:284
  7.6 0.4 %collective-permute-done.3.b3 = bf16[8,1024]{1,0:T(8,128)(2,1)S(1)} collective-permute-done((bf16[8,1024]{1,0:T(8,128)(2,1)S(1)}, bf16[8,1024]{1,0:T(8,128)(2,1)S(1)}, u32[]{:S(2)}, u32[]{:S(2)}) %collective-permute-start.3) | collective-permute-done | bytes 16416 | tf_op jit(solution)/shard_map/ppermute | solution.py:284
  8.0 0.4 %collective-permute-done.2.b2 = bf16[8,1024]{1,0:T(8,128)(2,1)S(1)} collective-permute-done((bf16[8,1024]{1,0:T(8,128)(2,1)S(1)}, bf16[8,1024]{1,0:T(8,128)(2,1)S(1)}, u32[]{:S(2)}, u32[]{:S(2)}) %collective-permute-start.2) | collective-permute-done | bytes 16416 | tf_op jit(solution)/shard_map/ppermute | solution.py:284
  8.4 0.0 collective-permute-done.4.refs_2_
  8.5 0.5 %sums.1 = (f32[16,512]{1,0:T(8,128)S(1)}, f32[8,512]{1,0:T(8,128)S(1)}, f32[8,512]{1,0:T(8,128)S(1)}) custom-call(bf16[8,1024]{1,0:T(8,128)(2,1)S(1)} %fold.1.b0, bf16[8,1024]{1,0:T(8,128)(2,1)S(1)} %collective-permute-done.1.b1, bf16[8,1024]{1,0:T(8,128)(2,1)S(1)} %collective-permute-done.2.b2, bf16[8,1024]{1,0:T(8,128)(2,1)S(1)} %collective-permute-done.3.b3, ...), custom_call_target="tpu_custom_call" | custom-call | flops 268435456 | bytes 2097152 | tf_op jit(solution)/shard_map/sums/pallas_call | solution.py:225
  8.9 1.7 %collective-permute-start.5 = (f32[16,512]{1,0:T(8,128)S(1)}, f32[16,512]{1,0:T(8,128)S(1)}, u32[]{:S(2)}, u32[]{:S(2)}) collective-permute-start(f32[16,512]{1,0:T(8,128)S(1)} %get-tuple-element.25), channel_id=1, source_target_pairs={{0,5},{1,6},{2,7},{3,4},{4,2},{5,3},{6,0},{7,1},{8,13},{9,14},{10,... | collective-permute-start | bytes 98312 | tf_op jit(solution)/shard_map/ppermute | solution.py:284
  10.6 2.1 %collective-permute-start.6 = (f32[8,512]{1,0:T(8,128)S(1)}, f32[8,512]{1,0:T(8,128)S(1)}, u32[]{:S(2)}, u32[]{:S(2)}) collective-permute-start(f32[8,512]{1,0:T(8,128)S(1)} %get-tuple-element.26), channel_id=1, source_target_pairs={{0,7},{1,4},{2,5},{3,6},{4,3},{5,0},{6,1},{7,2},{8,15},{9,12},{10,... | collective-permute-start | bytes 49160 | tf_op jit(solution)/shard_map/ppermute | solution.py:284
  12.7 0.5 %collective-permute-done.5.got_ref = f32[16,512]{1,0:T(8,128)S(1)} collective-permute-done((f32[16,512]{1,0:T(8,128)S(1)}, f32[16,512]{1,0:T(8,128)S(1)}, u32[]{:S(2)}, u32[]{:S(2)}) %collective-permute-start.5) | collective-permute-done | bytes 32800 | tf_op jit(solution)/shard_map/ppermute | solution.py:284
  13.2 1.3 %collective-permute-start.7 = (f32[8,512]{1,0:T(8,128)S(1)}, f32[8,512]{1,0:T(8,128)S(1)}, u32[]{:S(2)}, u32[]{:S(2)}) collective-permute-start(f32[8,512]{1,0:T(8,128)S(1)} %slice.4), channel_id=1, source_target_pairs={{0,4},{1,5},{2,6},{3,7},{4,0},{5,1},{6,2},{7,3},{8,12},{9,13},{10,... | collective-permute-start | bytes 49160 | tf_op jit(solution)/shard_map/ppermute | solution.py:284
  14.6 0.0 collective-permute-done.6.far_ref
  14.6 0.8 %collective-permute-done.7.too_ref = f32[8,512]{1,0:T(8,128)S(1)} collective-permute-done((f32[8,512]{1,0:T(8,128)S(1)}, f32[8,512]{1,0:T(8,128)S(1)}, u32[]{:S(2)}, u32[]{:S(2)}) %collective-permute-start.7) | collective-permute-done | bytes 16416 | tf_op jit(solution)/shard_map/ppermute | solution.py:284
  15.4 0.8 %expand.1 = f32[64,512]{1,0:T(8,128)} custom-call(f32[8,512]{1,0:T(8,128)S(1)} %get-tuple-element.24.keep_ref, f32[16,512]{1,0:T(8,128)S(1)} %collective-permute-done.5.got_ref, f32[8,512]{1,0:T(8,128)S(1)} %collective-permute-done.6.far_ref, f32[8,512]{1,0:T(8,128)S(1)} %collective-permute-done.7.too_ref, s32[64,128]{1,0:T(8,128)S(1)} %get-tuple-element.27.key_ref, ...), custom_call_target="tpu_custom_call" | custom-call | flops 1048576 | bytes 262144 | tf_op jit(solution)/shard_map/expand/pallas_call | solution.py:266
  (1 shorter events, 0.0 us)
Async XLA Ops:
  0.0 1.8 %collective-permute-start = (bf16[32,1024]{1,0:T(8,128)(2,1)}, bf16[32,1024]{1,0:T(8,128)(2,1)S(1)}, u32[]{:S(2)}, u32[]{:S(2)}) collective-permute-start(bf16[32,1024]{1,0:T(8,128)(2,1)} %amplitudes_ref.1), channel_id=1, source_target_pairs={{0,4},{1,5},{2,6},{3,7},{4,0},{5,1},{6,2},{7,3},{8,12},{9,13},{10,... | collective-permute-start | bytes 196616 | tf_op jit(solution)/shard_map/ppermute | solution.py:284
  1.8 6.6 %collective-permute-start.4 = (bf16[1040,512]{1,0:T(8,128)(2,1)S(1)}, bf16[1040,512]{1,0:T(8,128)(2,1)S(1)}, u32[]{:S(2)}, u32[]{:S(2)}) collective-permute-start(bf16[1040,512]{1,0:T(8,128)(2,1)S(1)} %get-tuple-element.23.refs_1_), channel_id=1, source_target_pairs={{0,4},{1,5},{2,6},{3,7},{4,0},{5,1},{6,2},{7,3},{8,12},{9,13},{10,... | collective-permute-start | bytes 3194888 | tf_op jit(solution)/shard_map/ppermute | solution.py:284
  2.1 4.2 %collective-permute-start.1 = (bf16[8,1024]{1,0:T(8,128)(2,1)S(1)}, bf16[8,1024]{1,0:T(8,128)(2,1)S(1)}, u32[]{:S(2)}, u32[]{:S(2)}) collective-permute-start(bf16[8,1024]{1,0:T(8,128)(2,1)S(1)} %fold.1.b0), channel_id=1, source_target_pairs={{0,12},{1,13},{2,14},{3,15},{4,16},{5,17},{6,18},{7,19},{8,20},{9,... | collective-permute-start | bytes 49160 | tf_op jit(solution)/shard_map/ppermute | solution.py:284
  4.7 3.3 %collective-permute-start.3 = (bf16[8,1024]{1,0:T(8,128)(2,1)S(1)}, bf16[8,1024]{1,0:T(8,128)(2,1)S(1)}, u32[]{:S(2)}, u32[]{:S(2)}) collective-permute-start(bf16[8,1024]{1,0:T(8,128)(2,1)S(1)} %fold.1.b0), channel_id=1, source_target_pairs={{0,28},{1,29},{2,30},{3,31},{4,24},{5,25},{6,26},{7,27},{8,4},{9,5... | collective-permute-start | bytes 49160 | tf_op jit(solution)/shard_map/ppermute | solution.py:284
  6.3 2.1 %collective-permute-start.2 = (bf16[8,1024]{1,0:T(8,128)(2,1)S(1)}, bf16[8,1024]{1,0:T(8,128)(2,1)S(1)}, u32[]{:S(2)}, u32[]{:S(2)}) collective-permute-start(bf16[8,1024]{1,0:T(8,128)(2,1)S(1)} %collective-permute-done.1.b1), channel_id=1, source_target_pairs={{0,4},{1,5},{2,6},{3,7},{4,0},{5,1},{6,2},{7,3},{8,12},{9,13},{10,... | collective-permute-start | bytes 49160 | tf_op jit(solution)/shard_map/ppermute | solution.py:284
  8.9 4.3 %collective-permute-start.5 = (f32[16,512]{1,0:T(8,128)S(1)}, f32[16,512]{1,0:T(8,128)S(1)}, u32[]{:S(2)}, u32[]{:S(2)}) collective-permute-start(f32[16,512]{1,0:T(8,128)S(1)} %get-tuple-element.25), channel_id=1, source_target_pairs={{0,5},{1,6},{2,7},{3,4},{4,2},{5,3},{6,0},{7,1},{8,13},{9,14},{10,... | collective-permute-start | bytes 98312 | tf_op jit(solution)/shard_map/ppermute | solution.py:284
  10.6 3.9 %collective-permute-start.6 = (f32[8,512]{1,0:T(8,128)S(1)}, f32[8,512]{1,0:T(8,128)S(1)}, u32[]{:S(2)}, u32[]{:S(2)}) collective-permute-start(f32[8,512]{1,0:T(8,128)S(1)} %get-tuple-element.26), channel_id=1, source_target_pairs={{0,7},{1,4},{2,5},{3,6},{4,3},{5,0},{6,1},{7,2},{8,15},{9,12},{10,... | collective-permute-start | bytes 49160 | tf_op jit(solution)/shard_map/ppermute | solution.py:284
  13.2 2.2 %collective-permute-start.7 = (f32[8,512]{1,0:T(8,128)S(1)}, f32[8,512]{1,0:T(8,128)S(1)}, u32[]{:S(2)}, u32[]{:S(2)}) collective-permute-start(f32[8,512]{1,0:T(8,128)S(1)} %slice.4), channel_id=1, source_target_pairs={{0,4},{1,5},{2,6},{3,7},{4,0},{5,1},{6,2},{7,3},{8,12},{9,13},{10,... | collective-permute-start | bytes 49160 | tf_op jit(solution)/shard_map/ppermute | solution.py:284

commit v7 on v6

--- a/solution.py
+++ b/solution.py
@@ -206,12 +206,12 @@
             total = jnp.where(outputs == g, each[g * 2 * slots : (g + 1) * 2 * slots], total)
         return total
 
-    sent = block(1 + member)
+    sent = block(2 - member)
     theirs = product(jnp.concatenate([sent, block(3)], 0), other_ref)
-    send_ref[:slots] = theirs[:slots]
+    send_ref[slots:] = theirs[:slots]
     far_ref[...] = theirs[slots:]
     ours = product(jnp.concatenate([sent, block(0)], 0), staged_ref)
-    send_ref[slots:] = ours[:slots]
+    send_ref[:slots] = ours[:slots]
     keep_ref[...] = ours[slots:]
 
 
@@ -304,7 +304,7 @@
     send, send_far, keep = sums(
         (packed, side, side_too, far), contracted, staged, other, slots
     )
-    got = move(send, lambda p, m, c: (p, 1 - m, (c + 1 + m) % COLS))
+    got = move(send, lambda p, m, c: (p, m, (c + 2 - m) % COLS))
     got_far = move(send_far, lambda p, m, c: (p, 1 - m, (c + 3) % COLS))
     got_too = move(got[slots:], sibling)
     return expand(keep, got, got_far, got_too, key, outputs)

time: 16.3 us -> 15.9 us (0.975)
  starting transfers between devices: 11.2 us -> 10.1 us
  waiting for transfers between devices: 2.17 us -> 2.86 us
    ppermute x8, starting transfers between devices: 11.2 us -> 10.1 us  [move(): return lax.ppermute(x, ('row', 'col'), pairs)]
    ppermute x8, waiting for transfers between devices: 2.17 us -> 2.86 us  [move(): return lax.ppermute(x, ('row', 'col'), pairs)]
  transfers between devices with their start and end apart: 8 -> 8, of which waited for: 4 -> 5; matrix products, arithmetic and copies ran while one was open for 0% -> 0% of each run, Pallas kernels for 9% -> 10%
where the time goes in v7:
time: 15.9 us; the launch traced here: 15.8 us
  starting transfers between devices  10.1 us (64%)
  waiting for transfers between devices  2.86 us (18%)
  Pallas kernels  2.77 us (17%)
    ppermute x8, starting transfers between devices, move(): return lax.ppermute(x, ('row', 'col'), pairs)  10.1 us
    ppermute x8, waiting for transfers between devices, move(): return lax.ppermute(x, ('row', 'col'), pairs)  2.86 us
    pallas_call x1, Pallas kernels, pack(): pl.pallas_call(functools.partial(pack_kernel, block), out_shape=(pltpu.VM...  1.35 us
    pallas_call x1, Pallas kernels, expand(): pl.pallas_call(expand_kernel, out_shape=pltpu.HBM((block, width), jnp.flo...  0.78 us
    pallas_call x1, Pallas kernels, sums(): pl.pallas_call(kernel, out_shape=(pltpu.VMEM((2 * slots, width), jnp.floa...  0.46 us
  transfers between devices with their start and end apart: 8, of which 5 were waited for; matrix products, arithmetic and copies ran while one was open for 0% of the time, Pallas kernels for 10%

profile of v7, /device:TPU:0, one launch (start us, length us, event | category | flops | bytes accessed | tf_op | source)
XLA Modules:
  0.0 15.8 jit_solution(13365465049251933417)
XLA Ops:
  0.0 0.5 %collective-permute-start = (bf16[32,1024]{1,0:T(8,128)(2,1)}, bf16[32,1024]{1,0:T(8,128)(2,1)S(1)}, u32[]{:S(2)}, u32[]{:S(2)}) collective-permute-start(bf16[32,1024]{1,0:T(8,128)(2,1)} %amplitudes_ref.1), channel_id=1, source_target_pairs={{0,4},{1,5},{2,6},{3,7},{4,0},{5,1},{6,2},{7,3},{8,12},{9,13},{10,... | collective-permute-start | bytes 196616 | tf_op jit(solution)/shard_map/ppermute | solution.py:284
  0.5 1.4 %pack.1 = (bf16[64,64]{1,0:T(8,128)(2,1)S(1)}, s32[64,128]{1,0:T(8,128)S(1)}, s32[1,1024]{1,0:T(1,128)S(1)}, s32[1,512]{1,0:T(1,128)S(1)}, bf16[32,1024]{1,0:T(8,128)(2,1)S(1)}, /*index=5*/bf16[1040,512]{1,0:T(8,128)(2,1)S(1)}) custom-call(s32[1,256]{1,0:T(1,128)} %bitcast.5, s32[1,1024]{1,0:T(1,128)} %bitcast.3, s32[1,512]{1,0:T(1,128)} %bitcast.4, ...), custom_call_target="tpu_custom_call" | custom-call | flops 1048576 | bytes 262144 | tf_op jit(solution)/shard_map/pack/pallas_call | solution.py:140
  1.8 0.0 collective-permute-done.raw_ref
  1.8 0.1 collective-permute-start.4
  1.9 0.2 %fold.1.b0 = bf16[8,1024]{1,0:T(8,128)(2,1)S(1)} custom-call(bf16[64,64]{1,0:T(8,128)(2,1)S(1)} %get-tuple-element.19.order_ref, s32[1,1024]{1,0:T(1,128)S(1)} %get-tuple-element.20.contracted_ref.refs_0_, bf16[32,1024]{1,0:T(8,128)(2,1)S(1)} %get-tuple-element.21.own_ref, bf16[32,1024]{1,0:T(8,128)(2,1)S(1)} %collective-permute-done.raw_ref), custom_call_target="tpu_custom_call" | custom-call | flops 8388608 | bytes 131072 | tf_op jit(solution)/shard_map/fold/pallas_call | solution.py:173
  2.1 2.6 %collective-permute-start.1 = (bf16[8,1024]{1,0:T(8,128)(2,1)S(1)}, bf16[8,1024]{1,0:T(8,128)(2,1)S(1)}, u32[]{:S(2)}, u32[]{:S(2)}) collective-permute-start(bf16[8,1024]{1,0:T(8,128)(2,1)S(1)} %fold.1.b0), channel_id=1, source_target_pairs={{0,12},{1,13},{2,14},{3,15},{4,16},{5,17},{6,18},{7,19},{8,20},{9,... | collective-permute-start | bytes 49160 | tf_op jit(solution)/shard_map/ppermute | solution.py:284
  4.7 1.6 %collective-permute-start.3 = (bf16[8,1024]{1,0:T(8,128)(2,1)S(1)}, bf16[8,1024]{1,0:T(8,128)(2,1)S(1)}, u32[]{:S(2)}, u32[]{:S(2)}) collective-permute-start(bf16[8,1024]{1,0:T(8,128)(2,1)S(1)} %fold.1.b0), channel_id=1, source_target_pairs={{0,28},{1,29},{2,30},{3,31},{4,24},{5,25},{6,26},{7,27},{8,4},{9,5... | collective-permute-start | bytes 49160 | tf_op jit(solution)/shard_map/ppermute | solution.py:284
  6.3 0.0 collective-permute-done.1.b1
  6.3 1.3 %collective-permute-start.2 = (bf16[8,1024]{1,0:T(8,128)(2,1)S(1)}, bf16[8,1024]{1,0:T(8,128)(2,1)S(1)}, u32[]{:S(2)}, u32[]{:S(2)}) collective-permute-start(bf16[8,1024]{1,0:T(8,128)(2,1)S(1)} %collective-permute-done.1.b1), channel_id=1, source_target_pairs={{0,4},{1,5},{2,6},{3,7},{4,0},{5,1},{6,2},{7,3},{8,12},{9,13},{10,... | collective-permute-start | bytes 49160 | tf_op jit(solution)/shard_map/ppermute | solution.py:284
  7.6 0.4 %collective-permute-done.3.b3 = bf16[8,1024]{1,0:T(8,128)(2,1)S(1)} collective-permute-done((bf16[8,1024]{1,0:T(8,128)(2,1)S(1)}, bf16[8,1024]{1,0:T(8,128)(2,1)S(1)}, u32[]{:S(2)}, u32[]{:S(2)}) %collective-permute-start.3) | collective-permute-done | bytes 16416 | tf_op jit(solution)/shard_map/ppermute | solution.py:284
  8.0 0.4 %collective-permute-done.2.b2 = bf16[8,1024]{1,0:T(8,128)(2,1)S(1)} collective-permute-done((bf16[8,1024]{1,0:T(8,128)(2,1)S(1)}, bf16[8,1024]{1,0:T(8,128)(2,1)S(1)}, u32[]{:S(2)}, u32[]{:S(2)}) %collective-permute-start.2) | collective-permute-done | bytes 16416 | tf_op jit(solution)/shard_map/ppermute | solution.py:284
  8.4 0.0 collective-permute-done.4.refs_2_
  8.5 0.5 %sums.1 = (f32[16,512]{1,0:T(8,128)S(1)}, f32[8,512]{1,0:T(8,128)S(1)}, f32[8,512]{1,0:T(8,128)S(1)}) custom-call(bf16[8,1024]{1,0:T(8,128)(2,1)S(1)} %fold.1.b0, bf16[8,1024]{1,0:T(8,128)(2,1)S(1)} %collective-permute-done.1.b1, bf16[8,1024]{1,0:T(8,128)(2,1)S(1)} %collective-permute-done.2.b2, bf16[8,1024]{1,0:T(8,128)(2,1)S(1)} %collective-permute-done.3.b3, ...), custom_call_target="tpu_custom_call" | custom-call | flops 268435456 | bytes 2097152 | tf_op jit(solution)/shard_map/sums/pallas_call | solution.py:225
  8.9 2.7 %collective-permute-start.5 = (f32[16,512]{1,0:T(8,128)S(1)}, f32[16,512]{1,0:T(8,128)S(1)}, u32[]{:S(2)}, u32[]{:S(2)}) collective-permute-start(f32[16,512]{1,0:T(8,128)S(1)} %get-tuple-element.25), channel_id=1, source_target_pairs={{0,2},{1,3},{2,0},{3,1},{4,5},{5,6},{6,7},{7,4},{8,10},{9,11},{10,... | collective-permute-start | bytes 98312 | tf_op jit(solution)/shard_map/ppermute | solution.py:284
  11.7 1.0 %collective-permute-start.6 = (f32[8,512]{1,0:T(8,128)S(1)}, f32[8,512]{1,0:T(8,128)S(1)}, u32[]{:S(2)}, u32[]{:S(2)}) collective-permute-start(f32[8,512]{1,0:T(8,128)S(1)} %get-tuple-element.26), channel_id=1, source_target_pairs={{0,7},{1,4},{2,5},{3,6},{4,3},{5,0},{6,1},{7,2},{8,15},{9,12},{10,... | collective-permute-start | bytes 49160 | tf_op jit(solution)/shard_map/ppermute | solution.py:284
  12.7 1.1 %collective-permute-done.5.got_ref = f32[16,512]{1,0:T(8,128)S(1)} collective-permute-done((f32[16,512]{1,0:T(8,128)S(1)}, f32[16,512]{1,0:T(8,128)S(1)}, u32[]{:S(2)}, u32[]{:S(2)}) %collective-permute-start.5) | collective-permute-done | bytes 32800 | tf_op jit(solution)/shard_map/ppermute | solution.py:284
  13.8 0.3 %collective-permute-start.7 = (f32[8,512]{1,0:T(8,128)S(1)}, f32[8,512]{1,0:T(8,128)S(1)}, u32[]{:S(2)}, u32[]{:S(2)}) collective-permute-start(f32[8,512]{1,0:T(8,128)S(1)} %slice.4), channel_id=1, source_target_pairs={{0,4},{1,5},{2,6},{3,7},{4,0},{5,1},{6,2},{7,3},{8,12},{9,13},{10,... | collective-permute-start | bytes 49160 | tf_op jit(solution)/shard_map/ppermute | solution.py:284
  14.0 0.8 %collective-permute-done.6.far_ref = f32[8,512]{1,0:T(8,128)S(1)} collective-permute-done((f32[8,512]{1,0:T(8,128)S(1)}, f32[8,512]{1,0:T(8,128)S(1)}, u32[]{:S(2)}, u32[]{:S(2)}) %collective-permute-start.6) | collective-permute-done | bytes 16416 | tf_op jit(solution)/shard_map/ppermute | solution.py:284
  14.9 0.1 collective-permute-done.7.too_ref
  15.0 0.8 %expand.1 = f32[64,512]{1,0:T(8,128)} custom-call(f32[8,512]{1,0:T(8,128)S(1)} %get-tuple-element.24.keep_ref, f32[16,512]{1,0:T(8,128)S(1)} %collective-permute-done.5.got_ref, f32[8,512]{1,0:T(8,128)S(1)} %collective-permute-done.6.far_ref, f32[8,512]{1,0:T(8,128)S(1)} %collective-permute-done.7.too_ref, s32[64,128]{1,0:T(8,128)S(1)} %get-tuple-element.27.key_ref, ...), custom_call_target="tpu_custom_call" | custom-call | flops 1048576 | bytes 262144 | tf_op jit(solution)/shard_map/expand/pallas_call | solution.py:266
  (1 shorter events, 0.0 us)
Async XLA Ops:
  0.0 1.8 %collective-permute-start = (bf16[32,1024]{1,0:T(8,128)(2,1)}, bf16[32,1024]{1,0:T(8,128)(2,1)S(1)}, u32[]{:S(2)}, u32[]{:S(2)}) collective-permute-start(bf16[32,1024]{1,0:T(8,128)(2,1)} %amplitudes_ref.1), channel_id=1, source_target_pairs={{0,4},{1,5},{2,6},{3,7},{4,0},{5,1},{6,2},{7,3},{8,12},{9,13},{10,... | collective-permute-start | bytes 196616 | tf_op jit(solution)/shard_map/ppermute | solution.py:284
  1.8 6.6 %collective-permute-start.4 = (bf16[1040,512]{1,0:T(8,128)(2,1)S(1)}, bf16[1040,512]{1,0:T(8,128)(2,1)S(1)}, u32[]{:S(2)}, u32[]{:S(2)}) collective-permute-start(bf16[1040,512]{1,0:T(8,128)(2,1)S(1)} %get-tuple-element.23.refs_1_), channel_id=1, source_target_pairs={{0,4},{1,5},{2,6},{3,7},{4,0},{5,1},{6,2},{7,3},{8,12},{9,13},{10,... | collective-permute-start | bytes 3194888 | tf_op jit(solution)/shard_map/ppermute | solution.py:284
  2.1 4.2 %collective-permute-start.1 = (bf16[8,1024]{1,0:T(8,128)(2,1)S(1)}, bf16[8,1024]{1,0:T(8,128)(2,1)S(1)}, u32[]{:S(2)}, u32[]{:S(2)}) collective-permute-start(bf16[8,1024]{1,0:T(8,128)(2,1)S(1)} %fold.1.b0), channel_id=1, source_target_pairs={{0,12},{1,13},{2,14},{3,15},{4,16},{5,17},{6,18},{7,19},{8,20},{9,... | collective-permute-start | bytes 49160 | tf_op jit(solution)/shard_map/ppermute | solution.py:284
  4.7 3.3 %collective-permute-start.3 = (bf16[8,1024]{1,0:T(8,128)(2,1)S(1)}, bf16[8,1024]{1,0:T(8,128)(2,1)S(1)}, u32[]{:S(2)}, u32[]{:S(2)}) collective-permute-start(bf16[8,1024]{1,0:T(8,128)(2,1)S(1)} %fold.1.b0), channel_id=1, source_target_pairs={{0,28},{1,29},{2,30},{3,31},{4,24},{5,25},{6,26},{7,27},{8,4},{9,5... | collective-permute-start | bytes 49160 | tf_op jit(solution)/shard_map/ppermute | solution.py:284
  6.3 2.1 %collective-permute-start.2 = (bf16[8,1024]{1,0:T(8,128)(2,1)S(1)}, bf16[8,1024]{1,0:T(8,128)(2,1)S(1)}, u32[]{:S(2)}, u32[]{:S(2)}) collective-permute-start(bf16[8,1024]{1,0:T(8,128)(2,1)S(1)} %collective-permute-done.1.b1), channel_id=1, source_target_pairs={{0,4},{1,5},{2,6},{3,7},{4,0},{5,1},{6,2},{7,3},{8,12},{9,13},{10,... | collective-permute-start | bytes 49160 | tf_op jit(solution)/shard_map/ppermute | solution.py:284
  8.9 4.9 %collective-permute-start.5 = (f32[16,512]{1,0:T(8,128)S(1)}, f32[16,512]{1,0:T(8,128)S(1)}, u32[]{:S(2)}, u32[]{:S(2)}) collective-permute-start(f32[16,512]{1,0:T(8,128)S(1)} %get-tuple-element.25), channel_id=1, source_target_pairs={{0,2},{1,3},{2,0},{3,1},{4,5},{5,6},{6,7},{7,4},{8,10},{9,11},{10,... | collective-permute-start | bytes 98312 | tf_op jit(solution)/shard_map/ppermute | solution.py:284
  11.7 3.2 %collective-permute-start.6 = (f32[8,512]{1,0:T(8,128)S(1)}, f32[8,512]{1,0:T(8,128)S(1)}, u32[]{:S(2)}, u32[]{:S(2)}) collective-permute-start(f32[8,512]{1,0:T(8,128)S(1)} %get-tuple-element.26), channel_id=1, source_target_pairs={{0,7},{1,4},{2,5},{3,6},{4,3},{5,0},{6,1},{7,2},{8,15},{9,12},{10,... | collective-permute-start | bytes 49160 | tf_op jit(solution)/shard_map/ppermute | solution.py:284
  13.8 1.2 %collective-permute-start.7 = (f32[8,512]{1,0:T(8,128)S(1)}, f32[8,512]{1,0:T(8,128)S(1)}, u32[]{:S(2)}, u32[]{:S(2)}) collective-permute-start(f32[8,512]{1,0:T(8,128)S(1)} %slice.4), channel_id=1, source_target_pairs={{0,4},{1,5},{2,6},{3,7},{4,0},{5,1},{6,2},{7,3},{8,12},{9,13},{10,... | collective-permute-start | bytes 49160 | tf_op jit(solution)/shard_map/ppermute | solution.py:284

commit v8 on v7

--- a/solution.py
+++ b/solution.py
@@ -181,10 +181,37 @@
     )(*[in_vmem(x) for x in args])
 
 
-def sums_kernel(slots, blocks_refs, contracted_ref, staged_ref, other_ref, send_ref, far_ref, keep_ref):
+def mask_kernel(contracted_ref, staged_ref, other_ref, masked_ref, other_masked_ref):
+    depth = masked_ref.shape[0]
+    size = 128
+    lane = lax.broadcasted_iota(jnp.int32, (size, size), 1)
+    sublane = lax.broadcasted_iota(jnp.int32, (size, size), 0)
+    labels = [ref[depth : depth + 1].astype(jnp.float32) for ref in (staged_ref, other_ref)]
+    for n in range(depth // size):
+        rows = slice(n * size, (n + 1) * size)
+        row = contracted_ref[:, rows].astype(jnp.float32)
+        column = jnp.sum(jnp.where(lane == sublane, row, 0.0), axis=1, keepdims=True)
+        for label, src, dst in zip(labels, (staged_ref, other_ref), (masked_ref, other_masked_ref)):
+            kept = jnp.where(column == label, src[rows].astype(jnp.float32), 0.0)
+            dst[rows] = kept.astype(jnp.bfloat16)
+
+
+def mask(contracted, staged, other):
+    depth, width = contracted.shape[1], staged.shape[1]
+    return pl.pallas_call(
+        mask_kernel,
+        out_shape=(pltpu.VMEM((depth, width), jnp.bfloat16),) * 2,
+        in_specs=[pl.BlockSpec(memory_space=pltpu.VMEM)] * 3,
+        out_specs=[pl.BlockSpec(memory_space=pltpu.VMEM)] * 2,
+        compiler_params=pltpu.CompilerParams(vmem_limit_bytes=16 << 20),
+        cost_estimate=pl.CostEstimate(flops=1 << 21, bytes_accessed=1 << 22, transcendentals=0),
+        name="mask",
+    )(*[in_vmem(x) for x in (contracted, staged, other)])
+
+
+def sums_kernel(slots, blocks_refs, staged_ref, other_ref, send_ref, far_ref, keep_ref):
     row, col = lax.axis_index("row"), lax.axis_index("col")
     place, member = row // CORES, row % CORES
-    contracted = contracted_ref[...]
     blocks = [ref[...].astype(jnp.float32) for ref in blocks_refs]
 
     def block(t):
@@ -195,16 +222,8 @@
             chosen = jnp.where(turned == n, blocks[n], chosen)
         return chosen
 
-    depth = contracted.shape[1]
-
     def product(rows, ref):
-        outputs = ref[depth : depth + 1].astype(jnp.float32)
-        spread = jnp.concatenate([jnp.where(contracted == g, rows, 0.0) for g in range(IRREPS)], axis=0)
-        each = jnp.dot(spread.astype(jnp.bfloat16), ref[:depth], preferred_element_type=jnp.float32)
-        total = jnp.zeros((2 * slots, each.shape[1]), jnp.float32)
-        for g in range(IRREPS):
-            total = jnp.where(outputs == g, each[g * 2 * slots : (g + 1) * 2 * slots], total)
-        return total
+        return jnp.dot(rows.astype(jnp.bfloat16), ref[...], preferred_element_type=jnp.float32)
 
     sent = block(2 - member)
     theirs = product(jnp.concatenate([sent, block(3)], 0), other_ref)
@@ -215,13 +234,13 @@
     keep_ref[...] = ours[slots:]
 
 
-def sums(blocks, contracted, staged, other, slots):
+def sums(blocks, staged, other, slots):
     width = staged.shape[1]
 
     def kernel(b0, b1, b2, b3, *refs):
         sums_kernel(slots, (b0, b1, b2, b3), *refs)
 
-    args = [*blocks, contracted, staged, other]
+    args = [*blocks, staged, other]
     return pl.pallas_call(
         kernel,
         out_shape=(
@@ -301,8 +320,9 @@
     side = move(packed, lambda p, m, c: ((p + 1 + m) % PLACES, 1 - m, c))
     far = move(packed, lambda p, m, c: ((p + 3) % PLACES, 1 - m, c))
     side_too = move(side, sibling)
+    masked, other_masked = mask(contracted, staged, other)
     send, send_far, keep = sums(
-        (packed, side, side_too, far), contracted, staged, other, slots
+        (packed, side, side_too, far), masked, other_masked, slots
     )
     got = move(send, lambda p, m, c: (p, m, (c + 2 - m) % COLS))
     got_far = move(send_far, lambda p, m, c: (p, 1 - m, (c + 3) % COLS))

time: 15.9 us -> 15.8 us (level)
  waiting for transfers between devices: 2.86 us -> 2.34 us
  Pallas kernels: 2.77 us -> 3.24 us
    pallas_call x0 -> x1, Pallas kernels: none -> 0.56 us  [mask(): pl.pallas_call(mask_kernel, out_shape=(pltpu.VMEM((depth, width), jnp.bfl...]
    ppermute x8, waiting for transfers between devices: 2.86 us -> 2.34 us  [move(): return lax.ppermute(x, ('row', 'col'), pairs)]
  transfers between devices with their start and end apart: 8 -> 8, of which waited for: 5 -> 4; matrix products, arithmetic and copies ran while one was open for 0% -> 0% of each run, Pallas kernels for 10% -> 13%
where the time goes in v8:
time: 15.8 us; the launch traced here: 15.6 us
  starting transfers between devices  10 us (63%)
  Pallas kernels  3.24 us (21%)
  waiting for transfers between devices  2.34 us (15%)
    ppermute x8, starting transfers between devices, move(): return lax.ppermute(x, ('row', 'col'), pairs)  10 us
    ppermute x8, waiting for transfers between devices, move(): return lax.ppermute(x, ('row', 'col'), pairs)  2.34 us
    pallas_call x1, Pallas kernels, pack(): pl.pallas_call(functools.partial(pack_kernel, block), out_shape=(pltpu.VM...  1.35 us
    pallas_call x1, Pallas kernels, expand(): pl.pallas_call(expand_kernel, out_shape=pltpu.HBM((block, width), jnp.flo...  0.78 us
    pallas_call x1, Pallas kernels, mask(): pl.pallas_call(mask_kernel, out_shape=(pltpu.VMEM((depth, width), jnp.bfl...  0.56 us
    pallas_call x1, Pallas kernels, sums(): pl.pallas_call(kernel, out_shape=(pltpu.VMEM((2 * slots, width), jnp.floa...  0.38 us
  transfers between devices with their start and end apart: 8, of which 4 were waited for; matrix products, arithmetic and copies ran while one was open for 0% of the time, Pallas kernels for 13%

profile of v8, /device:TPU:0, one launch (start us, length us, event | category | flops | bytes accessed | tf_op | source)
XLA Modules:
  0.0 15.6 jit_solution(6058379640226977836)
XLA Ops:
  0.0 0.5 %collective-permute-start = (bf16[32,1024]{1,0:T(8,128)(2,1)}, bf16[32,1024]{1,0:T(8,128)(2,1)S(1)}, u32[]{:S(2)}, u32[]{:S(2)}) collective-permute-start(bf16[32,1024]{1,0:T(8,128)(2,1)} %amplitudes_ref.1), channel_id=1, source_target_pairs={{0,4},{1,5},{2,6},{3,7},{4,0},{5,1},{6,2},{7,3},{8,12},{9,13},{10,... | collective-permute-start | bytes 196616 | tf_op jit(solution)/shard_map/ppermute | solution.py:303
  0.5 1.4 %pack.1 = (bf16[64,64]{1,0:T(8,128)(2,1)S(1)}, s32[64,128]{1,0:T(8,128)S(1)}, s32[1,1024]{1,0:T(1,128)S(1)}, s32[1,512]{1,0:T(1,128)S(1)}, bf16[32,1024]{1,0:T(8,128)(2,1)S(1)}, /*index=5*/bf16[1040,512]{1,0:T(8,128)(2,1)S(1)}) custom-call(s32[1,256]{1,0:T(1,128)} %bitcast.5, s32[1,1024]{1,0:T(1,128)} %bitcast.3, s32[1,512]{1,0:T(1,128)} %bitcast.4, ...), custom_call_target="tpu_custom_call" | custom-call | flops 1048576 | bytes 262144 | tf_op jit(solution)/shard_map/pack/pallas_call | solution.py:140
  1.8 0.0 collective-permute-done.raw_ref
  1.8 0.1 collective-permute-start.4
  1.9 0.2 %fold.1.b0 = bf16[8,1024]{1,0:T(8,128)(2,1)S(1)} custom-call(bf16[64,64]{1,0:T(8,128)(2,1)S(1)} %get-tuple-element.21.order_ref, s32[1,1024]{1,0:T(1,128)S(1)} %get-tuple-element.22.contracted_ref, bf16[32,1024]{1,0:T(8,128)(2,1)S(1)} %get-tuple-element.23.own_ref, bf16[32,1024]{1,0:T(8,128)(2,1)S(1)} %collective-permute-done.raw_ref), custom_call_target="tpu_custom_call" | custom-call | flops 8388608 | bytes 131072 | tf_op jit(solution)/shard_map/fold/pallas_call | solution.py:173
  2.1 2.6 %collective-permute-start.1 = (bf16[8,1024]{1,0:T(8,128)(2,1)S(1)}, bf16[8,1024]{1,0:T(8,128)(2,1)S(1)}, u32[]{:S(2)}, u32[]{:S(2)}) collective-permute-start(bf16[8,1024]{1,0:T(8,128)(2,1)S(1)} %fold.1.b0), channel_id=1, source_target_pairs={{0,12},{1,13},{2,14},{3,15},{4,16},{5,17},{6,18},{7,19},{8,20},{9,... | collective-permute-start | bytes 49160 | tf_op jit(solution)/shard_map/ppermute | solution.py:303
  4.7 1.6 %collective-permute-start.3 = (bf16[8,1024]{1,0:T(8,128)(2,1)S(1)}, bf16[8,1024]{1,0:T(8,128)(2,1)S(1)}, u32[]{:S(2)}, u32[]{:S(2)}) collective-permute-start(bf16[8,1024]{1,0:T(8,128)(2,1)S(1)} %fold.1.b0), channel_id=1, source_target_pairs={{0,28},{1,29},{2,30},{3,31},{4,24},{5,25},{6,26},{7,27},{8,4},{9,5... | collective-permute-start | bytes 49160 | tf_op jit(solution)/shard_map/ppermute | solution.py:303
  6.3 0.0 collective-permute-done.1.b1
  6.3 1.3 %collective-permute-start.2 = (bf16[8,1024]{1,0:T(8,128)(2,1)S(1)}, bf16[8,1024]{1,0:T(8,128)(2,1)S(1)}, u32[]{:S(2)}, u32[]{:S(2)}) collective-permute-start(bf16[8,1024]{1,0:T(8,128)(2,1)S(1)} %collective-permute-done.1.b1), channel_id=1, source_target_pairs={{0,4},{1,5},{2,6},{3,7},{4,0},{5,1},{6,2},{7,3},{8,12},{9,13},{10,... | collective-permute-start | bytes 49160 | tf_op jit(solution)/shard_map/ppermute | solution.py:303
  7.6 0.0 collective-permute-done.4.other_ref
  7.6 0.6 %mask.1 = (bf16[1024,512]{1,0:T(8,128)(2,1)S(1)}, bf16[1024,512]{1,0:T(8,128)(2,1)S(1)}) custom-call(s32[1,1024]{1,0:T(1,128)S(1)} %get-tuple-element.22.contracted_ref, bf16[1040,512]{1,0:T(8,128)(2,1)S(1)} %get-tuple-element.25.staged_ref, bf16[1040,512]{1,0:T(8,128)(2,1)S(1)} %collective-permute-done.4.other_ref), custom_call_target="tpu_custom_call" | custom-call | flops 2097152 | bytes 4194304 | tf_op jit(solution)/shard_map/mask/pallas_call | solution.py:201
  8.2 0.0 collective-permute-done.3.b3
  8.2 0.3 %collective-permute-done.2.b2 = bf16[8,1024]{1,0:T(8,128)(2,1)S(1)} collective-permute-done((bf16[8,1024]{1,0:T(8,128)(2,1)S(1)}, bf16[8,1024]{1,0:T(8,128)(2,1)S(1)}, u32[]{:S(2)}, u32[]{:S(2)}) %collective-permute-start.2) | collective-permute-done | bytes 16416 | tf_op jit(solution)/shard_map/ppermute | solution.py:303
  8.4 0.4 %sums.1 = (f32[16,512]{1,0:T(8,128)S(1)}, f32[8,512]{1,0:T(8,128)S(1)}, f32[8,512]{1,0:T(8,128)S(1)}) custom-call(bf16[8,1024]{1,0:T(8,128)(2,1)S(1)} %fold.1.b0, bf16[8,1024]{1,0:T(8,128)(2,1)S(1)} %collective-permute-done.1.b1, bf16[8,1024]{1,0:T(8,128)(2,1)S(1)} %collective-permute-done.2.b2, bf16[8,1024]{1,0:T(8,128)(2,1)S(1)} %collective-permute-done.3.b3, ...), custom_call_target="tpu_custom_call" | custom-call | flops 268435456 | bytes 2097152 | tf_op jit(solution)/shard_map/sums/pallas_call | solution.py:244
  8.8 2.7 %collective-permute-start.5 = (f32[16,512]{1,0:T(8,128)S(1)}, f32[16,512]{1,0:T(8,128)S(1)}, u32[]{:S(2)}, u32[]{:S(2)}) collective-permute-start(f32[16,512]{1,0:T(8,128)S(1)} %get-tuple-element.29), channel_id=1, source_target_pairs={{0,2},{1,3},{2,0},{3,1},{4,5},{5,6},{6,7},{7,4},{8,10},{9,11},{10,... | collective-permute-start | bytes 98312 | tf_op jit(solution)/shard_map/ppermute | solution.py:303
  11.5 1.0 %collective-permute-start.6 = (f32[8,512]{1,0:T(8,128)S(1)}, f32[8,512]{1,0:T(8,128)S(1)}, u32[]{:S(2)}, u32[]{:S(2)}) collective-permute-start(f32[8,512]{1,0:T(8,128)S(1)} %get-tuple-element.30), channel_id=1, source_target_pairs={{0,7},{1,4},{2,5},{3,6},{4,3},{5,0},{6,1},{7,2},{8,15},{9,12},{10,... | collective-permute-start | bytes 49160 | tf_op jit(solution)/shard_map/ppermute | solution.py:303
  12.5 1.1 %collective-permute-done.5.got_ref = f32[16,512]{1,0:T(8,128)S(1)} collective-permute-done((f32[16,512]{1,0:T(8,128)S(1)}, f32[16,512]{1,0:T(8,128)S(1)}, u32[]{:S(2)}, u32[]{:S(2)}) %collective-permute-start.5) | collective-permute-done | bytes 32800 | tf_op jit(solution)/shard_map/ppermute | solution.py:303
  13.7 0.3 %collective-permute-start.7 = (f32[8,512]{1,0:T(8,128)S(1)}, f32[8,512]{1,0:T(8,128)S(1)}, u32[]{:S(2)}, u32[]{:S(2)}) collective-permute-start(f32[8,512]{1,0:T(8,128)S(1)} %slice.4), channel_id=1, source_target_pairs={{0,4},{1,5},{2,6},{3,7},{4,0},{5,1},{6,2},{7,3},{8,12},{9,13},{10,... | collective-permute-start | bytes 49160 | tf_op jit(solution)/shard_map/ppermute | solution.py:303
  13.9 0.8 %collective-permute-done.6.far_ref = f32[8,512]{1,0:T(8,128)S(1)} collective-permute-done((f32[8,512]{1,0:T(8,128)S(1)}, f32[8,512]{1,0:T(8,128)S(1)}, u32[]{:S(2)}, u32[]{:S(2)}) %collective-permute-start.6) | collective-permute-done | bytes 16416 | tf_op jit(solution)/shard_map/ppermute | solution.py:303
  14.7 0.1 collective-permute-done.7.too_ref
  14.8 0.8 %expand.1 = f32[64,512]{1,0:T(8,128)} custom-call(f32[8,512]{1,0:T(8,128)S(1)} %get-tuple-element.28.keep_ref, f32[16,512]{1,0:T(8,128)S(1)} %collective-permute-done.5.got_ref, f32[8,512]{1,0:T(8,128)S(1)} %collective-permute-done.6.far_ref, f32[8,512]{1,0:T(8,128)S(1)} %collective-permute-done.7.too_ref, s32[64,128]{1,0:T(8,128)S(1)} %get-tuple-element.31.key_ref, ...), custom_call_target="tpu_custom_call" | custom-call | flops 1048576 | bytes 262144 | tf_op jit(solution)/shard_map/expand/pallas_call | solution.py:285
  (1 shorter events, 0.0 us)
Async XLA Ops:
  0.0 1.8 %collective-permute-start = (bf16[32,1024]{1,0:T(8,128)(2,1)}, bf16[32,1024]{1,0:T(8,128)(2,1)S(1)}, u32[]{:S(2)}, u32[]{:S(2)}) collective-permute-start(bf16[32,1024]{1,0:T(8,128)(2,1)} %amplitudes_ref.1), channel_id=1, source_target_pairs={{0,4},{1,5},{2,6},{3,7},{4,0},{5,1},{6,2},{7,3},{8,12},{9,13},{10,... | collective-permute-start | bytes 196616 | tf_op jit(solution)/shard_map/ppermute | solution.py:303
  1.8 5.8 %collective-permute-start.4 = (bf16[1040,512]{1,0:T(8,128)(2,1)S(1)}, bf16[1040,512]{1,0:T(8,128)(2,1)S(1)}, u32[]{:S(2)}, u32[]{:S(2)}) collective-permute-start(bf16[1040,512]{1,0:T(8,128)(2,1)S(1)} %get-tuple-element.25.staged_ref), channel_id=1, source_target_pairs={{0,4},{1,5},{2,6},{3,7},{4,0},{5,1},{6,2},{7,3},{8,12},{9,13},{10,... | collective-permute-start | bytes 3194888 | tf_op jit(solution)/shard_map/ppermute | solution.py:303
  2.1 4.2 %collective-permute-start.1 = (bf16[8,1024]{1,0:T(8,128)(2,1)S(1)}, bf16[8,1024]{1,0:T(8,128)(2,1)S(1)}, u32[]{:S(2)}, u32[]{:S(2)}) collective-permute-start(bf16[8,1024]{1,0:T(8,128)(2,1)S(1)} %fold.1.b0), channel_id=1, source_target_pairs={{0,12},{1,13},{2,14},{3,15},{4,16},{5,17},{6,18},{7,19},{8,20},{9,... | collective-permute-start | bytes 49160 | tf_op jit(solution)/shard_map/ppermute | solution.py:303
  4.7 3.4 %collective-permute-start.3 = (bf16[8,1024]{1,0:T(8,128)(2,1)S(1)}, bf16[8,1024]{1,0:T(8,128)(2,1)S(1)}, u32[]{:S(2)}, u32[]{:S(2)}) collective-permute-start(bf16[8,1024]{1,0:T(8,128)(2,1)S(1)} %fold.1.b0), channel_id=1, source_target_pairs={{0,28},{1,29},{2,30},{3,31},{4,24},{5,25},{6,26},{7,27},{8,4},{9,5... | collective-permute-start | bytes 49160 | tf_op jit(solution)/shard_map/ppermute | solution.py:303
  6.3 2.1 %collective-permute-start.2 = (bf16[8,1024]{1,0:T(8,128)(2,1)S(1)}, bf16[8,1024]{1,0:T(8,128)(2,1)S(1)}, u32[]{:S(2)}, u32[]{:S(2)}) collective-permute-start(bf16[8,1024]{1,0:T(8,128)(2,1)S(1)} %collective-permute-done.1.b1), channel_id=1, source_target_pairs={{0,4},{1,5},{2,6},{3,7},{4,0},{5,1},{6,2},{7,3},{8,12},{9,13},{10,... | collective-permute-start | bytes 49160 | tf_op jit(solution)/shard_map/ppermute | solution.py:303
  8.8 4.8 %collective-permute-start.5 = (f32[16,512]{1,0:T(8,128)S(1)}, f32[16,512]{1,0:T(8,128)S(1)}, u32[]{:S(2)}, u32[]{:S(2)}) collective-permute-start(f32[16,512]{1,0:T(8,128)S(1)} %get-tuple-element.29), channel_id=1, source_target_pairs={{0,2},{1,3},{2,0},{3,1},{4,5},{5,6},{6,7},{7,4},{8,10},{9,11},{10,... | collective-permute-start | bytes 98312 | tf_op jit(solution)/shard_map/ppermute | solution.py:303
  11.5 3.2 %collective-permute-start.6 = (f32[8,512]{1,0:T(8,128)S(1)}, f32[8,512]{1,0:T(8,128)S(1)}, u32[]{:S(2)}, u32[]{:S(2)}) collective-permute-start(f32[8,512]{1,0:T(8,128)S(1)} %get-tuple-element.30), channel_id=1, source_target_pairs={{0,7},{1,4},{2,5},{3,6},{4,3},{5,0},{6,1},{7,2},{8,15},{9,12},{10,... | collective-permute-start | bytes 49160 | tf_op jit(solution)/shard_map/ppermute | solution.py:303
  13.7 1.2 %collective-permute-start.7 = (f32[8,512]{1,0:T(8,128)S(1)}, f32[8,512]{1,0:T(8,128)S(1)}, u32[]{:S(2)}, u32[]{:S(2)}) collective-permute-start(f32[8,512]{1,0:T(8,128)S(1)} %slice.4), channel_id=1, source_target_pairs={{0,4},{1,5},{2,6},{3,7},{4,0},{5,1},{6,2},{7,3},{8,12},{9,13},{10,... | collective-permute-start | bytes 49160 | tf_op jit(solution)/shard_map/ppermute | solution.py:303

commit v9 on v8

--- a/solution.py
+++ b/solution.py
@@ -319,8 +319,9 @@
 
     side = move(packed, lambda p, m, c: ((p + 1 + m) % PLACES, 1 - m, c))
     far = move(packed, lambda p, m, c: ((p + 3) % PLACES, 1 - m, c))
+    masked, other_masked = mask(contracted, staged, other)
+    side, masked = lax.optimization_barrier((side, masked))
     side_too = move(side, sibling)
-    masked, other_masked = mask(contracted, staged, other)
     send, send_far, keep = sums(
         (packed, side, side_too, far), masked, other_masked, slots
     )

time: 15.8 us -> 15.8 us (level)
  starting transfers between devices: 10 us -> 9.42 us
  waiting for transfers between devices: 2.34 us -> 2.92 us
    ppermute x8, starting transfers between devices: 10 us -> 9.42 us  [move(): return lax.ppermute(x, ('row', 'col'), pairs)]
    ppermute x8, waiting for transfers between devices: 2.34 us -> 2.92 us  [move(): return lax.ppermute(x, ('row', 'col'), pairs)]
  transfers between devices with their start and end apart: 8 -> 8, of which waited for: 4 -> 5; matrix products, arithmetic and copies ran while one was open for 0% -> 0% of each run, Pallas kernels for 13% -> 13%
where the time goes in v9:
time: 15.8 us; the launch traced here: 15.6 us
  starting transfers between devices  9.42 us (60%)
  Pallas kernels  3.24 us (21%)
  waiting for transfers between devices  2.92 us (18%)
    ppermute x8, starting transfers between devices, move(): return lax.ppermute(x, ('row', 'col'), pairs)  9.42 us
    ppermute x8, waiting for transfers between devices, move(): return lax.ppermute(x, ('row', 'col'), pairs)  2.92 us
    pallas_call x1, Pallas kernels, pack(): pl.pallas_call(functools.partial(pack_kernel, block), out_shape=(pltpu.VM...  1.35 us
    pallas_call x1, Pallas kernels, expand(): pl.pallas_call(expand_kernel, out_shape=pltpu.HBM((block, width), jnp.flo...  0.78 us
    pallas_call x1, Pallas kernels, mask(): pl.pallas_call(mask_kernel, out_shape=(pltpu.VMEM((depth, width), jnp.bfl...  0.56 us
    pallas_call x1, Pallas kernels, sums(): pl.pallas_call(kernel, out_shape=(pltpu.VMEM((2 * slots, width), jnp.floa...  0.38 us
  transfers between devices with their start and end apart: 8, of which 5 were waited for; matrix products, arithmetic and copies ran while one was open for 0% of the time, Pallas kernels for 13%

profile of v9, /device:TPU:0, one launch (start us, length us, event | category | flops | bytes accessed | tf_op | source)
XLA Modules:
  0.0 15.6 jit_solution(4273714676949022554)
XLA Ops:
  0.0 0.5 %collective-permute-start = (bf16[32,1024]{1,0:T(8,128)(2,1)}, bf16[32,1024]{1,0:T(8,128)(2,1)S(1)}, u32[]{:S(2)}, u32[]{:S(2)}) collective-permute-start(bf16[32,1024]{1,0:T(8,128)(2,1)} %amplitudes_ref.1), channel_id=1, source_target_pairs={{0,4},{1,5},{2,6},{3,7},{4,0},{5,1},{6,2},{7,3},{8,12},{9,13},{10,... | collective-permute-start | bytes 196616 | tf_op jit(solution)/shard_map/ppermute | solution.py:303
  0.5 1.4 %pack.1 = (bf16[64,64]{1,0:T(8,128)(2,1)S(1)}, s32[64,128]{1,0:T(8,128)S(1)}, s32[1,1024]{1,0:T(1,128)S(1)}, s32[1,512]{1,0:T(1,128)S(1)}, bf16[32,1024]{1,0:T(8,128)(2,1)S(1)}, /*index=5*/bf16[1040,512]{1,0:T(8,128)(2,1)S(1)}) custom-call(s32[1,256]{1,0:T(1,128)} %bitcast.5, s32[1,1024]{1,0:T(1,128)} %bitcast.3, s32[1,512]{1,0:T(1,128)} %bitcast.4, ...), custom_call_target="tpu_custom_call" | custom-call | flops 1048576 | bytes 262144 | tf_op jit(solution)/shard_map/pack/pallas_call | solution.py:140
  1.8 0.0 collective-permute-done.raw_ref
  1.8 0.1 collective-permute-start.2
  1.9 0.2 %fold.1.b0 = bf16[8,1024]{1,0:T(8,128)(2,1)S(1)} custom-call(bf16[64,64]{1,0:T(8,128)(2,1)S(1)} %get-tuple-element.23.order_ref, s32[1,1024]{1,0:T(1,128)S(1)} %get-tuple-element.24.contracted_ref, bf16[32,1024]{1,0:T(8,128)(2,1)S(1)} %get-tuple-element.25.own_ref, bf16[32,1024]{1,0:T(8,128)(2,1)S(1)} %collective-permute-done.raw_ref), custom_call_target="tpu_custom_call" | custom-call | flops 8388608 | bytes 131072 | tf_op jit(solution)/shard_map/fold/pallas_call | solution.py:173
  2.1 2.6 %collective-permute-start.1 = (bf16[8,1024]{1,0:T(8,128)(2,1)S(1)}, bf16[8,1024]{1,0:T(8,128)(2,1)S(1)}, u32[]{:S(2)}, u32[]{:S(2)}) collective-permute-start(bf16[8,1024]{1,0:T(8,128)(2,1)S(1)} %fold.1.b0), channel_id=1, source_target_pairs={{0,12},{1,13},{2,14},{3,15},{4,16},{5,17},{6,18},{7,19},{8,20},{9,... | collective-permute-start | bytes 49160 | tf_op jit(solution)/shard_map/ppermute | solution.py:303
  4.7 1.6 %collective-permute-start.4 = (bf16[8,1024]{1,0:T(8,128)(2,1)S(1)}, bf16[8,1024]{1,0:T(8,128)(2,1)S(1)}, u32[]{:S(2)}, u32[]{:S(2)}) collective-permute-start(bf16[8,1024]{1,0:T(8,128)(2,1)S(1)} %fold.1.b0), channel_id=1, source_target_pairs={{0,28},{1,29},{2,30},{3,31},{4,24},{5,25},{6,26},{7,27},{8,4},{9,5... | collective-permute-start | bytes 49160 | tf_op jit(solution)/shard_map/ppermute | solution.py:303
  6.3 0.0 collective-permute-done.2.other_ref
  6.3 0.6 %mask.1 = (bf16[1024,512]{1,0:T(8,128)(2,1)S(1)}, bf16[1024,512]{1,0:T(8,128)(2,1)S(1)}) custom-call(s32[1,1024]{1,0:T(1,128)S(1)} %get-tuple-element.24.contracted_ref, bf16[1040,512]{1,0:T(8,128)(2,1)S(1)} %get-tuple-element.27.staged_ref, bf16[1040,512]{1,0:T(8,128)(2,1)S(1)} %collective-permute-done.2.other_ref), custom_call_target="tpu_custom_call" | custom-call | flops 2097152 | bytes 4194304 | tf_op jit(solution)/shard_map/mask/pallas_call | solution.py:201
  6.9 0.0 collective-permute-done.1.b1
  6.9 0.7 %collective-permute-start.3 = (bf16[8,1024]{1,0:T(8,128)(2,1)S(1)}, bf16[8,1024]{1,0:T(8,128)(2,1)S(1)}, u32[]{:S(2)}, u32[]{:S(2)}) collective-permute-start(bf16[8,1024]{1,0:T(8,128)(2,1)S(1)} %collective-permute-done.1.b1), channel_id=1, source_target_pairs={{0,4},{1,5},{2,6},{3,7},{4,0},{5,1},{6,2},{7,3},{8,12},{9,13},{10,... | collective-permute-start | bytes 49160 | tf_op jit(solution)/shard_map/ppermute | solution.py:303
  7.6 0.4 %collective-permute-done.4.b3 = bf16[8,1024]{1,0:T(8,128)(2,1)S(1)} collective-permute-done((bf16[8,1024]{1,0:T(8,128)(2,1)S(1)}, bf16[8,1024]{1,0:T(8,128)(2,1)S(1)}, u32[]{:S(2)}, u32[]{:S(2)}) %collective-permute-start.4) | collective-permute-done | bytes 16416 | tf_op jit(solution)/shard_map/ppermute | solution.py:303
  8.0 0.4 %collective-permute-done.3.b2 = bf16[8,1024]{1,0:T(8,128)(2,1)S(1)} collective-permute-done((bf16[8,1024]{1,0:T(8,128)(2,1)S(1)}, bf16[8,1024]{1,0:T(8,128)(2,1)S(1)}, u32[]{:S(2)}, u32[]{:S(2)}) %collective-permute-start.3) | collective-permute-done | bytes 16416 | tf_op jit(solution)/shard_map/ppermute | solution.py:303
  8.4 0.4 %sums.1 = (f32[16,512]{1,0:T(8,128)S(1)}, f32[8,512]{1,0:T(8,128)S(1)}, f32[8,512]{1,0:T(8,128)S(1)}) custom-call(bf16[8,1024]{1,0:T(8,128)(2,1)S(1)} %fold.1.b0, bf16[8,1024]{1,0:T(8,128)(2,1)S(1)} %collective-permute-done.1.b1, bf16[8,1024]{1,0:T(8,128)(2,1)S(1)} %collective-permute-done.3.b2, bf16[8,1024]{1,0:T(8,128)(2,1)S(1)} %collective-permute-done.4.b3, ...), custom_call_target="tpu_custom_call" | custom-call | flops 268435456 | bytes 2097152 | tf_op jit(solution)/shard_map/sums/pallas_call | solution.py:244
  8.8 2.7 %collective-permute-start.5 = (f32[16,512]{1,0:T(8,128)S(1)}, f32[16,512]{1,0:T(8,128)S(1)}, u32[]{:S(2)}, u32[]{:S(2)}) collective-permute-start(f32[16,512]{1,0:T(8,128)S(1)} %get-tuple-element.33), channel_id=1, source_target_pairs={{0,2},{1,3},{2,0},{3,1},{4,5},{5,6},{6,7},{7,4},{8,10},{9,11},{10,... | collective-permute-start | bytes 98312 | tf_op jit(solution)/shard_map/ppermute | solution.py:303
  11.5 1.0 %collective-permute-start.6 = (f32[8,512]{1,0:T(8,128)S(1)}, f32[8,512]{1,0:T(8,128)S(1)}, u32[]{:S(2)}, u32[]{:S(2)}) collective-permute-start(f32[8,512]{1,0:T(8,128)S(1)} %get-tuple-element.34), channel_id=1, source_target_pairs={{0,7},{1,4},{2,5},{3,6},{4,3},{5,0},{6,1},{7,2},{8,15},{9,12},{10,... | collective-permute-start | bytes 49160 | tf_op jit(solution)/shard_map/ppermute | solution.py:303
  12.5 1.1 %collective-permute-done.5.got_ref = f32[16,512]{1,0:T(8,128)S(1)} collective-permute-done((f32[16,512]{1,0:T(8,128)S(1)}, f32[16,512]{1,0:T(8,128)S(1)}, u32[]{:S(2)}, u32[]{:S(2)}) %collective-permute-start.5) | collective-permute-done | bytes 32800 | tf_op jit(solution)/shard_map/ppermute | solution.py:303
  13.7 0.3 %collective-permute-start.7 = (f32[8,512]{1,0:T(8,128)S(1)}, f32[8,512]{1,0:T(8,128)S(1)}, u32[]{:S(2)}, u32[]{:S(2)}) collective-permute-start(f32[8,512]{1,0:T(8,128)S(1)} %slice.4), channel_id=1, source_target_pairs={{0,4},{1,5},{2,6},{3,7},{4,0},{5,1},{6,2},{7,3},{8,12},{9,13},{10,... | collective-permute-start | bytes 49160 | tf_op jit(solution)/shard_map/ppermute | solution.py:303
  13.9 0.8 %collective-permute-done.6.far_ref = f32[8,512]{1,0:T(8,128)S(1)} collective-permute-done((f32[8,512]{1,0:T(8,128)S(1)}, f32[8,512]{1,0:T(8,128)S(1)}, u32[]{:S(2)}, u32[]{:S(2)}) %collective-permute-start.6) | collective-permute-done | bytes 16416 | tf_op jit(solution)/shard_map/ppermute | solution.py:303
  14.7 0.1 collective-permute-done.7.too_ref
  14.8 0.8 %expand.1 = f32[64,512]{1,0:T(8,128)} custom-call(f32[8,512]{1,0:T(8,128)S(1)} %get-tuple-element.32.keep_ref, f32[16,512]{1,0:T(8,128)S(1)} %collective-permute-done.5.got_ref, f32[8,512]{1,0:T(8,128)S(1)} %collective-permute-done.6.far_ref, f32[8,512]{1,0:T(8,128)S(1)} %collective-permute-done.7.too_ref, s32[64,128]{1,0:T(8,128)S(1)} %get-tuple-element.35.key_ref, ...), custom_call_target="tpu_custom_call" | custom-call | flops 1048576 | bytes 262144 | tf_op jit(solution)/shard_map/expand/pallas_call | solution.py:285
  (1 shorter events, 0.0 us)
Async XLA Ops:
  0.0 1.8 %collective-permute-start = (bf16[32,1024]{1,0:T(8,128)(2,1)}, bf16[32,1024]{1,0:T(8,128)(2,1)S(1)}, u32[]{:S(2)}, u32[]{:S(2)}) collective-permute-start(bf16[32,1024]{1,0:T(8,128)(2,1)} %amplitudes_ref.1), channel_id=1, source_target_pairs={{0,4},{1,5},{2,6},{3,7},{4,0},{5,1},{6,2},{7,3},{8,12},{9,13},{10,... | collective-permute-start | bytes 196616 | tf_op jit(solution)/shard_map/ppermute | solution.py:303
  1.8 4.5 %collective-permute-start.2 = (bf16[1040,512]{1,0:T(8,128)(2,1)S(1)}, bf16[1040,512]{1,0:T(8,128)(2,1)S(1)}, u32[]{:S(2)}, u32[]{:S(2)}) collective-permute-start(bf16[1040,512]{1,0:T(8,128)(2,1)S(1)} %get-tuple-element.27.staged_ref), channel_id=1, source_target_pairs={{0,4},{1,5},{2,6},{3,7},{4,0},{5,1},{6,2},{7,3},{8,12},{9,13},{10,... | collective-permute-start | bytes 3194888 | tf_op jit(solution)/shard_map/ppermute | solution.py:303
  2.1 4.7 %collective-permute-start.1 = (bf16[8,1024]{1,0:T(8,128)(2,1)S(1)}, bf16[8,1024]{1,0:T(8,128)(2,1)S(1)}, u32[]{:S(2)}, u32[]{:S(2)}) collective-permute-start(bf16[8,1024]{1,0:T(8,128)(2,1)S(1)} %fold.1.b0), channel_id=1, source_target_pairs={{0,12},{1,13},{2,14},{3,15},{4,16},{5,17},{6,18},{7,19},{8,20},{9,... | collective-permute-start | bytes 49160 | tf_op jit(solution)/shard_map/ppermute | solution.py:303
  4.7 3.3 %collective-permute-start.4 = (bf16[8,1024]{1,0:T(8,128)(2,1)S(1)}, bf16[8,1024]{1,0:T(8,128)(2,1)S(1)}, u32[]{:S(2)}, u32[]{:S(2)}) collective-permute-start(bf16[8,1024]{1,0:T(8,128)(2,1)S(1)} %fold.1.b0), channel_id=1, source_target_pairs={{0,28},{1,29},{2,30},{3,31},{4,24},{5,25},{6,26},{7,27},{8,4},{9,5... | collective-permute-start | bytes 49160 | tf_op jit(solution)/shard_map/ppermute | solution.py:303
  6.9 1.6 %collective-permute-start.3 = (bf16[8,1024]{1,0:T(8,128)(2,1)S(1)}, bf16[8,1024]{1,0:T(8,128)(2,1)S(1)}, u32[]{:S(2)}, u32[]{:S(2)}) collective-permute-start(bf16[8,1024]{1,0:T(8,128)(2,1)S(1)} %collective-permute-done.1.b1), channel_id=1, source_target_pairs={{0,4},{1,5},{2,6},{3,7},{4,0},{5,1},{6,2},{7,3},{8,12},{9,13},{10,... | collective-permute-start | bytes 49160 | tf_op jit(solution)/shard_map/ppermute | solution.py:303
  8.8 4.8 %collective-permute-start.5 = (f32[16,512]{1,0:T(8,128)S(1)}, f32[16,512]{1,0:T(8,128)S(1)}, u32[]{:S(2)}, u32[]{:S(2)}) collective-permute-start(f32[16,512]{1,0:T(8,128)S(1)} %get-tuple-element.33), channel_id=1, source_target_pairs={{0,2},{1,3},{2,0},{3,1},{4,5},{5,6},{6,7},{7,4},{8,10},{9,11},{10,... | collective-permute-start | bytes 98312 | tf_op jit(solution)/shard_map/ppermute | solution.py:303
  11.5 3.2 %collective-permute-start.6 = (f32[8,512]{1,0:T(8,128)S(1)}, f32[8,512]{1,0:T(8,128)S(1)}, u32[]{:S(2)}, u32[]{:S(2)}) collective-permute-start(f32[8,512]{1,0:T(8,128)S(1)} %get-tuple-element.34), channel_id=1, source_target_pairs={{0,7},{1,4},{2,5},{3,6},{4,3},{5,0},{6,1},{7,2},{8,15},{9,12},{10,... | collective-permute-start | bytes 49160 | tf_op jit(solution)/shard_map/ppermute | solution.py:303
  13.7 1.2 %collective-permute-start.7 = (f32[8,512]{1,0:T(8,128)S(1)}, f32[8,512]{1,0:T(8,128)S(1)}, u32[]{:S(2)}, u32[]{:S(2)}) collective-permute-start(f32[8,512]{1,0:T(8,128)S(1)} %slice.4), channel_id=1, source_target_pairs={{0,4},{1,5},{2,6},{3,7},{4,0},{5,1},{6,2},{7,3},{8,12},{9,13},{10,... | collective-permute-start | bytes 49160 | tf_op jit(solution)/shard_map/ppermute | solution.py:303
